TPU v7x, 256 devices: a whole 4x4x8 slice. The times are simulated.
256 devices in a mesh: row: 16 (over x, z_lo, core), col: 16 (over y, z_hi).
Axes of the slice: x: 4, y: 4, z: 8 (z_hi: 4, z_lo: 2; z = z_hi * 2 + z_lo), core: 2. Of those that a mesh axis runs over, the one named last changes fastest.
Arguments:
- vectors: bfloat16 [2048, 1024], P(('row', 'col')), may hold values from -6 to 6
- block_values: bfloat16 [16, 16, 512, 4096], P('row', 'col'), may hold values from -0.09375 to 0.09375
- block_rows: int32 [16, 16, 512], P('row', 'col'), may hold values from 0 to 127, as said below
- block_cols: int32 [16, 16, 512], P('row', 'col'), may hold values from 0 to 127, as said below
- block_count: int32 [16, 16], P('row', 'col'), may hold values from 0 to 512, as said below
Outputs:
- product: float32 [2048, 1024], P(('row', 'col'))
Inputs may be any that keep to these rules, and one draw needn't show every extreme that they name: `block_rows`: in each tile the live slots name distinct positions with gi >= gj and come first, sorted by block row and then block column; slots past the count hold in-range indices that are not part of the matrix. `block_cols`: same slots as block_rows. `block_count`: some tile fills all 512 slots in every draw.
All inputs are finite; a program needn't handle non-finite values.
Results may differ from a plain program's by a relative error of at most 0.0003.
Values may be sent and summed in bfloat16 or wider, within the bound.
No kernel may reach another device: no remote copies, remote signals or barrier semaphores. Data moves between devices by JAX's collectives and lax.ppermute only.
A program may use at most 64 MiB of HBM per device.

v0:
```python
import jax
import jax.numpy as jnp
from jax import lax
from jax.sharding import PartitionSpec as P

NV = 16
BS = 64


def on_device(vectors, block_values, block_rows, block_cols, block_count):
    col_devices = lax.axis_size("col")
    row_index = lax.axis_index("row")
    col_index = lax.axis_index("col")
    piece_blocks = vectors.shape[0]
    width = vectors.shape[1]
    slot_count = block_rows.shape[2]
    matrices = block_values.reshape(slot_count, BS, BS)
    local_rows = block_rows.reshape(slot_count)
    local_cols = block_cols.reshape(slot_count)
    live_count = block_count.reshape(())
    row_segment = lax.all_gather(vectors, "col", axis=0, tiled=True)
    column_set = lax.all_gather(vectors, "row", axis=0, tiled=True)
    global_row = row_index * col_devices * piece_blocks + local_rows
    global_col = (
        local_cols // piece_blocks * col_devices + col_index
    ) * piece_blocks + local_cols % piece_blocks
    live = jnp.arange(slot_count, dtype=jnp.int32) < live_count
    weight = jnp.where(live, jnp.where(global_row == global_col, 0.5, 1.0), 0.0).astype(jnp.float32)
    col_vectors = jnp.take(column_set, local_cols, axis=0).reshape(slot_count, NV, BS)
    row_vectors = jnp.take(row_segment, local_rows, axis=0).reshape(slot_count, NV, BS)
    forward = jnp.einsum("nvk,nik->nvi", col_vectors, matrices, preferred_element_type=jnp.float32)
    backward = jnp.einsum("nvi,nik->nvk", row_vectors, matrices, preferred_element_type=jnp.float32)
    forward = (forward * weight[:, None, None]).reshape(slot_count, width)
    backward = (backward * weight[:, None, None]).reshape(slot_count, width)
    row_part = jax.ops.segment_sum(forward, local_rows, num_segments=row_segment.shape[0])
    col_part = jax.ops.segment_sum(backward, local_cols, num_segments=column_set.shape[0])
    whole_rows = lax.psum(row_part, "col")
    whole_cols = lax.psum(col_part, "row")
    mine_rows = lax.dynamic_slice_in_dim(whole_rows, col_index * piece_blocks, piece_blocks, 0)
    mine_cols = lax.dynamic_slice_in_dim(whole_cols, row_index * piece_blocks, piece_blocks, 0)
    return mine_rows + mine_cols


def solution(mesh):
    placed = (
        P(("row", "col"), None),
        P("row", "col", None, None),
        P("row", "col", None),
        P("row", "col", None),
        P("row", "col"),
    )
    return jax.shard_map(
        on_device, mesh=mesh, in_specs=placed, out_specs=P(("row", "col"), None), check_vma=False
    )
```

profile of v0, /device:TPU:6, one launch (start us, length us, event | category | flops | bytes accessed | tf_op | source)
XLA Modules:
  0.0 371.7 jit_solution(11786903282523296864)
XLA Ops:
  6.5 0.0 all-reduce.3.cloned.1.call-start
  6.5 0.7 add_select_fusion
  7.2 0.7 compare_and_fusion.1
  8.6 18.1 %all_gather.6 = bf16[128,1024]{1,0:T(8,128)(2,1)S(1)} all-gather(bf16[8,1024]{1,0:T(8,128)(2,1)} %param.7), channel_id=1, replica_groups=mesh['row'=16,'col'=16] {'row'}, dimensions={0}, use_global_device_ids=true | all-gather | bytes 278528 | tf_op jit(solution)/shard_map/all_gather | solution.py:22
  26.6 2.0 gather_fusion
  28.7 1.2 broadcast_select_fusion.1
  29.9 1.5 copy.6
  31.4 2.0 copy.8
  33.4 6.5 %copy.7 = bf16[1,1,512,4096]{2,3,1,0:T(8,128)(2,1)} copy(bf16[1,1,512,4096]{3,2,1,0:T(8,128)(2,1)} %param.8) | data formatting | bytes 8388608 | tf_op args[1]
  39.9 0.0 copy-start.1
  39.9 0.0 copy-start.2
  39.9 13.0 %copy.9 = bf16[512,64,64]{2,1,0:T(8,128)(2,1)} copy(bf16[512,64,64]{0,2,1:T(8,128)(2,1)} %bitcast.13) | data formatting | bytes 8388608 | tf_op jit(solution)/shard_map/reshape | solution.py:17
  52.9 0.0 copy-done.1
  52.9 0.0 copy-done.2
  52.9 9.8 %convolution_multiply_fusion.1 = f32[512,16,64]{2,1,0:T(8,128)} fusion(bf16[512,16,64]{2,1,0:T(8,128)(2,1)S(1)} %copy.8, bf16[512,64,64]{2,1,0:T(8,128)(2,1)} %copy.9, f32[512]{0:T(512)S(1)} %select_select_fusion), kind=kOutput, calls=%fused_computation.5 | convolution fusion | flops 67633152 | bytes 7342080 | tf_op jit(solution)/shard_map/nvk,nik->nvi/dot_general | solution.py:31
  62.7 2.8 copy.10
  65.6 0.0 copy-start
  65.6 1.9 copy.11
  67.5 6.5 %scatter_custom_fusion = f32[128,1024]{1,0:T(8,128)} fusion(s32[512]{0:T(512)S(1)} %bitcast.19, f32[512,1024]{1,0:T(8,128)} %copy.11, f32[]{:T(128)} %constant.47.clone.1), kind=kCustom, calls=%fused_computation.10 | custom fusion | flops 524288 | bytes 524800 | tf_op jit(solution)/shard_map/scatter-add | solution.py:35
  74.0 0.0 all-reduce.3.cloned.1.call-update
  74.0 0.0 all-reduce.5.cloned.1.call-start
  74.1 0.0 copy-done
  74.1 48.1 %all_gather.7 = bf16[128,1024]{1,0:T(8,128)(2,1)S(1)} all-gather(bf16[8,1024]{1,0:T(8,128)(2,1)S(1)} %copy-done), channel_id=1, replica_groups=mesh['row'=16,'col'=16] {'col'}, dimensions={0}, use_global_device_ids=true | all-gather | bytes 278528 | tf_op jit(solution)/shard_map/all_gather | solution.py:21
  122.2 2.1 gather_fusion.1
  124.2 1.2 broadcast_select_fusion
  125.5 1.5 copy.12
  127.0 2.0 copy.13
  129.0 7.7 %convolution_multiply_fusion = f32[512,16,64]{2,1,0:T(8,128)} fusion(bf16[512,16,64]{2,1,0:T(8,128)(2,1)S(1)} %copy.13, bf16[512,64,64]{2,1,0:T(8,128)(2,1)} %copy.9, f32[512]{0:T(512)S(1)} %select_select_fusion), kind=kOutput, calls=%fused_computation.4 | convolution fusion | flops 67633152 | bytes 7342080 | tf_op jit(solution)/shard_map/nvi,nik->nvk/dot_general | solution.py:32
  136.7 2.8 copy.15
  139.6 1.9 copy.16
  141.4 6.5 %scatter_custom_fusion.1 = f32[128,1024]{1,0:T(8,128)} fusion(s32[512]{0:T(512)S(1)} %bitcast.25, f32[512,1024]{1,0:T(8,128)} %copy.16, f32[]{:T(128)} %constant.47.clone.1), kind=kCustom, calls=%fused_computation.8 | custom fusion | flops 524288 | bytes 524800 | tf_op jit(solution)/shard_map/scatter-add | solution.py:36
  147.9 0.0 all-reduce.5.cloned.1.call-update
  147.9 97.7 %all-reduce.3.cloned.1.call-done = f32[128,1024]{1,0:T(8,128)} async-done(((f32[128,1024]{1,0:T(8,128)}), f32[128,1024]{1,0:T(8,128)}) %all-reduce.3.cloned.1.call-update) | async-done | bytes 524304 | tf_op jit(solution)/shard_map/psum | solution.py:37
  245.7 117.8 %all-reduce.5.cloned.1.call-done = f32[128,1024]{1,0:T(8,128)} async-done(((f32[128,1024]{1,0:T(8,128)}), f32[128,1024]{1,0:T(8,128)}) %all-reduce.5.cloned.1.call-update) | async-done | bytes 524304 | tf_op jit(solution)/shard_map/psum | solution.py:38
  363.5 1.4 dynamic-slice_add_fusion
  (5 shorter events, 0.0 us)
Async XLA Ops:
  6.5 239.1 %all-reduce.3.cloned.1.call-start = ((), (), s32[]{:S(2)}) async-start(), calls=%async_computation | async-start | bytes 1048576 | tf_op jit(solution)/shard_map/psum | solution.py:37
  39.9 13.0 %copy-start.1 = (s32[1,1,512]{2,1,0:T(1,128)S(1)}, s32[1,1,512]{2,1,0:T(1,128)}, u32[]{:S(2)}) copy-start(s32[1,1,512]{2,1,0:T(1,128)} %param.9) | copy-start | bytes 6148
  39.9 13.0 %copy-start.2 = (s32[1,1,512]{2,1,0:T(1,128)S(1)}, s32[1,1,512]{2,1,0:T(1,128)}, u32[]{:S(2)}) copy-start(s32[1,1,512]{2,1,0:T(1,128)} %param.10) | copy-start | bytes 6148
  65.6 8.5 %copy-start = (bf16[8,1024]{1,0:T(8,128)(2,1)S(1)}, bf16[8,1024]{1,0:T(8,128)(2,1)}, u32[]{:S(2)}) copy-start(bf16[8,1024]{1,0:T(8,128)(2,1)} %param.7) | copy-start | bytes 49156
  74.0 289.5 %all-reduce.5.cloned.1.call-start = ((), (), s32[]{:S(2)}) async-start(), calls=%async_computation.1 | async-start | bytes 1048576 | tf_op jit(solution)/shard_map/psum | solution.py:38
Sparse Core Ops, SparseCore 0:
  74.1 171.4 all-reduce.2
  248.3 115.1 all-reduce.4
where the time goes:
time: 379 us; the launch traced here: 372 us
  waiting for transfers between devices  216 us (57%)
  blocking collectives  66.1 us (17%)
  local copies, waits for them, and re-layouts  40.1 us (11%)
  other arithmetic  18.2 us (5%)
  matrix products  17.5 us (5%)
  between operations  14.2 us (4%)
    psum x1, waiting for transfers between devices, on_device(): whole_cols = lax.psum(col_part, 'row')  118 us
    psum x1, waiting for transfers between devices, on_device(): whole_rows = lax.psum(row_part, 'col')  97.7 us
    all_gather x1, blocking collectives, on_device(): row_segment = lax.all_gather(vectors, 'col', axis=0, tiled=True)  48.1 us
    all_gather x1, blocking collectives, on_device(): column_set = lax.all_gather(vectors, 'row', axis=0, tiled=True)  18.1 us
    reshape x1, local copies, waits for them, and re-layouts, on_device(): matrices = block_values.reshape(slot_count, BS, BS)  13 us
    dot_general x1, matrix products, on_device(): jnp.einsum('nvk,nik->nvi', col_vectors, matrices, preferred_element_type=...  9.8 us
    dot_general x1, matrix products, on_device(): jnp.einsum('nvi,nik->nvk', row_vectors, matrices, preferred_element_type=...  7.7 us
  transfers between devices with their start and end apart: 2, of which 2 were waited for; matrix products, arithmetic and copies ran while one was open for 7% of the time, Pallas kernels for 0%

commit v1 on v0

v1 whole, which is shorter than its diff:
```python
import jax
import jax.numpy as jnp
from jax import lax
from jax.experimental import pallas as pl
from jax.experimental.pallas import tpu as pltpu
from jax.sharding import PartitionSpec as P

NV = 16
BS = 64
NB = 128
SLOTS = 512
GROUP = 128
PAD = 33
PITCH = 17
UNROLL = 32


def relayout_kernel(v_ref, w_ref, f_ref):
    for t in range(32):
        x = v_ref[:, t * 128 : (t + 1) * 128].astype(jnp.float32)
        for h in range(GROUP // 8):
            f_ref[pl.ds(h * 8 * PAD + t, 8, stride=PAD), :] = x[h * 8 : (h + 1) * 8]
    for s in range(GROUP):
        w_ref[s * 32 : (s + 1) * 32] = f_ref[s * PAD : s * PAD + 32].astype(jnp.bfloat16)


def relayout(values):
    return pl.pallas_call(
        relayout_kernel,
        grid=(SLOTS // GROUP,),
        in_specs=[pl.BlockSpec((GROUP, BS * BS), lambda i: (i, 0))],
        out_specs=pl.BlockSpec((GROUP * 32, 128), lambda i: (i, 0)),
        out_shape=jax.ShapeDtypeStruct((SLOTS * 32, 128), jnp.bfloat16),
        scratch_shapes=[pltpu.VMEM((GROUP * PAD, 128), jnp.float32)],
        name="relayout",
    )(values)


def even_odd(n, dtype):
    i = lax.broadcasted_iota(jnp.int32, (n, n), 0)
    j = lax.broadcasted_iota(jnp.int32, (n, n), 1)
    k = j % 64
    return (i == (j - k) + 2 * (k % 32) + k // 32).astype(dtype)


def expand(x_ref, xs_ref, tmp, permutation):
    for b in range(NB // 16):
        for q in range(8):
            x = x_ref[b * 16 : (b + 1) * 16, q * 128 : (q + 1) * 128].astype(jnp.float32)
            y = pltpu.roll(x, 64, 1)
            for h in range(2):
                base = (b * 16 + h * 8) * PITCH + 2 * q
                tmp[pl.ds(base, 8, stride=PITCH), :] = x[h * 8 : (h + 1) * 8]
                tmp[pl.ds(base + 1, 8, stride=PITCH), :] = y[h * 8 : (h + 1) * 8]
    for b in range(NB):
        z = tmp[b * PITCH : b * PITCH + 16, 0:64].astype(jnp.bfloat16)
        if permutation is not None:
            z = jnp.dot(z, permutation, preferred_element_type=jnp.float32).astype(jnp.bfloat16)
        xs_ref[b * 16 : (b + 1) * 16, :] = z


def compress(acc_ref, out_ref):
    lane = lax.broadcasted_iota(jnp.int32, (8, 128), 1)
    for b in range(NB // 8):
        for q in range(8):
            base = b * 8 * PITCH + 2 * q
            low = acc_ref[pl.ds(base, 8, stride=PITCH), :]
            high = acc_ref[pl.ds(base + 1, 8, stride=PITCH), :]
            out_ref[b * 8 : (b + 1) * 8, q * 128 : (q + 1) * 128] = jnp.where(
                lane < 64, low, pltpu.roll(high, 64, 1)
            )


def blocks_kernel(
    rows_ref, cols_ref, place_ref, xr_ref, xc_ref, w_ref, of_ref, og_ref, xrs, xcs, accf, accg, tmp
):
    expand(xr_ref, xrs, tmp, even_odd(64, jnp.bfloat16))
    expand(xc_ref, xcs, tmp, None)
    accf[...] = jnp.zeros_like(accf)
    accg[...] = jnp.zeros_like(accg)
    count = place_ref[0]
    row_index = place_ref[1]
    col_index = place_ref[2]

    def step(j, carry):
        for u in range(UNROLL):
            s = j * UNROLL + u
            r = rows_ref[s]
            c = cols_ref[s]
            global_row = row_index * NB + r
            global_col = ((c >> 3) * 16 + col_index) * 8 + (c & 7)
            weight = jnp.where(s < count, jnp.where(global_row == global_col, 0.5, 1.0), 0.0)
            w = w_ref[pl.ds(pl.multiple_of(s * 32, 32), 32), :]
            b = jnp.concatenate([w[:, :64], w[:, 64:]], 0)
            xc = xcs[pl.ds(pl.multiple_of(c * 16, 16), 16), :]
            xr = xrs[pl.ds(pl.multiple_of(r * 16, 16), 16), :]
            f = lax.dot_general(
                xc, b, (((1,), (1,)), ((), ())), preferred_element_type=jnp.float32
            )
            g = jnp.dot(xr, b, preferred_element_type=jnp.float32)
            accf[pl.ds(r * PITCH, 16), 0:64] += f * weight
            accg[pl.ds(c * PITCH, 16), 0:64] += g * weight
        return carry

    lax.fori_loop(0, (count + UNROLL - 1) // UNROLL, step, 0)
    compress(accf, of_ref)
    compress(accg, og_ref)


def blocks(rows, cols, place, row_vectors, col_vectors, w):
    smem = pl.BlockSpec(memory_space=pltpu.SMEM)
    vmem = pl.BlockSpec(memory_space=pltpu.VMEM)
    return pl.pallas_call(
        blocks_kernel,
        in_specs=[smem] * 3 + [vmem] * 3,
        out_specs=[vmem] * 2,
        out_shape=[jax.ShapeDtypeStruct((NB, NV * BS), jnp.float32)] * 2,
        scratch_shapes=[pltpu.VMEM((NB * NV, BS), jnp.bfloat16)] * 2
        + [pltpu.VMEM((NB * PITCH, 128), jnp.float32)] * 3,
        name="blocks",
    )(rows, cols, place, row_vectors, col_vectors, w)


def finish_kernel(a_ref, b_ref, o_ref):
    back = even_odd(128, jnp.float32)
    a = a_ref[0]
    b = b_ref[0]
    for i in range(1, 16):
        a = a + a_ref[i]
        b = b + b_ref[i]
    for q in range(8):
        piece = slice(q * 128, (q + 1) * 128)
        o_ref[:, piece] = b[:, piece] + lax.dot_general(
            a[:, piece],
            back,
            (((1,), (1,)), ((), ())),
            preferred_element_type=jnp.float32,
            precision=lax.Precision.HIGHEST,
        )


def finish(a, b):
    vmem = pl.BlockSpec(memory_space=pltpu.VMEM)
    return pl.pallas_call(
        finish_kernel,
        in_specs=[vmem] * 2,
        out_specs=vmem,
        out_shape=jax.ShapeDtypeStruct((8, NV * BS), jnp.float32),
        name="finish",
    )(a, b)


def on_device(vectors, block_values, block_rows, block_cols, block_count):
    row_index = lax.axis_index("row")
    col_index = lax.axis_index("col")
    copies = jnp.broadcast_to(vectors[None], (16,) + vectors.shape)
    column_set = lax.all_to_all(copies, "row", 0, 0, tiled=True).reshape(NB, NV * BS)
    row_segment = lax.all_to_all(copies, "col", 0, 0, tiled=True).reshape(NB, NV * BS)
    w = relayout(block_values.reshape(SLOTS, BS * BS))
    place = jnp.stack([block_count.reshape(()), row_index, col_index])
    row_part, col_part = blocks(
        block_rows.reshape(SLOTS), block_cols.reshape(SLOTS), place, row_segment, column_set, w
    )
    mine_rows = lax.all_to_all(row_part.reshape(16, 8, NV * BS), "col", 0, 0, tiled=True)
    mine_cols = lax.all_to_all(col_part.reshape(16, 8, NV * BS), "row", 0, 0, tiled=True)
    return finish(mine_rows, mine_cols)


def solution(mesh):
    placed = (
        P(("row", "col"), None),
        P("row", "col", None, None),
        P("row", "col", None),
        P("row", "col", None),
        P("row", "col"),
    )
    return jax.shard_map(
        on_device, mesh=mesh, in_specs=placed, out_specs=P(("row", "col"), None), check_vma=False
    )
```

time: 379 us -> 91.9 us (0.24); the launches traced: 372 us -> 90.7 us
  waiting for transfers between devices: 216 us -> 6.72 us
  local copies, waits for them, and re-layouts: 40.1 us -> 2.16 us
  Pallas kernels: 0 us -> 20 us
  other arithmetic: 18.2 us -> 0.65 us
  matrix products: 17.5 us -> 0 us
  blocking collectives: 66.1 us -> 50.2 us
  between operations: 14.2 us -> 0.67 us
  starting transfers between devices: 0.04 us -> 10.3 us
    psum x2 -> x0, waiting for transfers between devices: 216 us -> none  [the longest x1 118 us: on_device(): whole_cols = lax.psum(col_part, 'row')]
    all_gather x2 -> x0, blocking collectives: 66.1 us -> none  [the longest x1 48.1 us: on_device(): row_segment = lax.all_gather(vectors, 'col', axis=0, tiled=True)]
    all_to_all x0 -> x3, blocking collectives: none -> 50.2 us  [the longest x1 23.1 us: on_device(): lax.all_to_all(row_part.reshape(16, 8, NV * BS), 'col', 0, 0, tiled=True)]
    reshape x5 -> x0, local copies, waits for them, and re-layouts: 20.8 us -> none  [the longest x1 13 us: on_device(): matrices = block_values.reshape(slot_count, BS, BS)]
    pallas_call x0 -> x3, Pallas kernels: none -> 20 us  [the longest x1 12.2 us: blocks(): pl.pallas_call(blocks_kernel, in_specs=[smem] * 3 + [vmem] * 3, out_specs...]
    dot_general x2 -> x0, matrix products: 17.5 us -> none  [the longest x1 9.8 us: on_device(): jnp.einsum('nvk,nik->nvi', col_vectors, matrices, preferred_element_type=...]
    scatter-add x2 -> x0, other arithmetic: 13 us -> none  [the longest x1 6.52 us: on_device(): jax.ops.segment_sum(forward, local_rows, num_segments=row_segment.shape[0])]
    all_to_all x0 -> x1, starting transfers between devices: none -> 10.3 us  [on_device(): lax.all_to_all(copies, 'col', 0, 0, tiled=True).reshape(NB, NV * BS)]
  transfers between devices with their start and end apart: 2 -> 1, of which waited for: 2 -> 1; matrix products, arithmetic and copies ran while one was open for 7% -> 1% of each run, Pallas kernels for 0% -> 6%
where the time goes in v1:
time: 91.9 us; the launch traced here: 90.7 us
  blocking collectives  50.2 us (55%)
  Pallas kernels  20 us (22%)
  starting transfers between devices  10.3 us (11%)
  waiting for transfers between devices  6.72 us (7%)
  local copies, waits for them, and re-layouts  2.16 us (2%)
    all_to_all x1, blocking collectives, on_device(): lax.all_to_all(row_part.reshape(16, 8, NV * BS), 'col', 0, 0, tiled=True)  23.1 us
    all_to_all x1, blocking collectives, on_device(): lax.all_to_all(col_part.reshape(16, 8, NV * BS), 'row', 0, 0, tiled=True)  15 us
    pallas_call x1, Pallas kernels, blocks(): pl.pallas_call(blocks_kernel, in_specs=[smem] * 3 + [vmem] * 3, out_specs...  12.2 us
    all_to_all x1, blocking collectives, on_device(): lax.all_to_all(copies, 'row', 0, 0, tiled=True).reshape(NB, NV * BS)  12 us
    all_to_all x1, starting transfers between devices, on_device(): lax.all_to_all(copies, 'col', 0, 0, tiled=True).reshape(NB, NV * BS)  10.3 us
    all_to_all x1, waiting for transfers between devices, on_device(): lax.all_to_all(copies, 'col', 0, 0, tiled=True).reshape(NB, NV * BS)  6.72 us
    pallas_call x1, Pallas kernels, relayout(): pl.pallas_call(relayout_kernel, grid=(SLOTS // GROUP,), in_specs=[pl.Bloc...  5.05 us
    pallas_call x1, Pallas kernels, finish(): pl.pallas_call(finish_kernel, in_specs=[vmem] * 2, out_specs=vmem, out_sh...  2.75 us
  transfers between devices with their start and end apart: 1, of which 1 were waited for; matrix products, arithmetic and copies ran while one was open for 1% of the time, Pallas kernels for 6%

profile of v1, /device:TPU:6, one launch (start us, length us, event | category | flops | bytes accessed | tf_op | source)
XLA Modules:
  0.0 90.7 jit_solution(18093925707455129839)
XLA Ops:
  0.0 1.4 %broadcast_in_dim.2 = bf16[16,8,1024]{2,1,0:T(8,128)(2,1)} broadcast(bf16[8,1024]{1,0:T(8,128)(2,1)} %param.5), dimensions={1,2} | broadcast | bytes 278528 | tf_op jit(solution)/shard_map/broadcast_in_dim | solution.py:156
  1.4 12.0 %all_to_all.20 = bf16[16,8,1024]{2,1,0:T(8,128)(2,1)} all-to-all(bf16[16,8,1024]{2,1,0:T(8,128)(2,1)} %broadcast_in_dim.2), channel_id=1, replica_groups=mesh['row'=16,'col'=16] {'row'}, dimensions={0} | all-to-all | bytes 524288 | tf_op jit(solution)/shard_map/all_to_all | solution.py:157
  13.4 10.3 %all-to-all-start = ((bf16[16,8,1024]{2,1,0:T(8,128)(2,1)}), bf16[16,8,1024]{2,1,0:T(8,128)(2,1)S(1)}, u32[]{:S(2)}, u32[]{:S(2)}) async-start(bf16[16,8,1024]{2,1,0:T(8,128)(2,1)} %broadcast_in_dim.2), calls=%async_computation | async-start | bytes 524288 | tf_op jit(solution)/shard_map/all_to_all | solution.py:158
  24.4 5.0 %relayout.1.w_ref = bf16[16384,128]{1,0:T(8,128)(2,1)} custom-call(bf16[512,4096]{1,0:T(8,128)(2,1)} %bitcast.11), custom_call_target="tpu_custom_call" | custom-call | tf_op jit(solution)/shard_map/relayout/pallas_call | solution.py:28
  29.4 0.7 pad_add_fusion.place_ref
  30.1 6.7 %all-to-all-done = bf16[16,8,1024]{2,1,0:T(8,128)(2,1)S(1)} async-done(((bf16[16,8,1024]{2,1,0:T(8,128)(2,1)}), bf16[16,8,1024]{2,1,0:T(8,128)(2,1)S(1)}, u32[]{:S(2)}, u32[]{:S(2)}) %all-to-all-start) | async-done | bytes 262176 | tf_op jit(solution)/shard_map/all_to_all | solution.py:158
  36.8 0.0 copy-start
  36.8 0.7 copy-done
  37.5 12.2 %blocks.1 = (f32[128,1024]{1,0:T(8,128)}, f32[128,1024]{1,0:T(8,128)}) custom-call(s32[512]{0:T(512)} %bitcast.16, s32[512]{0:T(512)} %bitcast.17, s32[3]{0:T(128)} %pad_add_fusion.place_ref, bf16[128,1024]{1,0:T(8,128)(2,1)} %bitcast.13, bf16[128,1024]{1,0:T(8,128)(2,1)} %bitcast.12, bf16[16384,128]{1,0:T(8,128)(2,1)} %relayout.1.w_ref), custom_call_target="tpu_custom_call" | custom-call | tf_op jit(solution)/shard_map/blocks/pallas_call | solution.py:113
  49.8 15.0 %all_to_all.21.b_ref = f32[16,8,1024]{2,1,0:T(8,128)} all-to-all(f32[16,8,1024]{2,1,0:T(8,128)} %bitcast.15), channel_id=1, replica_groups=mesh['row'=16,'col'=16] {'row'}, dimensions={0} | all-to-all | bytes 1048576 | tf_op jit(solution)/shard_map/all_to_all | solution.py:165
  64.8 23.1 %all_to_all.22.a_ref = f32[16,8,1024]{2,1,0:T(8,128)} all-to-all(f32[16,8,1024]{2,1,0:T(8,128)} %bitcast.14), channel_id=1, replica_groups=mesh['row'=16,'col'=16] {'col'}, dimensions={0} | all-to-all | bytes 1048576 | tf_op jit(solution)/shard_map/all_to_all | solution.py:164
  87.9 2.8 %finish.1 = f32[8,1024]{1,0:T(8,128)} custom-call(f32[16,8,1024]{2,1,0:T(8,128)} %all_to_all.22.a_ref, f32[16,8,1024]{2,1,0:T(8,128)} %all_to_all.21.b_ref), custom_call_target="tpu_custom_call" | custom-call | tf_op jit(solution)/shard_map/finish/pallas_call | solution.py:144
Async XLA Ops:
  13.4 23.4 %all-to-all-start = ((bf16[16,8,1024]{2,1,0:T(8,128)(2,1)}), bf16[16,8,1024]{2,1,0:T(8,128)(2,1)S(1)}, u32[]{:S(2)}, u32[]{:S(2)}) async-start(bf16[16,8,1024]{2,1,0:T(8,128)(2,1)} %broadcast_in_dim.2), calls=%async_computation | async-start | bytes 524288 | tf_op jit(solution)/shard_map/all_to_all | solution.py:158
  36.8 0.7 copy-start

commit v2 on v1

v2 whole, which is shorter than its diff:
```python
import functools

import jax
import jax.numpy as jnp
from jax import lax
from jax.experimental import pallas as pl
from jax.experimental.pallas import tpu as pltpu
from jax.sharding import PartitionSpec as P

NV = 16
BS = 64
NB = 128
SLOTS = 512
GROUP = 128
PAD = 33
PITCH = 17
UNROLL = 32
ROW_BITS = (3, 2, 1, 0)
COL_BITS = (1, 0, 3, 2)


def relayout_kernel(v_ref, w_ref, f_ref):
    for t in range(32):
        x = v_ref[:, t * 128 : (t + 1) * 128].astype(jnp.float32)
        for h in range(GROUP // 8):
            f_ref[pl.ds(h * 8 * PAD + t, 8, stride=PAD), :] = x[h * 8 : (h + 1) * 8]
    for s in range(GROUP):
        w_ref[s * 32 : (s + 1) * 32] = f_ref[s * PAD : s * PAD + 32].astype(jnp.bfloat16)


def relayout(values):
    return pl.pallas_call(
        relayout_kernel,
        grid=(SLOTS // GROUP,),
        in_specs=[pl.BlockSpec((GROUP, BS * BS), lambda i: (i, 0))],
        out_specs=pl.BlockSpec((GROUP * 32, 128), lambda i: (i, 0)),
        out_shape=jax.ShapeDtypeStruct((SLOTS * 32, 128), jnp.bfloat16),
        scratch_shapes=[pltpu.VMEM((GROUP * PAD, 128), jnp.float32)],
        name="relayout",
    )(values)


def even_odd(n, dtype):
    i = lax.broadcasted_iota(jnp.int32, (n, n), 0)
    j = lax.broadcasted_iota(jnp.int32, (n, n), 1)
    k = j % 64
    return (i == (j - k) + 2 * (k % 32) + k // 32).astype(dtype)


def expand(x_ref, xs_ref, tmp, permutation):
    for b in range(NB // 16):
        for q in range(8):
            x = x_ref[b * 16 : (b + 1) * 16, q * 128 : (q + 1) * 128].astype(jnp.float32)
            y = pltpu.roll(x, 64, 1)
            for h in range(2):
                base = (b * 16 + h * 8) * PITCH + 2 * q
                tmp[pl.ds(base, 8, stride=PITCH), :] = x[h * 8 : (h + 1) * 8]
                tmp[pl.ds(base + 1, 8, stride=PITCH), :] = y[h * 8 : (h + 1) * 8]
    for b in range(NB):
        z = tmp[b * PITCH : b * PITCH + 16, 0:64].astype(jnp.bfloat16)
        if permutation is not None:
            z = jnp.dot(z, permutation, preferred_element_type=jnp.float32).astype(jnp.bfloat16)
        xs_ref[b * 16 : (b + 1) * 16, :] = z


def compress(acc_ref, out_ref, first):
    lane = lax.broadcasted_iota(jnp.int32, (8, 128), 1)
    for b in range(out_ref.shape[0] // 8):
        for q in range(8):
            base = (first + b * 8) * PITCH + 2 * q
            low = acc_ref[pl.ds(base, 8, stride=PITCH), :]
            high = acc_ref[pl.ds(base + 1, 8, stride=PITCH), :]
            out_ref[b * 8 : (b + 1) * 8, q * 128 : (q + 1) * 128] = jnp.where(
                lane < 64, low, pltpu.roll(high, 64, 1)
            )


def product_kernel(
    backward, rows_ref, cols_ref, place_ref, x_ref, w_ref, keep_ref, send_ref, xs, acc, tmp
):
    expand(x_ref, xs, tmp, even_odd(64, jnp.bfloat16) if backward else None)
    acc[...] = jnp.zeros_like(acc)
    count = place_ref[0]
    row_index = place_ref[1]
    col_index = place_ref[2]
    contract = ((1,), (0,)) if backward else ((1,), (1,))

    def step(j, carry):
        for u in range(UNROLL):
            s = j * UNROLL + u
            r = rows_ref[s]
            c = cols_ref[s]
            global_row = row_index * NB + r
            global_col = ((c >> 3) * 16 + col_index) * 8 + (c & 7)
            weight = jnp.where(s < count, jnp.where(global_row == global_col, 0.5, 1.0), 0.0)
            r = place_ref[3 + (r >> 3)] + (r & 7)
            c = place_ref[19 + (c >> 3)] + (c & 7)
            source, target = (r, c) if backward else (c, r)
            w = w_ref[pl.ds(pl.multiple_of(s * 32, 32), 32), :]
            b = jnp.concatenate([w[:, :64], w[:, 64:]], 0)
            x = xs[pl.ds(pl.multiple_of(source * 16, 16), 16), :]
            f = lax.dot_general(x, b, (contract, ((), ())), preferred_element_type=jnp.float32)
            acc[pl.ds(target * PITCH, 16), 0:64] += f * weight
        return carry

    lax.fori_loop(0, (count + UNROLL - 1) // UNROLL, step, 0)
    compress(acc, keep_ref, 0)
    compress(acc, send_ref, NB // 2)


def product(backward, rows, cols, place, x, w):
    smem = pl.BlockSpec(memory_space=pltpu.SMEM)
    vmem = pl.BlockSpec(memory_space=pltpu.VMEM)
    return pl.pallas_call(
        functools.partial(product_kernel, backward),
        in_specs=[smem] * 3 + [vmem] * 2,
        out_specs=[vmem] * 2,
        out_shape=[jax.ShapeDtypeStruct((NB // 2, NV * BS), jnp.float32)] * 2,
        scratch_shapes=[pltpu.VMEM((NB * NV, BS), jnp.bfloat16)]
        + [pltpu.VMEM((NB * PITCH, 128), jnp.float32)] * 2,
        name="backward" if backward else "forward",
    )(rows, cols, place, x, w)


def finish_kernel(a0_ref, a1_ref, b0_ref, b1_ref, o_ref):
    back = even_odd(128, jnp.float32)
    for q in range(8):
        piece = slice(q * 128, (q + 1) * 128)
        a = a0_ref[:, piece] + a1_ref[:, piece]
        o_ref[:, piece] = (b0_ref[:, piece] + b1_ref[:, piece]) + lax.dot_general(
            a,
            back,
            (((1,), (1,)), ((), ())),
            preferred_element_type=jnp.float32,
            precision=lax.Precision.HIGHEST,
        )


def finish(a, b):
    vmem = pl.BlockSpec(memory_space=pltpu.VMEM)
    return pl.pallas_call(
        finish_kernel,
        in_specs=[vmem] * 4,
        out_specs=vmem,
        out_shape=jax.ShapeDtypeStruct((8, NV * BS), jnp.float32),
        name="finish",
    )(*a, *b)


def swap(x, axis, bit):
    return lax.ppermute(x, axis, [(s, s ^ (1 << bit)) for s in range(16)])


def gather(x, axis, bits):
    for bit in bits:
        x = jnp.concatenate([x, swap(x, axis, bit)], 0)
    return x


def scatter(keep, send, axis, bits):
    for k in reversed(range(4)):
        received = swap(send, axis, bits[k])
        if k == 0:
            return keep, received
        half = keep.shape[0] // 2
        keep, send = keep[:half] + received[:half], keep[half:] + received[half:]


def slots(me, bits):
    m = jnp.arange(16, dtype=jnp.int32) ^ me
    return sum(((m >> bit) & 1) << (k + 3) for k, bit in enumerate(bits))


def on_device(vectors, block_values, block_rows, block_cols, block_count):
    row_index = lax.axis_index("row")
    col_index = lax.axis_index("col")
    column_set = gather(vectors, "row", ROW_BITS)
    row_segment = gather(vectors, "col", COL_BITS)
    w = relayout(block_values.reshape(SLOTS, BS * BS))
    place = jnp.concatenate(
        [
            jnp.stack([block_count.reshape(()), row_index, col_index]),
            slots(col_index, COL_BITS),
            slots(row_index, ROW_BITS),
        ]
    )
    rows = block_rows.reshape(SLOTS)
    cols = block_cols.reshape(SLOTS)
    row_part = product(False, rows, cols, place, column_set, w)
    col_part = product(True, rows, cols, place, row_segment, w)
    mine_rows = scatter(*row_part, "col", COL_BITS)
    mine_cols = scatter(*col_part, "row", ROW_BITS)
    return finish(mine_rows, mine_cols)


def solution(mesh):
    placed = (
        P(("row", "col"), None),
        P("row", "col", None, None),
        P("row", "col", None),
        P("row", "col", None),
        P("row", "col"),
    )
    return jax.shard_map(
        on_device, mesh=mesh, in_specs=placed, out_specs=P(("row", "col"), None), check_vma=False
    )
```

time: 91.9 us -> 87.2 us (0.949)
  blocking collectives: 50.2 us -> 0 us
  waiting for transfers between devices: 6.72 us -> 33.5 us
  starting transfers between devices: 10.3 us -> 20.8 us
  Pallas kernels: 20 us -> 25.4 us
  other arithmetic: 0.65 us -> 2.35 us
  local copies, waits for them, and re-layouts: 2.16 us -> 3.42 us
    all_to_all x3 -> x0, blocking collectives: 50.2 us -> none  [the longest x1 23.1 us: on_device(): lax.all_to_all(row_part.reshape(16, 8, NV * BS), 'col', 0, 0, tiled=True)]
    ppermute x0 -> x16, waiting for transfers between devices: none -> 33.5 us  [swap(): return lax.ppermute(x, axis, [(s, s ^ 1 << bit) for s in range(16)])]
    ppermute x0 -> x16, starting transfers between devices: none -> 20.8 us  [swap(): return lax.ppermute(x, axis, [(s, s ^ 1 << bit) for s in range(16)])]
    all_to_all x1 -> x0, starting transfers between devices: 10.3 us -> none  [on_device(): lax.all_to_all(copies, 'col', 0, 0, tiled=True).reshape(NB, NV * BS)]
    all_to_all x1 -> x0, waiting for transfers between devices: 6.72 us -> none  [on_device(): lax.all_to_all(copies, 'col', 0, 0, tiled=True).reshape(NB, NV * BS)]
    pallas_call x2 -> x3, Pallas kernels: 15 us -> 20.4 us  [the longest x2 18 us: product(): pl.pallas_call(functools.partial(product_kernel, backward), in_specs=[sme...]
    add x0 -> x7, other arithmetic: none -> 2.31 us  [the longest x6 2.3 us: scatter(): keep, send = (keep[:half] + received[:half], keep[half:] + received[half:])]
    unnamed x2 -> x20, local copies, waits for them, and re-layouts: 0.73 us -> 2.81 us
  transfers between devices with their start and end apart: 1 -> 16, of which waited for: 1 -> 10; matrix products, arithmetic and copies ran while one was open for 1% -> 4% of each run, Pallas kernels for 6% -> 27%
where the time goes in v2:
time: 87.2 us; the launch traced here: 86.3 us
  waiting for transfers between devices  33.5 us (38%)
  Pallas kernels  25.4 us (29%)
  starting transfers between devices  20.8 us (24%)
  local copies, waits for them, and re-layouts  3.42 us (4%)
  other arithmetic  2.35 us (3%)
    ppermute x16, waiting for transfers between devices, swap(): return lax.ppermute(x, axis, [(s, s ^ 1 << bit) for s in range(16)])  33.5 us
    ppermute x16, starting transfers between devices, swap(): return lax.ppermute(x, axis, [(s, s ^ 1 << bit) for s in range(16)])  20.8 us
    pallas_call x2, Pallas kernels, product(): pl.pallas_call(functools.partial(product_kernel, backward), in_specs=[sme...  18 us
    pallas_call x1, Pallas kernels, relayout(): pl.pallas_call(relayout_kernel, grid=(SLOTS // GROUP,), in_specs=[pl.Bloc...  5.04 us
    unnamed x20, local copies, waits for them, and re-layouts  2.81 us
    pallas_call x1, Pallas kernels, finish(): pl.pallas_call(finish_kernel, in_specs=[vmem] * 4, out_specs=vmem, out_sh...  2.36 us
    add x6, other arithmetic, scatter(): keep, send = (keep[:half] + received[:half], keep[half:] + received[half:])  2.3 us
  transfers between devices with their start and end apart: 16, of which 10 were waited for; matrix products, arithmetic and copies ran while one was open for 4% of the time, Pallas kernels for 27%

profile of v2, /device:TPU:6, one launch (start us, length us, event | category | flops | bytes accessed | tf_op | source)
XLA Modules:
  0.0 86.3 jit_solution(16184976138450673482)
XLA Ops:
  0.0 1.4 %collective-permute-start = (bf16[8,1024]{1,0:T(8,128)(2,1)}, bf16[8,1024]{1,0:T(8,128)(2,1)S(1)}, u32[]{:S(2)}, u32[]{:S(2)}) collective-permute-start(bf16[8,1024]{1,0:T(8,128)(2,1)} %param.5), channel_id=1, source_target_pairs={{0,128},{16,144},{32,160},{48,176},{64,192},{80,208},{96,224},{112... | collective-permute-start | bytes 49160 | tf_op jit(solution)/shard_map/ppermute | solution.py:151
  1.4 7.2 %collective-permute-start.8 = (bf16[8,1024]{1,0:T(8,128)(2,1)}, bf16[8,1024]{1,0:T(8,128)(2,1)S(1)}, u32[]{:S(2)}, u32[]{:S(2)}) collective-permute-start(bf16[8,1024]{1,0:T(8,128)(2,1)} %param.5), channel_id=1, source_target_pairs={{0,2},{1,3},{2,0},{3,1},{4,6},{5,7},{6,4},{7,5},{8,10},{9,11},{10,... | collective-permute-start | bytes 49160 | tf_op jit(solution)/shard_map/ppermute | solution.py:151
  8.6 0.8 constant_dynamic-update-slice_fusion.4
  10.0 0.0 copy-start.3
  10.0 5.0 %relayout.1.w_ref = bf16[16384,128]{1,0:T(8,128)(2,1)} custom-call(bf16[512,4096]{1,0:T(8,128)(2,1)} %bitcast.7), custom_call_target="tpu_custom_call" | custom-call | tf_op jit(solution)/shard_map/relayout/pallas_call | solution.py:32
  15.1 0.6 concatenate.33.place_ref
  15.7 0.0 collective-permute-done
  15.7 0.0 collective-permute-done.8
  15.7 0.0 copy-done.3
  15.7 0.1 collective-permute-start.1
  15.8 1.6 %collective-permute-start.9 = (bf16[16,1024]{1,0:T(8,128)(2,1)S(1)}, bf16[16,1024]{1,0:T(8,128)(2,1)S(1)}, u32[]{:S(2)}, u32[]{:S(2)}) collective-permute-start(bf16[16,1024]{1,0:T(8,128)(2,1)S(1)} %get-tuple-element.29), channel_id=1, source_target_pairs={{0,1},{1,0},{2,3},{3,2},{4,5},{5,4},{6,7},{7,6},{8,9},{9,8},{10,11... | collective-permute-start | bytes 98312 | tf_op jit(solution)/shard_map/ppermute | solution.py:151
  17.4 2.3 %collective-permute-done.1 = bf16[16,1024]{1,0:T(8,128)(2,1)S(1)} collective-permute-done((bf16[16,1024]{1,0:T(8,128)(2,1)S(1)}, bf16[16,1024]{1,0:T(8,128)(2,1)S(1)}, u32[]{:S(2)}, u32[]{:S(2)}) %collective-permute-start.1) | collective-permute-done | bytes 32800 | tf_op jit(solution)/shard_map/ppermute | solution.py:151
  19.7 1.0 %collective-permute-done.9 = bf16[16,1024]{1,0:T(8,128)(2,1)S(1)} collective-permute-done((bf16[16,1024]{1,0:T(8,128)(2,1)S(1)}, bf16[16,1024]{1,0:T(8,128)(2,1)S(1)}, u32[]{:S(2)}, u32[]{:S(2)}) %collective-permute-start.9) | collective-permute-done | bytes 32800 | tf_op jit(solution)/shard_map/ppermute | solution.py:151
  20.7 3.3 %collective-permute-start.10 = (bf16[32,1024]{1,0:T(8,128)(2,1)S(1)}, bf16[32,1024]{1,0:T(8,128)(2,1)S(1)}, u32[]{:S(2)}, u32[]{:S(2)}) collective-permute-start(bf16[32,1024]{1,0:T(8,128)(2,1)S(1)} %get-tuple-element.27), channel_id=1, source_target_pairs={{0,8},{1,9},{2,10},{3,11},{4,12},{5,13},{6,14},{7,15},{8,0},{9,1},... | collective-permute-start | bytes 196616 | tf_op jit(solution)/shard_map/ppermute | solution.py:151
  24.0 1.0 %collective-permute-start.2 = (bf16[32,1024]{1,0:T(8,128)(2,1)S(1)}, bf16[32,1024]{1,0:T(8,128)(2,1)S(1)}, u32[]{:S(2)}, u32[]{:S(2)}) collective-permute-start(bf16[32,1024]{1,0:T(8,128)(2,1)S(1)} %get-tuple-element.28), channel_id=1, source_target_pairs={{0,32},{16,48},{32,0},{48,16},{64,96},{80,112},{96,64},{112,80},{1... | collective-permute-start | bytes 196616 | tf_op jit(solution)/shard_map/ppermute | solution.py:151
  25.0 1.6 %collective-permute-done.10 = bf16[32,1024]{1,0:T(8,128)(2,1)S(1)} collective-permute-done((bf16[32,1024]{1,0:T(8,128)(2,1)S(1)}, bf16[32,1024]{1,0:T(8,128)(2,1)S(1)}, u32[]{:S(2)}, u32[]{:S(2)}) %collective-permute-start.10) | collective-permute-done | bytes 65568 | tf_op jit(solution)/shard_map/ppermute | solution.py:151
  26.6 1.7 %collective-permute-done.2 = bf16[32,1024]{1,0:T(8,128)(2,1)S(1)} collective-permute-done((bf16[32,1024]{1,0:T(8,128)(2,1)S(1)}, bf16[32,1024]{1,0:T(8,128)(2,1)S(1)}, u32[]{:S(2)}, u32[]{:S(2)}) %collective-permute-start.2) | collective-permute-done | bytes 65568 | tf_op jit(solution)/shard_map/ppermute | solution.py:151
  28.3 0.8 collective-permute-start.11
  29.1 0.0 collective-permute-start.3
  29.1 4.3 %collective-permute-done.11 = bf16[64,1024]{1,0:T(8,128)(2,1)S(1)} collective-permute-done((bf16[64,1024]{1,0:T(8,128)(2,1)S(1)}, bf16[64,1024]{1,0:T(8,128)(2,1)S(1)}, u32[]{:S(2)}, u32[]{:S(2)}) %collective-permute-start.11) | collective-permute-done | bytes 131104 | tf_op jit(solution)/shard_map/ppermute | solution.py:151
  33.4 0.0 copy-start.1
  33.4 0.7 copy-done.1
  34.1 8.5 %backward.1 = (f32[64,1024]{1,0:T(8,128)}, f32[64,1024]{1,0:T(8,128)}) custom-call(s32[512]{0:T(512)} %bitcast.8, s32[512]{0:T(512)} %bitcast.10, s32[35]{0:T(128)} %concatenate.33.place_ref, bf16[128,1024]{1,0:T(8,128)(2,1)} %copy-done.1, bf16[16384,128]{1,0:T(8,128)(2,1)} %relayout.1.w_ref), custom_call_target="tpu_custom_call" | custom-call | tf_op jit(solution)/shard_map/backward/pallas_call | solution.py:114
  42.6 0.0 copy-start.2
  42.6 0.0 collective-permute-start.12
  42.6 0.0 collective-permute-done.3
  42.7 0.0 copy-start
  42.7 0.7 copy-done
  43.4 9.5 %forward.1 = (f32[64,1024]{1,0:T(8,128)}, f32[64,1024]{1,0:T(8,128)}) custom-call(s32[512]{0:T(512)} %bitcast.9, s32[512]{0:T(512)} %bitcast.11, s32[35]{0:T(128)} %concatenate.33.place_ref, bf16[128,1024]{1,0:T(8,128)(2,1)} %copy-done, bf16[16384,128]{1,0:T(8,128)(2,1)} %relayout.1.w_ref), custom_call_target="tpu_custom_call" | custom-call | tf_op jit(solution)/shard_map/forward/pallas_call | solution.py:114
  52.9 0.7 collective-permute-start.4
  53.6 0.0 collective-permute-done.12
  53.6 0.0 copy-done.2
  53.6 2.1 %collective-permute-start.13 = (f32[32,1024]{1,0:T(8,128)S(1)}, f32[32,1024]{1,0:T(8,128)S(1)}, u32[]{:S(2)}, u32[]{:S(2)}) collective-permute-start(f32[32,1024]{1,0:T(8,128)S(1)} %get-tuple-element.14), channel_id=1, source_target_pairs={{0,32},{16,48},{32,0},{48,16},{64,96},{80,112},{96,64},{112,80},{1... | collective-permute-start | bytes 393224 | tf_op jit(solution)/shard_map/ppermute | solution.py:151
  55.7 6.1 %collective-permute-done.4 = f32[64,1024]{1,0:T(8,128)S(1)} collective-permute-done((f32[64,1024]{1,0:T(8,128)}, f32[64,1024]{1,0:T(8,128)S(1)}, u32[]{:S(2)}, u32[]{:S(2)}) %collective-permute-start.4) | collective-permute-done | bytes 262176 | tf_op jit(solution)/shard_map/ppermute | solution.py:151
  61.8 1.0 %slice_add_fusion.3 = (f32[32,1024]{1,0:T(8,128)S(1)}, f32[32,1024]{1,0:T(8,128)S(1)}) fusion(f32[64,1024]{1,0:T(8,128)S(1)} %collective-permute-done.4, f32[64,1024]{1,0:T(8,128)} %get-tuple-element.9), kind=kLoop, calls=%fused_computation.9 | loop fusion | flops 65536 | bytes 786432 | tf_op jit(solution)/shard_map/add | solution.py:166
  62.8 0.2 collective-permute-start.5
  63.1 0.0 collective-permute-done.13
  63.1 0.1 collective-permute-start.14
  63.2 6.3 %collective-permute-done.5 = f32[32,1024]{1,0:T(8,128)S(1)} collective-permute-done((f32[32,1024]{1,0:T(8,128)S(1)}, f32[32,1024]{1,0:T(8,128)S(1)}, u32[]{:S(2)}, u32[]{:S(2)}) %collective-permute-start.5) | collective-permute-done | bytes 131104 | tf_op jit(solution)/shard_map/ppermute | solution.py:151
  69.5 2.4 %collective-permute-start.6 = (f32[16,1024]{1,0:T(8,128)S(1)}, f32[16,1024]{1,0:T(8,128)S(1)}, u32[]{:S(2)}, u32[]{:S(2)}) collective-permute-start(f32[16,1024]{1,0:T(8,128)S(1)} %get-tuple-element.20), channel_id=1, source_target_pairs={{0,1},{1,0},{2,3},{3,2},{4,5},{5,4},{6,7},{7,6},{8,9},{9,8},{10,11... | collective-permute-start | bytes 196616 | tf_op jit(solution)/shard_map/ppermute | solution.py:151
  71.9 0.0 collective-permute-done.14
  71.9 0.6 slice_add_fusion.8
  72.5 0.0 collective-permute-start.15
  72.5 2.2 %collective-permute-done.6 = f32[16,1024]{1,0:T(8,128)S(1)} collective-permute-done((f32[16,1024]{1,0:T(8,128)S(1)}, f32[16,1024]{1,0:T(8,128)S(1)}, u32[]{:S(2)}, u32[]{:S(2)}) %collective-permute-start.6) | collective-permute-done | bytes 65568 | tf_op jit(solution)/shard_map/ppermute | solution.py:151
  74.7 0.6 slice_add_fusion.10
  75.3 0.0 collective-permute-start.7
  75.3 2.6 %collective-permute-done.15.b1_ref = f32[8,1024]{1,0:T(8,128)S(1)} collective-permute-done((f32[8,1024]{1,0:T(8,128)S(1)}, f32[8,1024]{1,0:T(8,128)S(1)}, u32[]{:S(2)}, u32[]{:S(2)}) %collective-permute-start.15) | collective-permute-done | bytes 32800 | tf_op jit(solution)/shard_map/ppermute | solution.py:151
  77.9 0.0 copy-start.4
  77.9 5.4 %collective-permute-done.7.a1_ref = f32[8,1024]{1,0:T(8,128)S(1)} collective-permute-done((f32[8,1024]{1,0:T(8,128)S(1)}, f32[8,1024]{1,0:T(8,128)S(1)}, u32[]{:S(2)}, u32[]{:S(2)}) %collective-permute-start.7) | collective-permute-done | bytes 32800 | tf_op jit(solution)/shard_map/ppermute | solution.py:151
  83.3 0.0 copy-start.5
  83.3 0.0 copy-done.4
  83.3 0.6 copy-done.5
  83.9 2.4 %finish.1 = f32[8,1024]{1,0:T(8,128)} custom-call(f32[8,1024]{1,0:T(8,128)} %get-tuple-element.24.a0_ref, f32[8,1024]{1,0:T(8,128)} %copy-done.5, f32[8,1024]{1,0:T(8,128)} %get-tuple-element.22.b0_ref, f32[8,1024]{1,0:T(8,128)} %copy-done.4), custom_call_target="tpu_custom_call" | custom-call | tf_op jit(solution)/shard_map/finish/pallas_call | solution.py:141
  (16 shorter events, 0.2 us)
Async XLA Ops:
  0.0 15.7 %collective-permute-start = (bf16[8,1024]{1,0:T(8,128)(2,1)}, bf16[8,1024]{1,0:T(8,128)(2,1)S(1)}, u32[]{:S(2)}, u32[]{:S(2)}) collective-permute-start(bf16[8,1024]{1,0:T(8,128)(2,1)} %param.5), channel_id=1, source_target_pairs={{0,128},{16,144},{32,160},{48,176},{64,192},{80,208},{96,224},{112... | collective-permute-start | bytes 49160 | tf_op jit(solution)/shard_map/ppermute | solution.py:151
  1.4 14.3 %collective-permute-start.8 = (bf16[8,1024]{1,0:T(8,128)(2,1)}, bf16[8,1024]{1,0:T(8,128)(2,1)S(1)}, u32[]{:S(2)}, u32[]{:S(2)}) collective-permute-start(bf16[8,1024]{1,0:T(8,128)(2,1)} %param.5), channel_id=1, source_target_pairs={{0,2},{1,3},{2,0},{3,1},{4,6},{5,7},{6,4},{7,5},{8,10},{9,11},{10,... | collective-permute-start | bytes 49160 | tf_op jit(solution)/shard_map/ppermute | solution.py:151
  10.0 5.7 %copy-start.3 = (bf16[8,1024]{1,0:T(8,128)(2,1)S(1)}, bf16[8,1024]{1,0:T(8,128)(2,1)}, u32[]{:S(2)}) copy-start(bf16[8,1024]{1,0:T(8,128)(2,1)} %param.5) | copy-start | bytes 49156
  15.7 4.0 %collective-permute-start.1 = (bf16[16,1024]{1,0:T(8,128)(2,1)S(1)}, bf16[16,1024]{1,0:T(8,128)(2,1)S(1)}, u32[]{:S(2)}, u32[]{:S(2)}) collective-permute-start(bf16[16,1024]{1,0:T(8,128)(2,1)S(1)} %get-tuple-element.30), channel_id=1, source_target_pairs={{0,64},{16,80},{32,96},{48,112},{64,0},{80,16},{96,32},{112,48},{1... | collective-permute-start | bytes 98312 | tf_op jit(solution)/shard_map/ppermute | solution.py:151
  15.8 4.9 %collective-permute-start.9 = (bf16[16,1024]{1,0:T(8,128)(2,1)S(1)}, bf16[16,1024]{1,0:T(8,128)(2,1)S(1)}, u32[]{:S(2)}, u32[]{:S(2)}) collective-permute-start(bf16[16,1024]{1,0:T(8,128)(2,1)S(1)} %get-tuple-element.29), channel_id=1, source_target_pairs={{0,1},{1,0},{2,3},{3,2},{4,5},{5,4},{6,7},{7,6},{8,9},{9,8},{10,11... | collective-permute-start | bytes 98312 | tf_op jit(solution)/shard_map/ppermute | solution.py:151
  20.7 5.9 %collective-permute-start.10 = (bf16[32,1024]{1,0:T(8,128)(2,1)S(1)}, bf16[32,1024]{1,0:T(8,128)(2,1)S(1)}, u32[]{:S(2)}, u32[]{:S(2)}) collective-permute-start(bf16[32,1024]{1,0:T(8,128)(2,1)S(1)} %get-tuple-element.27), channel_id=1, source_target_pairs={{0,8},{1,9},{2,10},{3,11},{4,12},{5,13},{6,14},{7,15},{8,0},{9,1},... | collective-permute-start | bytes 196616 | tf_op jit(solution)/shard_map/ppermute | solution.py:151
  24.0 4.3 %collective-permute-start.2 = (bf16[32,1024]{1,0:T(8,128)(2,1)S(1)}, bf16[32,1024]{1,0:T(8,128)(2,1)S(1)}, u32[]{:S(2)}, u32[]{:S(2)}) collective-permute-start(bf16[32,1024]{1,0:T(8,128)(2,1)S(1)} %get-tuple-element.28), channel_id=1, source_target_pairs={{0,32},{16,48},{32,0},{48,16},{64,96},{80,112},{96,64},{112,80},{1... | collective-permute-start | bytes 196616 | tf_op jit(solution)/shard_map/ppermute | solution.py:151
  28.3 5.1 %collective-permute-start.11 = (bf16[64,1024]{1,0:T(8,128)(2,1)S(1)}, bf16[64,1024]{1,0:T(8,128)(2,1)S(1)}, u32[]{:S(2)}, u32[]{:S(2)}) collective-permute-start(bf16[64,1024]{1,0:T(8,128)(2,1)S(1)} %get-tuple-element.25), channel_id=1, source_target_pairs={{0,4},{1,5},{2,6},{3,7},{4,0},{5,1},{6,2},{7,3},{8,12},{9,13},{10,... | collective-permute-start | bytes 393224 | tf_op jit(solution)/shard_map/ppermute | solution.py:151
  29.1 13.6 %collective-permute-start.3 = (bf16[64,1024]{1,0:T(8,128)(2,1)S(1)}, bf16[64,1024]{1,0:T(8,128)(2,1)S(1)}, u32[]{:S(2)}, u32[]{:S(2)}) collective-permute-start(bf16[64,1024]{1,0:T(8,128)(2,1)S(1)} %get-tuple-element.26), channel_id=1, source_target_pairs={{0,16},{16,0},{32,48},{48,32},{64,80},{80,64},{96,112},{112,96},{1... | collective-permute-start | bytes 393224 | tf_op jit(solution)/shard_map/ppermute | solution.py:151
  33.4 0.7 copy-start.1
  42.6 11.0 %copy-start.2 = (f32[64,1024]{1,0:T(8,128)S(1)}, f32[64,1024]{1,0:T(8,128)}, u32[]{:S(2)}) copy-start(f32[64,1024]{1,0:T(8,128)} %get-tuple-element.11) | copy-start | bytes 786436
  42.6 11.0 %collective-permute-start.12 = (f32[64,1024]{1,0:T(8,128)}, f32[64,1024]{1,0:T(8,128)S(1)}, u32[]{:S(2)}, u32[]{:S(2)}) collective-permute-start(f32[64,1024]{1,0:T(8,128)} %get-tuple-element.12), channel_id=1, source_target_pairs={{0,16},{16,0},{32,48},{48,32},{64,80},{80,64},{96,112},{112,96},{1... | collective-permute-start | bytes 786440 | tf_op jit(solution)/shard_map/ppermute | solution.py:151
  42.7 0.7 copy-start
  52.9 8.9 %collective-permute-start.4 = (f32[64,1024]{1,0:T(8,128)}, f32[64,1024]{1,0:T(8,128)S(1)}, u32[]{:S(2)}, u32[]{:S(2)}) collective-permute-start(f32[64,1024]{1,0:T(8,128)} %get-tuple-element.10), channel_id=1, source_target_pairs={{0,4},{1,5},{2,6},{3,7},{4,0},{5,1},{6,2},{7,3},{8,12},{9,13},{10,... | collective-permute-start | bytes 786440 | tf_op jit(solution)/shard_map/ppermute | solution.py:151
  53.6 9.5 %collective-permute-start.13 = (f32[32,1024]{1,0:T(8,128)S(1)}, f32[32,1024]{1,0:T(8,128)S(1)}, u32[]{:S(2)}, u32[]{:S(2)}) collective-permute-start(f32[32,1024]{1,0:T(8,128)S(1)} %get-tuple-element.14), channel_id=1, source_target_pairs={{0,32},{16,48},{32,0},{48,16},{64,96},{80,112},{96,64},{112,80},{1... | collective-permute-start | bytes 393224 | tf_op jit(solution)/shard_map/ppermute | solution.py:151
  62.8 6.6 %collective-permute-start.5 = (f32[32,1024]{1,0:T(8,128)S(1)}, f32[32,1024]{1,0:T(8,128)S(1)}, u32[]{:S(2)}, u32[]{:S(2)}) collective-permute-start(f32[32,1024]{1,0:T(8,128)S(1)} %get-tuple-element.16), channel_id=1, source_target_pairs={{0,8},{1,9},{2,10},{3,11},{4,12},{5,13},{6,14},{7,15},{8,0},{9,1},... | collective-permute-start | bytes 393224 | tf_op jit(solution)/shard_map/ppermute | solution.py:151
  63.1 8.8 %collective-permute-start.14 = (f32[16,1024]{1,0:T(8,128)S(1)}, f32[16,1024]{1,0:T(8,128)S(1)}, u32[]{:S(2)}, u32[]{:S(2)}) collective-permute-start(f32[16,1024]{1,0:T(8,128)S(1)} %get-tuple-element.18), channel_id=1, source_target_pairs={{0,64},{16,80},{32,96},{48,112},{64,0},{80,16},{96,32},{112,48},{1... | collective-permute-start | bytes 196616 | tf_op jit(solution)/shard_map/ppermute | solution.py:151
  69.5 5.3 %collective-permute-start.6 = (f32[16,1024]{1,0:T(8,128)S(1)}, f32[16,1024]{1,0:T(8,128)S(1)}, u32[]{:S(2)}, u32[]{:S(2)}) collective-permute-start(f32[16,1024]{1,0:T(8,128)S(1)} %get-tuple-element.20), channel_id=1, source_target_pairs={{0,1},{1,0},{2,3},{3,2},{4,5},{5,4},{6,7},{7,6},{8,9},{9,8},{10,11... | collective-permute-start | bytes 196616 | tf_op jit(solution)/shard_map/ppermute | solution.py:151
  72.5 5.4 %collective-permute-start.15 = (f32[8,1024]{1,0:T(8,128)S(1)}, f32[8,1024]{1,0:T(8,128)S(1)}, u32[]{:S(2)}, u32[]{:S(2)}) collective-permute-start(f32[8,1024]{1,0:T(8,128)S(1)} %get-tuple-element.21), channel_id=1, source_target_pairs={{0,128},{16,144},{32,160},{48,176},{64,192},{80,208},{96,224},{112... | collective-permute-start | bytes 98312 | tf_op jit(solution)/shard_map/ppermute | solution.py:151
  75.3 8.0 %collective-permute-start.7 = (f32[8,1024]{1,0:T(8,128)S(1)}, f32[8,1024]{1,0:T(8,128)S(1)}, u32[]{:S(2)}, u32[]{:S(2)}) collective-permute-start(f32[8,1024]{1,0:T(8,128)S(1)} %get-tuple-element.23), channel_id=1, source_target_pairs={{0,2},{1,3},{2,0},{3,1},{4,6},{5,7},{6,4},{7,5},{8,10},{9,11},{10,... | collective-permute-start | bytes 98312 | tf_op jit(solution)/shard_map/ppermute | solution.py:151
  77.9 5.4 %copy-start.4 = (f32[8,1024]{1,0:T(8,128)}, f32[8,1024]{1,0:T(8,128)S(1)}, u32[]{:S(2)}) copy-start(f32[8,1024]{1,0:T(8,128)S(1)} %collective-permute-done.15.b1_ref) | copy-start | bytes 98308
  83.3 0.6 copy-start.5

commit v3 on v0

v3 whole, which is shorter than its diff:
```python
import functools

import jax
import jax.numpy as jnp
from jax import lax
from jax.experimental import pallas as pl
from jax.experimental.pallas import tpu as pltpu
from jax.sharding import PartitionSpec as P

NV = 16
BS = 64
NB = 128
SLOTS = 512
GROUP = 128
PAD = 33
UNROLL = 64
ROW_BITS = (3, 2, 1, 0)
COL_BITS = (1, 0, 3, 2)
MIB = 1 << 20


def relayout_kernel(v_ref, weight_ref, w_ref, f_ref):
    weight = weight_ref[...]
    for t in range(32):
        x = v_ref[:, t * 128 : (t + 1) * 128].astype(jnp.float32) * weight
        for h in range(GROUP // 8):
            f_ref[pl.ds(h * 8 * PAD + t, 8, stride=PAD), :] = x[h * 8 : (h + 1) * 8]
    for s in range(GROUP):
        w_ref[s * 32 : (s + 1) * 32] = f_ref[s * PAD : s * PAD + 32].astype(jnp.bfloat16)


def relayout(values, weight):
    return pl.pallas_call(
        relayout_kernel,
        grid=(SLOTS // GROUP,),
        in_specs=[
            pl.BlockSpec((GROUP, BS * BS), lambda i: (i, 0)),
            pl.BlockSpec((GROUP, 128), lambda i: (i, 0)),
        ],
        out_specs=pl.BlockSpec((GROUP * 32, 128), lambda i: (i, 0)),
        out_shape=jax.ShapeDtypeStruct((SLOTS * 32, 128), jnp.bfloat16),
        scratch_shapes=[pltpu.VMEM((GROUP * PAD, 128), jnp.float32)],
        compiler_params=pltpu.CompilerParams(vmem_limit_bytes=16 * MIB),
        name="relayout",
    )(values, weight)


def even_odd(dtype):
    i = lax.broadcasted_iota(jnp.int32, (128, 128), 0)
    j = lax.broadcasted_iota(jnp.int32, (128, 128), 1)
    k = j % 64
    return (i == (j - k) + 2 * (k % 32) + k // 32).astype(dtype)


def below(shape):
    return lax.broadcasted_iota(jnp.int32, shape, 1) < 64


def offset(ref, s):
    return pl.ds(pl.multiple_of(ref[s], 16), 16)


def pair_of_blocks(w_ref, s):
    w = w_ref[pl.ds(pl.multiple_of(s * 32, 64), 64), :]
    a, b = w[:32], w[32:]
    low = below((32, 128))
    return jnp.concatenate(
        [
            jnp.where(low, a, pltpu.roll(b, 64, 1)),
            jnp.where(low, pltpu.roll(a, 64, 1), b),
        ],
        0,
    )


def forward_kernel(count_ref, rows_ref, cols_ref, x_ref, w_ref, keep_ref, send_ref, xlo, xhi, acc):
    low = below((16, 128))
    for b in range(NB // 2):
        x = x_ref[b * 16 : (b + 1) * 16, :].astype(jnp.float32)
        y = pltpu.roll(x, 64, 1)
        for h in range(2):
            here = slice((2 * b + h) * 16, (2 * b + h + 1) * 16)
            p, q = x[h * 8 : (h + 1) * 8], y[h * 8 : (h + 1) * 8]
            zero = jnp.zeros((16, 128), jnp.float32)
            xlo[here, :] = jnp.where(low, jnp.concatenate([p, q], 0), zero).astype(jnp.bfloat16)
            xhi[here, :] = jnp.where(low, zero, jnp.concatenate([q, p], 0)).astype(jnp.bfloat16)
    acc[...] = jnp.zeros_like(acc)

    def step(j, carry):
        for u in range(0, UNROLL, 2):
            s = j * UNROLL + u
            b = pair_of_blocks(w_ref, s)
            x = jnp.concatenate([xlo[offset(cols_ref, s), :], xhi[offset(cols_ref, s + 1), :]], 0)
            f = lax.dot_general(
                x, b, (((1,), (1,)), ((), ())), preferred_element_type=jnp.float32
            )
            acc[offset(rows_ref, s), 0:64] += f[:16]
            acc[offset(rows_ref, s + 1), 0:64] += f[16:]
        return carry

    lax.fori_loop(0, (count_ref[0, 0] + UNROLL - 1) // UNROLL, step, 0)
    low = below((8, 128))
    for b in range(NB):
        a0, a1 = acc[b * 16 : b * 16 + 8, :], acc[b * 16 + 8 : b * 16 + 16, :]
        out, i = (keep_ref, b) if b < NB // 2 else (send_ref, b - NB // 2)
        out[i * 8 : (i + 1) * 8, :] = jnp.where(low, a0, pltpu.roll(a1, 64, 1))


def backward_kernel(count_ref, rows_ref, cols_ref, x_ref, w_ref, keep_ref, send_ref, xs, acc):
    order = even_odd(jnp.bfloat16)
    for b in range(NB // 8):
        x = jnp.dot(
            x_ref[b * 64 : (b + 1) * 64, :], order, preferred_element_type=jnp.float32
        )
        y = pltpu.roll(x, 64, 1)
        for h in range(8):
            here = slice((8 * b + h) * 16, (8 * b + h + 1) * 16)
            p, q = x[h * 8 : (h + 1) * 8], y[h * 8 : (h + 1) * 8]
            xs[here, :] = jnp.concatenate([p, q], 0).astype(jnp.bfloat16)
    acc[...] = jnp.zeros_like(acc)

    def step(j, carry):
        for u in range(0, UNROLL, 2):
            s = j * UNROLL + u
            b = pair_of_blocks(w_ref, s)
            x = jnp.concatenate(
                [xs[offset(rows_ref, s), 0:64], xs[offset(rows_ref, s + 1), 0:64]], 0
            )
            g = jnp.dot(x, b, preferred_element_type=jnp.float32)
            acc[offset(cols_ref, s), 0:64] += g[:16, 0:64]
            acc[offset(cols_ref, s + 1), 64:128] += g[16:, 64:128]
        return carry

    lax.fori_loop(0, (count_ref[0, 0] + UNROLL - 1) // UNROLL, step, 0)
    low = below((8, 128))
    for b in range(NB):
        a0, a1 = acc[b * 16 : b * 16 + 8, :], acc[b * 16 + 8 : b * 16 + 16, :]
        out, i = (keep_ref, b) if b < NB // 2 else (send_ref, b - NB // 2)
        out[i * 8 : (i + 1) * 8, :] = jnp.where(
            low, a0 + pltpu.roll(a0, 64, 1), a1 + pltpu.roll(a1, 64, 1)
        )


def product(backward, count, rows, cols, x, w):
    smem = pl.BlockSpec(memory_space=pltpu.SMEM)
    vmem = pl.BlockSpec(memory_space=pltpu.VMEM)
    tables = 1 if backward else 2
    return pl.pallas_call(
        backward_kernel if backward else forward_kernel,
        in_specs=[smem] * 3 + [vmem] * 2,
        out_specs=[vmem] * 2,
        out_shape=[jax.ShapeDtypeStruct((NB * 4, 128), jnp.float32)] * 2,
        scratch_shapes=[pltpu.VMEM((NB * NV, 128), jnp.bfloat16)] * tables
        + [pltpu.VMEM((NB * NV, 128), jnp.float32)],
        compiler_params=pltpu.CompilerParams(vmem_limit_bytes=16 * MIB),
        name="backward" if backward else "forward",
    )(count, rows, cols, x, w)


def finish_kernel(a0_ref, a1_ref, b0_ref, b1_ref, o_ref, tmp):
    back = even_odd(jnp.float32)
    tmp[...] = (b0_ref[...] + b1_ref[...]) + lax.dot_general(
        a0_ref[...] + a1_ref[...],
        back,
        (((1,), (1,)), ((), ())),
        preferred_element_type=jnp.float32,
        precision=lax.Precision.HIGHEST,
    )
    for q in range(8):
        o_ref[:, q * 128 : (q + 1) * 128] = tmp[pl.ds(q, 8, stride=8), :]


def finish(a, b):
    vmem = pl.BlockSpec(memory_space=pltpu.VMEM)
    return pl.pallas_call(
        finish_kernel,
        in_specs=[vmem] * 4,
        out_specs=vmem,
        out_shape=jax.ShapeDtypeStruct((8, NV * BS), jnp.float32),
        scratch_shapes=[pltpu.VMEM((64, 128), jnp.float32)],
        compiler_params=pltpu.CompilerParams(vmem_limit_bytes=4 * MIB),
        name="finish",
    )(*a, *b)


def swap(x, axis, bit):
    return lax.ppermute(x, axis, [(s, s ^ (1 << bit)) for s in range(16)])


def gather(x, axis, bits):
    for bit in bits:
        x = jnp.concatenate([x, swap(x, axis, bit)], 0)
    return x


def scatter(keep, send, axis, bits):
    for k in reversed(range(4)):
        received = swap(send, axis, bits[k])
        if k == 0:
            return keep, received
        half = keep.shape[0] // 2
        keep, send = keep[:half] + received[:half], keep[half:] + received[half:]


def place(position, me, bits):
    m = (position >> 3) ^ me
    slot = sum(((m >> bit) & 1) << k for k, bit in enumerate(bits))
    return (slot * 8 + (position & 7)) * 16


def on_device(vectors, block_values, block_rows, block_cols, block_count):
    row_index = lax.axis_index("row")
    col_index = lax.axis_index("col")
    piece = vectors.reshape(64, 128)
    column_set = gather(piece, "row", ROW_BITS)
    row_segment = gather(piece, "col", COL_BITS)
    local_rows = block_rows.reshape(SLOTS)
    local_cols = block_cols.reshape(SLOTS)
    global_row = row_index * NB + local_rows
    global_col = ((local_cols >> 3) * 16 + col_index) * 8 + (local_cols & 7)
    live = jnp.arange(SLOTS, dtype=jnp.int32) < block_count.reshape(())
    weight = jnp.where(live, jnp.where(global_row == global_col, 0.5, 1.0), 0.0)
    weight = jnp.broadcast_to(weight.astype(jnp.float32)[:, None], (SLOTS, 128))
    w = relayout(block_values.reshape(SLOTS, BS * BS), weight)
    rows = place(local_rows, col_index, COL_BITS)
    cols = place(local_cols, row_index, ROW_BITS)
    row_part = product(False, block_count, rows, cols, column_set, w)
    col_part = product(True, block_count, rows, cols, row_segment, w)
    mine_rows = scatter(*row_part, "col", COL_BITS)
    mine_cols = scatter(*col_part, "row", ROW_BITS)
    return finish(mine_rows, mine_cols)


def solution(mesh):
    placed = (
        P(("row", "col"), None),
        P("row", "col", None, None),
        P("row", "col", None),
        P("row", "col", None),
        P("row", "col"),
    )
    return jax.shard_map(
        on_device, mesh=mesh, in_specs=placed, out_specs=P(("row", "col"), None), check_vma=False
    )
```

time: 379 us -> 72.8 us (0.19); the launches traced: 372 us -> 71.8 us
  waiting for transfers between devices: 216 us -> 29.6 us
  blocking collectives: 66.1 us -> 0 us
  local copies, waits for them, and re-layouts: 40.1 us -> 3.16 us
  starting transfers between devices: 0.04 us -> 25.4 us
  matrix products: 17.5 us -> 0 us
  other arithmetic: 18.2 us -> 2.26 us
  between operations: 14.2 us -> 0.85 us
  Pallas kernels: 0 us -> 10.6 us
    psum x2 -> x0, waiting for transfers between devices: 216 us -> none  [the longest x1 118 us: on_device(): whole_cols = lax.psum(col_part, 'row')]
    all_gather x2 -> x0, blocking collectives: 66.1 us -> none  [the longest x1 48.1 us: on_device(): row_segment = lax.all_gather(vectors, 'col', axis=0, tiled=True)]
    ppermute x0 -> x16, waiting for transfers between devices: none -> 29.6 us  [swap(): return lax.ppermute(x, axis, [(s, s ^ 1 << bit) for s in range(16)])]
    ppermute x0 -> x16, starting transfers between devices: none -> 25.4 us  [swap(): return lax.ppermute(x, axis, [(s, s ^ 1 << bit) for s in range(16)])]
    reshape x5 -> x1, local copies, waits for them, and re-layouts: 20.8 us -> 0.73 us  [on_device(): piece = vectors.reshape(64, 128)]
    dot_general x2 -> x0, matrix products: 17.5 us -> none  [the longest x1 9.8 us: on_device(): jnp.einsum('nvk,nik->nvi', col_vectors, matrices, preferred_element_type=...]
    scatter-add x2 -> x0, other arithmetic: 13 us -> none  [the longest x1 6.52 us: on_device(): jax.ops.segment_sum(forward, local_rows, num_segments=row_segment.shape[0])]
    pallas_call x0 -> x4, Pallas kernels: none -> 10.6 us  [the longest x2 8.69 us: product(): pl.pallas_call(backward_kernel if backward else forward_kernel, in_specs=...]
  transfers between devices with their start and end apart: 2 -> 16, of which waited for: 2 -> 9; matrix products, arithmetic and copies ran while one was open for 7% -> 3% of each run, Pallas kernels for 0% -> 14%
where the time goes in v3:
time: 72.8 us; the launch traced here: 71.8 us
  waiting for transfers between devices  29.6 us (41%)
  starting transfers between devices  25.4 us (35%)
  Pallas kernels  10.6 us (15%)
  local copies, waits for them, and re-layouts  3.16 us (4%)
  other arithmetic  2.26 us (3%)
  between operations  0.85 us (1%)
    ppermute x16, waiting for transfers between devices, swap(): return lax.ppermute(x, axis, [(s, s ^ 1 << bit) for s in range(16)])  29.6 us
    ppermute x16, starting transfers between devices, swap(): return lax.ppermute(x, axis, [(s, s ^ 1 << bit) for s in range(16)])  25.4 us
    pallas_call x2, Pallas kernels, product(): pl.pallas_call(backward_kernel if backward else forward_kernel, in_specs=...  8.69 us
    unnamed x10, local copies, waits for them, and re-layouts  2.27 us
  transfers between devices with their start and end apart: 16, of which 9 were waited for; matrix products, arithmetic and copies ran while one was open for 3% of the time, Pallas kernels for 14%

profile of v3, /device:TPU:6, one launch (start us, length us, event | category | flops | bytes accessed | tf_op | source)
XLA Modules:
  0.0 71.8 jit_solution(9786728009433403006)
XLA Ops:
  0.0 0.7 %reshape.88 = bf16[64,128]{1,0:T(8,128)(2,1)S(1)} reshape(bf16[8,1024]{1,0:T(8,128)(2,1)} %param.5) | data formatting | bytes 32768 | tf_op jit(solution)/shard_map/reshape | solution.py:214
  0.7 1.5 %collective-permute-start = (bf16[64,128]{1,0:T(8,128)(2,1)S(1)}, bf16[64,128]{1,0:T(8,128)(2,1)S(1)}, u32[]{:S(2)}, u32[]{:S(2)}) collective-permute-start(bf16[64,128]{1,0:T(8,128)(2,1)S(1)} %reshape.88), channel_id=1, source_target_pairs={{0,128},{16,144},{32,160},{48,176},{64,192},{80,208},{96,224},{112... | collective-permute-start | bytes 49160 | tf_op jit(solution)/shard_map/ppermute | solution.py:187
  2.2 7.2 %collective-permute-start.8 = (bf16[64,128]{1,0:T(8,128)(2,1)S(1)}, bf16[64,128]{1,0:T(8,128)(2,1)S(1)}, u32[]{:S(2)}, u32[]{:S(2)}) collective-permute-start(bf16[64,128]{1,0:T(8,128)(2,1)S(1)} %reshape.88), channel_id=1, source_target_pairs={{0,2},{1,3},{2,0},{3,1},{4,6},{5,7},{6,4},{7,5},{8,10},{9,11},{10,... | collective-permute-start | bytes 49160 | tf_op jit(solution)/shard_map/ppermute | solution.py:187
  9.4 0.7 add_multiply_fusion
  10.1 0.7 add_multiply_fusion.1
  10.8 0.7 compare_select_fusion
  12.2 0.1 broadcast_in_dim.21.weight_ref
  12.4 0.0 copy-start
  12.4 2.2 %copy-done = bf16[1,1,512,4096]{3,2,1,0:T(8,128)(2,1)S(1)} copy-done((bf16[1,1,512,4096]{3,2,1,0:T(8,128)(2,1)S(1)}, bf16[1,1,512,4096]{3,2,1,0:T(8,128)(2,1)}, u32[]{:S(2)}) %copy-start) | copy-done | bytes 4194328
  14.6 1.0 %relayout.1.w_ref = bf16[16384,128]{1,0:T(8,128)(2,1)S(1)} custom-call(bf16[512,4096]{1,0:T(8,128)(2,1)S(1)} %bitcast.6, f32[512,128]{1,0:T(8,128)S(1)} %broadcast_in_dim.21.weight_ref), custom_call_target="tpu_custom_call" | custom-call | tf_op jit(solution)/shard_map/relayout/pallas_call | solution.py:33
  15.6 0.0 collective-permute-done
  15.6 0.0 collective-permute-done.8
  15.6 0.1 collective-permute-start.1
  15.7 1.6 %collective-permute-start.9 = (bf16[128,128]{1,0:T(8,128)(2,1)S(1)}, bf16[128,128]{1,0:T(8,128)(2,1)S(1)}, u32[]{:S(2)}, u32[]{:S(2)}) collective-permute-start(bf16[128,128]{1,0:T(8,128)(2,1)S(1)} %get-tuple-element.29), channel_id=1, source_target_pairs={{0,1},{1,0},{2,3},{3,2},{4,5},{5,4},{6,7},{7,6},{8,9},{9,8},{10,11... | collective-permute-start | bytes 98312 | tf_op jit(solution)/shard_map/ppermute | solution.py:187
  17.3 2.3 %collective-permute-done.1 = bf16[128,128]{1,0:T(8,128)(2,1)S(1)} collective-permute-done((bf16[128,128]{1,0:T(8,128)(2,1)S(1)}, bf16[128,128]{1,0:T(8,128)(2,1)S(1)}, u32[]{:S(2)}, u32[]{:S(2)}) %collective-permute-start.1) | collective-permute-done | bytes 32800 | tf_op jit(solution)/shard_map/ppermute | solution.py:187
  19.6 1.0 %collective-permute-done.9 = bf16[128,128]{1,0:T(8,128)(2,1)S(1)} collective-permute-done((bf16[128,128]{1,0:T(8,128)(2,1)S(1)}, bf16[128,128]{1,0:T(8,128)(2,1)S(1)}, u32[]{:S(2)}, u32[]{:S(2)}) %collective-permute-start.9) | collective-permute-done | bytes 32800 | tf_op jit(solution)/shard_map/ppermute | solution.py:187
  20.6 3.3 %collective-permute-start.10 = (bf16[256,128]{1,0:T(8,128)(2,1)S(1)}, bf16[256,128]{1,0:T(8,128)(2,1)S(1)}, u32[]{:S(2)}, u32[]{:S(2)}) collective-permute-start(bf16[256,128]{1,0:T(8,128)(2,1)S(1)} %get-tuple-element.27), channel_id=1, source_target_pairs={{0,8},{1,9},{2,10},{3,11},{4,12},{5,13},{6,14},{7,15},{8,0},{9,1},... | collective-permute-start | bytes 196616 | tf_op jit(solution)/shard_map/ppermute | solution.py:187
  23.9 1.0 %collective-permute-start.2 = (bf16[256,128]{1,0:T(8,128)(2,1)S(1)}, bf16[256,128]{1,0:T(8,128)(2,1)S(1)}, u32[]{:S(2)}, u32[]{:S(2)}) collective-permute-start(bf16[256,128]{1,0:T(8,128)(2,1)S(1)} %get-tuple-element.28), channel_id=1, source_target_pairs={{0,32},{16,48},{32,0},{48,16},{64,96},{80,112},{96,64},{112,80},{1... | collective-permute-start | bytes 196616 | tf_op jit(solution)/shard_map/ppermute | solution.py:187
  25.0 1.5 %collective-permute-done.10 = bf16[256,128]{1,0:T(8,128)(2,1)S(1)} collective-permute-done((bf16[256,128]{1,0:T(8,128)(2,1)S(1)}, bf16[256,128]{1,0:T(8,128)(2,1)S(1)}, u32[]{:S(2)}, u32[]{:S(2)}) %collective-permute-start.10) | collective-permute-done | bytes 65568 | tf_op jit(solution)/shard_map/ppermute | solution.py:187
  26.5 1.7 %collective-permute-done.2 = bf16[256,128]{1,0:T(8,128)(2,1)S(1)} collective-permute-done((bf16[256,128]{1,0:T(8,128)(2,1)S(1)}, bf16[256,128]{1,0:T(8,128)(2,1)S(1)}, u32[]{:S(2)}, u32[]{:S(2)}) %collective-permute-start.2) | collective-permute-done | bytes 65568 | tf_op jit(solution)/shard_map/ppermute | solution.py:187
  28.2 0.8 %collective-permute-start.11 = (bf16[512,128]{1,0:T(8,128)(2,1)S(1)}, bf16[512,128]{1,0:T(8,128)(2,1)S(1)}, u32[]{:S(2)}, u32[]{:S(2)}) collective-permute-start(bf16[512,128]{1,0:T(8,128)(2,1)S(1)} %get-tuple-element.25), channel_id=1, source_target_pairs={{0,4},{1,5},{2,6},{3,7},{4,0},{5,1},{6,2},{7,3},{8,12},{9,13},{10,... | collective-permute-start | bytes 393224 | tf_op jit(solution)/shard_map/ppermute | solution.py:187
  29.0 0.0 collective-permute-start.3
  29.0 4.3 %collective-permute-done.11 = bf16[512,128]{1,0:T(8,128)(2,1)S(1)} collective-permute-done((bf16[512,128]{1,0:T(8,128)(2,1)S(1)}, bf16[512,128]{1,0:T(8,128)(2,1)S(1)}, u32[]{:S(2)}, u32[]{:S(2)}) %collective-permute-start.11) | collective-permute-done | bytes 131104 | tf_op jit(solution)/shard_map/ppermute | solution.py:187
  33.3 4.3 %backward.1 = (f32[512,128]{1,0:T(8,128)S(1)}, f32[512,128]{1,0:T(8,128)S(1)}) custom-call(s32[1,1]{1,0:T(1,128)} %copy.14.count_ref, s32[512]{0:T(512)S(1)} %bitcast.9, s32[512]{0:T(512)S(1)} %bitcast.7, bf16[1024,128]{1,0:T(8,128)(2,1)S(1)} %constant_dynamic-update-slice_fusion.5.x_ref, bf16[16384,128]{1,0:T(8,128)(2,1)S(1)} %relayout.1.w_ref), custom_call_target="tpu_custom_call" | custom-call | tf_op jit(solution)/shard_map/backward/pallas_call | solution.py:148
  37.5 0.1 collective-permute-start.12
  37.7 0.0 collective-permute-done.3
  37.7 4.4 %forward.1 = (f32[512,128]{1,0:T(8,128)S(1)}, f32[512,128]{1,0:T(8,128)S(1)}) custom-call(s32[1,1]{1,0:T(1,128)} %copy.14.count_ref, s32[512]{0:T(512)S(1)} %bitcast.10, s32[512]{0:T(512)S(1)} %bitcast.8, bf16[1024,128]{1,0:T(8,128)(2,1)S(1)} %constant_dynamic-update-slice_fusion.x_ref, bf16[16384,128]{1,0:T(8,128)(2,1)S(1)} %relayout.1.w_ref), custom_call_target="tpu_custom_call" | custom-call | tf_op jit(solution)/shard_map/forward/pallas_call | solution.py:148
  42.2 0.8 %collective-permute-start.4 = (f32[512,128]{1,0:T(8,128)S(1)}, f32[512,128]{1,0:T(8,128)S(1)}, u32[]{:S(2)}, u32[]{:S(2)}) collective-permute-start(f32[512,128]{1,0:T(8,128)S(1)} %get-tuple-element.10), channel_id=1, source_target_pairs={{0,4},{1,5},{2,6},{3,7},{4,0},{5,1},{6,2},{7,3},{8,12},{9,13},{10,... | collective-permute-start | bytes 786440 | tf_op jit(solution)/shard_map/ppermute | solution.py:187
  42.9 0.0 collective-permute-done.12
  43.0 2.2 %collective-permute-start.13 = (f32[256,128]{1,0:T(8,128)S(1)}, f32[256,128]{1,0:T(8,128)S(1)}, u32[]{:S(2)}, u32[]{:S(2)}) collective-permute-start(f32[256,128]{1,0:T(8,128)S(1)} %get-tuple-element.14), channel_id=1, source_target_pairs={{0,32},{16,48},{32,0},{48,16},{64,96},{80,112},{96,64},{112,80},{1... | collective-permute-start | bytes 393224 | tf_op jit(solution)/shard_map/ppermute | solution.py:187
  45.2 5.7 %collective-permute-done.4 = f32[512,128]{1,0:T(8,128)S(1)} collective-permute-done((f32[512,128]{1,0:T(8,128)S(1)}, f32[512,128]{1,0:T(8,128)S(1)}, u32[]{:S(2)}, u32[]{:S(2)}) %collective-permute-start.4) | collective-permute-done | bytes 262176 | tf_op jit(solution)/shard_map/ppermute | solution.py:187
  51.0 2.1 %collective-permute-start.5 = (f32[256,128]{1,0:T(8,128)S(1)}, f32[256,128]{1,0:T(8,128)S(1)}, u32[]{:S(2)}, u32[]{:S(2)}) collective-permute-start(f32[256,128]{1,0:T(8,128)S(1)} %get-tuple-element.16), channel_id=1, source_target_pairs={{0,8},{1,9},{2,10},{3,11},{4,12},{5,13},{6,14},{7,15},{8,0},{9,1},... | collective-permute-start | bytes 393224 | tf_op jit(solution)/shard_map/ppermute | solution.py:187
  53.1 0.0 collective-permute-done.13
  53.1 0.1 collective-permute-start.14
  53.2 4.4 %collective-permute-done.5 = f32[256,128]{1,0:T(8,128)S(1)} collective-permute-done((f32[256,128]{1,0:T(8,128)S(1)}, f32[256,128]{1,0:T(8,128)S(1)}, u32[]{:S(2)}, u32[]{:S(2)}) %collective-permute-start.5) | collective-permute-done | bytes 131104 | tf_op jit(solution)/shard_map/ppermute | solution.py:187
  57.6 1.2 %collective-permute-start.6 = (f32[128,128]{1,0:T(8,128)S(1)}, f32[128,128]{1,0:T(8,128)S(1)}, u32[]{:S(2)}, u32[]{:S(2)}) collective-permute-start(f32[128,128]{1,0:T(8,128)S(1)} %get-tuple-element.20), channel_id=1, source_target_pairs={{0,1},{1,0},{2,3},{3,2},{4,5},{5,4},{6,7},{7,6},{8,9},{9,8},{10,11... | collective-permute-start | bytes 196616 | tf_op jit(solution)/shard_map/ppermute | solution.py:187
  58.8 0.0 collective-permute-done.14
  58.8 0.7 collective-permute-start.15
  59.5 3.5 %collective-permute-done.6 = f32[128,128]{1,0:T(8,128)S(1)} collective-permute-done((f32[128,128]{1,0:T(8,128)S(1)}, f32[128,128]{1,0:T(8,128)S(1)}, u32[]{:S(2)}, u32[]{:S(2)}) %collective-permute-start.6) | collective-permute-done | bytes 65568 | tf_op jit(solution)/shard_map/ppermute | solution.py:187
  63.1 2.7 %collective-permute-start.7 = (f32[64,128]{1,0:T(8,128)S(1)}, f32[64,128]{1,0:T(8,128)S(1)}, u32[]{:S(2)}, u32[]{:S(2)}) collective-permute-start(f32[64,128]{1,0:T(8,128)S(1)} %get-tuple-element.23), channel_id=1, source_target_pairs={{0,2},{1,3},{2,0},{3,1},{4,6},{5,7},{6,4},{7,5},{8,10},{9,11},{10,... | collective-permute-start | bytes 98312 | tf_op jit(solution)/shard_map/ppermute | solution.py:187
  65.8 0.0 collective-permute-done.15.b1_ref
  65.8 5.2 %collective-permute-done.7.a1_ref = f32[64,128]{1,0:T(8,128)S(1)} collective-permute-done((f32[64,128]{1,0:T(8,128)S(1)}, f32[64,128]{1,0:T(8,128)S(1)}, u32[]{:S(2)}, u32[]{:S(2)}) %collective-permute-start.7) | collective-permute-done | bytes 32800 | tf_op jit(solution)/shard_map/ppermute | solution.py:187
  71.0 0.9 %finish.1 = f32[8,1024]{1,0:T(8,128)} custom-call(f32[64,128]{1,0:T(8,128)S(1)} %get-tuple-element.24.a0_ref, f32[64,128]{1,0:T(8,128)S(1)} %collective-permute-done.7.a1_ref, f32[64,128]{1,0:T(8,128)S(1)} %get-tuple-element.22.b0_ref, f32[64,128]{1,0:T(8,128)S(1)} %collective-permute-done.15.b1_ref), custom_call_target="tpu_custom_call" | custom-call | tf_op jit(solution)/shard_map/finish/pallas_call | solution.py:175
  (20 shorter events, 0.3 us)
Async XLA Ops:
  0.7 14.9 %collective-permute-start = (bf16[64,128]{1,0:T(8,128)(2,1)S(1)}, bf16[64,128]{1,0:T(8,128)(2,1)S(1)}, u32[]{:S(2)}, u32[]{:S(2)}) collective-permute-start(bf16[64,128]{1,0:T(8,128)(2,1)S(1)} %reshape.88), channel_id=1, source_target_pairs={{0,128},{16,144},{32,160},{48,176},{64,192},{80,208},{96,224},{112... | collective-permute-start | bytes 49160 | tf_op jit(solution)/shard_map/ppermute | solution.py:187
  2.2 13.4 %collective-permute-start.8 = (bf16[64,128]{1,0:T(8,128)(2,1)S(1)}, bf16[64,128]{1,0:T(8,128)(2,1)S(1)}, u32[]{:S(2)}, u32[]{:S(2)}) collective-permute-start(bf16[64,128]{1,0:T(8,128)(2,1)S(1)} %reshape.88), channel_id=1, source_target_pairs={{0,2},{1,3},{2,0},{3,1},{4,6},{5,7},{6,4},{7,5},{8,10},{9,11},{10,... | collective-permute-start | bytes 49160 | tf_op jit(solution)/shard_map/ppermute | solution.py:187
  12.4 2.2 %copy-start = (bf16[1,1,512,4096]{3,2,1,0:T(8,128)(2,1)S(1)}, bf16[1,1,512,4096]{3,2,1,0:T(8,128)(2,1)}, u32[]{:S(2)}) copy-start(bf16[1,1,512,4096]{3,2,1,0:T(8,128)(2,1)} %param.6) | copy-start | bytes 12582916
  15.6 4.0 %collective-permute-start.1 = (bf16[128,128]{1,0:T(8,128)(2,1)S(1)}, bf16[128,128]{1,0:T(8,128)(2,1)S(1)}, u32[]{:S(2)}, u32[]{:S(2)}) collective-permute-start(bf16[128,128]{1,0:T(8,128)(2,1)S(1)} %get-tuple-element.30), channel_id=1, source_target_pairs={{0,64},{16,80},{32,96},{48,112},{64,0},{80,16},{96,32},{112,48},{1... | collective-permute-start | bytes 98312 | tf_op jit(solution)/shard_map/ppermute | solution.py:187
  15.7 4.9 %collective-permute-start.9 = (bf16[128,128]{1,0:T(8,128)(2,1)S(1)}, bf16[128,128]{1,0:T(8,128)(2,1)S(1)}, u32[]{:S(2)}, u32[]{:S(2)}) collective-permute-start(bf16[128,128]{1,0:T(8,128)(2,1)S(1)} %get-tuple-element.29), channel_id=1, source_target_pairs={{0,1},{1,0},{2,3},{3,2},{4,5},{5,4},{6,7},{7,6},{8,9},{9,8},{10,11... | collective-permute-start | bytes 98312 | tf_op jit(solution)/shard_map/ppermute | solution.py:187
  20.6 5.9 %collective-permute-start.10 = (bf16[256,128]{1,0:T(8,128)(2,1)S(1)}, bf16[256,128]{1,0:T(8,128)(2,1)S(1)}, u32[]{:S(2)}, u32[]{:S(2)}) collective-permute-start(bf16[256,128]{1,0:T(8,128)(2,1)S(1)} %get-tuple-element.27), channel_id=1, source_target_pairs={{0,8},{1,9},{2,10},{3,11},{4,12},{5,13},{6,14},{7,15},{8,0},{9,1},... | collective-permute-start | bytes 196616 | tf_op jit(solution)/shard_map/ppermute | solution.py:187
  23.9 4.3 %collective-permute-start.2 = (bf16[256,128]{1,0:T(8,128)(2,1)S(1)}, bf16[256,128]{1,0:T(8,128)(2,1)S(1)}, u32[]{:S(2)}, u32[]{:S(2)}) collective-permute-start(bf16[256,128]{1,0:T(8,128)(2,1)S(1)} %get-tuple-element.28), channel_id=1, source_target_pairs={{0,32},{16,48},{32,0},{48,16},{64,96},{80,112},{96,64},{112,80},{1... | collective-permute-start | bytes 196616 | tf_op jit(solution)/shard_map/ppermute | solution.py:187
  28.2 5.1 %collective-permute-start.11 = (bf16[512,128]{1,0:T(8,128)(2,1)S(1)}, bf16[512,128]{1,0:T(8,128)(2,1)S(1)}, u32[]{:S(2)}, u32[]{:S(2)}) collective-permute-start(bf16[512,128]{1,0:T(8,128)(2,1)S(1)} %get-tuple-element.25), channel_id=1, source_target_pairs={{0,4},{1,5},{2,6},{3,7},{4,0},{5,1},{6,2},{7,3},{8,12},{9,13},{10,... | collective-permute-start | bytes 393224 | tf_op jit(solution)/shard_map/ppermute | solution.py:187
  29.0 8.7 %collective-permute-start.3 = (bf16[512,128]{1,0:T(8,128)(2,1)S(1)}, bf16[512,128]{1,0:T(8,128)(2,1)S(1)}, u32[]{:S(2)}, u32[]{:S(2)}) collective-permute-start(bf16[512,128]{1,0:T(8,128)(2,1)S(1)} %get-tuple-element.26), channel_id=1, source_target_pairs={{0,16},{16,0},{32,48},{48,32},{64,80},{80,64},{96,112},{112,96},{1... | collective-permute-start | bytes 393224 | tf_op jit(solution)/shard_map/ppermute | solution.py:187
  37.5 5.4 %collective-permute-start.12 = (f32[512,128]{1,0:T(8,128)S(1)}, f32[512,128]{1,0:T(8,128)S(1)}, u32[]{:S(2)}, u32[]{:S(2)}) collective-permute-start(f32[512,128]{1,0:T(8,128)S(1)} %get-tuple-element.12), channel_id=1, source_target_pairs={{0,16},{16,0},{32,48},{48,32},{64,80},{80,64},{96,112},{112,96},{1... | collective-permute-start | bytes 786440 | tf_op jit(solution)/shard_map/ppermute | solution.py:187
  42.2 8.8 %collective-permute-start.4 = (f32[512,128]{1,0:T(8,128)S(1)}, f32[512,128]{1,0:T(8,128)S(1)}, u32[]{:S(2)}, u32[]{:S(2)}) collective-permute-start(f32[512,128]{1,0:T(8,128)S(1)} %get-tuple-element.10), channel_id=1, source_target_pairs={{0,4},{1,5},{2,6},{3,7},{4,0},{5,1},{6,2},{7,3},{8,12},{9,13},{10,... | collective-permute-start | bytes 786440 | tf_op jit(solution)/shard_map/ppermute | solution.py:187
  43.0 10.1 %collective-permute-start.13 = (f32[256,128]{1,0:T(8,128)S(1)}, f32[256,128]{1,0:T(8,128)S(1)}, u32[]{:S(2)}, u32[]{:S(2)}) collective-permute-start(f32[256,128]{1,0:T(8,128)S(1)} %get-tuple-element.14), channel_id=1, source_target_pairs={{0,32},{16,48},{32,0},{48,16},{64,96},{80,112},{96,64},{112,80},{1... | collective-permute-start | bytes 393224 | tf_op jit(solution)/shard_map/ppermute | solution.py:187
  51.0 6.6 %collective-permute-start.5 = (f32[256,128]{1,0:T(8,128)S(1)}, f32[256,128]{1,0:T(8,128)S(1)}, u32[]{:S(2)}, u32[]{:S(2)}) collective-permute-start(f32[256,128]{1,0:T(8,128)S(1)} %get-tuple-element.16), channel_id=1, source_target_pairs={{0,8},{1,9},{2,10},{3,11},{4,12},{5,13},{6,14},{7,15},{8,0},{9,1},... | collective-permute-start | bytes 393224 | tf_op jit(solution)/shard_map/ppermute | solution.py:187
  53.1 5.7 %collective-permute-start.14 = (f32[128,128]{1,0:T(8,128)S(1)}, f32[128,128]{1,0:T(8,128)S(1)}, u32[]{:S(2)}, u32[]{:S(2)}) collective-permute-start(f32[128,128]{1,0:T(8,128)S(1)} %get-tuple-element.18), channel_id=1, source_target_pairs={{0,64},{16,80},{32,96},{48,112},{64,0},{80,16},{96,32},{112,48},{1... | collective-permute-start | bytes 196616 | tf_op jit(solution)/shard_map/ppermute | solution.py:187
  57.6 5.5 %collective-permute-start.6 = (f32[128,128]{1,0:T(8,128)S(1)}, f32[128,128]{1,0:T(8,128)S(1)}, u32[]{:S(2)}, u32[]{:S(2)}) collective-permute-start(f32[128,128]{1,0:T(8,128)S(1)} %get-tuple-element.20), channel_id=1, source_target_pairs={{0,1},{1,0},{2,3},{3,2},{4,5},{5,4},{6,7},{7,6},{8,9},{9,8},{10,11... | collective-permute-start | bytes 196616 | tf_op jit(solution)/shard_map/ppermute | solution.py:187
  58.8 7.0 %collective-permute-start.15 = (f32[64,128]{1,0:T(8,128)S(1)}, f32[64,128]{1,0:T(8,128)S(1)}, u32[]{:S(2)}, u32[]{:S(2)}) collective-permute-start(f32[64,128]{1,0:T(8,128)S(1)} %get-tuple-element.21), channel_id=1, source_target_pairs={{0,128},{16,144},{32,160},{48,176},{64,192},{80,208},{96,224},{112... | collective-permute-start | bytes 98312 | tf_op jit(solution)/shard_map/ppermute | solution.py:187
  63.1 7.9 %collective-permute-start.7 = (f32[64,128]{1,0:T(8,128)S(1)}, f32[64,128]{1,0:T(8,128)S(1)}, u32[]{:S(2)}, u32[]{:S(2)}) collective-permute-start(f32[64,128]{1,0:T(8,128)S(1)} %get-tuple-element.23), channel_id=1, source_target_pairs={{0,2},{1,3},{2,0},{3,1},{4,6},{5,7},{6,4},{7,5},{8,10},{9,11},{10,... | collective-permute-start | bytes 98312 | tf_op jit(solution)/shard_map/ppermute | solution.py:187

commit v4 on v3

--- a/solution.py
+++ b/solution.py
@@ -17,6 +17,8 @@
 ROW_BITS = (3, 2, 1, 0)
 COL_BITS = (1, 0, 3, 2)
 MIB = 1 << 20
+MODE = "rd"
+BAR = "brf"
 
 
 def relayout_kernel(v_ref, weight_ref, w_ref, f_ref):
@@ -73,7 +75,8 @@
     )
 
 
-def forward_kernel(count_ref, rows_ref, cols_ref, x_ref, w_ref, keep_ref, send_ref, xlo, xhi, acc):
+def forward_kernel(count_ref, rows_ref, cols_ref, x_ref, w_ref, *outs_and_scratch):
+    *outs, xlo, xhi, acc = outs_and_scratch
     low = below((16, 128))
     for b in range(NB // 2):
         x = x_ref[b * 16 : (b + 1) * 16, :].astype(jnp.float32)
@@ -102,11 +105,12 @@
     low = below((8, 128))
     for b in range(NB):
         a0, a1 = acc[b * 16 : b * 16 + 8, :], acc[b * 16 + 8 : b * 16 + 16, :]
-        out, i = (keep_ref, b) if b < NB // 2 else (send_ref, b - NB // 2)
+        out, i = outs[b * len(outs) // NB], b % (NB // len(outs))
         out[i * 8 : (i + 1) * 8, :] = jnp.where(low, a0, pltpu.roll(a1, 64, 1))
 
 
-def backward_kernel(count_ref, rows_ref, cols_ref, x_ref, w_ref, keep_ref, send_ref, xs, acc):
+def backward_kernel(count_ref, rows_ref, cols_ref, x_ref, w_ref, *outs_and_scratch):
+    *outs, xs, acc = outs_and_scratch
     order = even_odd(jnp.bfloat16)
     for b in range(NB // 8):
         x = jnp.dot(
@@ -135,7 +139,7 @@
     low = below((8, 128))
     for b in range(NB):
         a0, a1 = acc[b * 16 : b * 16 + 8, :], acc[b * 16 + 8 : b * 16 + 16, :]
-        out, i = (keep_ref, b) if b < NB // 2 else (send_ref, b - NB // 2)
+        out, i = outs[b * len(outs) // NB], b % (NB // len(outs))
         out[i * 8 : (i + 1) * 8, :] = jnp.where(
             low, a0 + pltpu.roll(a0, 64, 1), a1 + pltpu.roll(a1, 64, 1)
         )
@@ -144,12 +148,12 @@
 def product(backward, count, rows, cols, x, w):
     smem = pl.BlockSpec(memory_space=pltpu.SMEM)
     vmem = pl.BlockSpec(memory_space=pltpu.VMEM)
-    tables = 1 if backward else 2
+    tables, outs = (1, 2) if backward else (2, 4)
     return pl.pallas_call(
         backward_kernel if backward else forward_kernel,
         in_specs=[smem] * 3 + [vmem] * 2,
-        out_specs=[vmem] * 2,
-        out_shape=[jax.ShapeDtypeStruct((NB * 4, 128), jnp.float32)] * 2,
+        out_specs=[vmem] * outs,
+        out_shape=[jax.ShapeDtypeStruct((NB * 8 // outs, 128), jnp.float32)] * outs,
         scratch_shapes=[pltpu.VMEM((NB * NV, 128), jnp.bfloat16)] * tables
         + [pltpu.VMEM((NB * NV, 128), jnp.float32)],
         compiler_params=pltpu.CompilerParams(vmem_limit_bytes=16 * MIB),
@@ -187,14 +191,17 @@
     return lax.ppermute(x, axis, [(s, s ^ (1 << bit)) for s in range(16)])
 
 
-def gather(x, axis, bits):
-    for bit in bits:
-        x = jnp.concatenate([x, swap(x, axis, bit)], 0)
+def gather(x, axis, bits, after=None):
+    for k, bit in enumerate(bits):
+        y = swap(x, axis, bit)
+        if after is not None:
+            after.append(y)
+        x = jnp.concatenate([x, y], 0)
     return x
 
 
 def scatter(keep, send, axis, bits):
-    for k in reversed(range(4)):
+    for k in reversed(range(len(bits))):
         received = swap(send, axis, bits[k])
         if k == 0:
             return keep, received
@@ -202,6 +209,19 @@
         keep, send = keep[:half] + received[:half], keep[half:] + received[half:]
 
 
+def scatter_by_four(parts, axis, bits):
+    masks = [0, 1 << bits[2], 1 << bits[3], (1 << bits[2]) | (1 << bits[3])]
+    got = [
+        lax.ppermute(parts[k], axis, [(s, s ^ masks[k]) for s in range(16)]) for k in (1, 3, 2)
+    ]
+    half = parts[0].shape[0] // 2
+    keep, send = (
+        (parts[0][cut] + got[0][cut]) + (got[1][cut] + got[2][cut])
+        for cut in (slice(0, half), slice(half, None))
+    )
+    return scatter(keep, send, axis, bits[:2])
+
+
 def place(position, me, bits):
     m = (position >> 3) ^ me
     slot = sum(((m >> bit) & 1) << k for k, bit in enumerate(bits))
@@ -211,9 +231,16 @@
 def on_device(vectors, block_values, block_rows, block_cols, block_count):
     row_index = lax.axis_index("row")
     col_index = lax.axis_index("col")
-    piece = vectors.reshape(64, 128)
-    column_set = gather(piece, "row", ROW_BITS)
-    row_segment = gather(piece, "col", COL_BITS)
+    piece = lax.optimization_barrier(vectors.reshape(64, 128))
+    got = []
+    row_segment = gather(piece, "col", COL_BITS, got)
+    if MODE == "a2a":
+        copies = jnp.broadcast_to(piece[None], (16, 64, 128))
+        column_set = lax.all_to_all(copies, "row", 0, 0, tiled=True).reshape(NB * 8, 128)
+    else:
+        column_set = gather(piece.reshape(8, 8, 128), "row", ROW_BITS).reshape(NB * 8, 128)
+    if "b" in BAR:
+        block_rows, block_cols, block_count, _ = lax.optimization_barrier((block_rows, block_cols, block_count, got[0]))
     local_rows = block_rows.reshape(SLOTS)
     local_cols = block_cols.reshape(SLOTS)
     global_row = row_index * NB + local_rows
@@ -221,12 +248,19 @@
     live = jnp.arange(SLOTS, dtype=jnp.int32) < block_count.reshape(())
     weight = jnp.where(live, jnp.where(global_row == global_col, 0.5, 1.0), 0.0)
     weight = jnp.broadcast_to(weight.astype(jnp.float32)[:, None], (SLOTS, 128))
+    if "r" in BAR:
+        weight, _ = lax.optimization_barrier((weight, got[1]))
     w = relayout(block_values.reshape(SLOTS, BS * BS), weight)
     rows = place(local_rows, col_index, COL_BITS)
     cols = place(local_cols, row_index, ROW_BITS)
-    row_part = product(False, block_count, rows, cols, column_set, w)
+    if MODE == "a2a":
+        row_part = product(False, block_count, rows, local_cols * 16, column_set, w)
+    else:
+        row_part = product(False, block_count, rows, cols, column_set, w)
+    if "f" in BAR:
+        row_segment, _ = lax.optimization_barrier((row_segment, row_part[0]))
     col_part = product(True, block_count, rows, cols, row_segment, w)
-    mine_rows = scatter(*row_part, "col", COL_BITS)
+    mine_rows = scatter_by_four(row_part, "col", COL_BITS)
     mine_cols = scatter(*col_part, "row", ROW_BITS)
     return finish(mine_rows, mine_cols)
 

time: 72.8 us -> 63.6 us (0.87)
  waiting for transfers between devices: 29.6 us -> 19.4 us
  starting transfers between devices: 25.4 us -> 26.8 us
  Pallas kernels: 10.6 us -> 11.7 us
    ppermute x16 -> x14, waiting for transfers between devices: 29.6 us -> 15.6 us  [swap(): return lax.ppermute(x, axis, [(s, s ^ 1 << bit) for s in range(16)])]
    ppermute x0 -> x3, starting transfers between devices: none -> 4.18 us  [scatter_by_four(): lax.ppermute(parts[k], axis, [(s, s ^ masks[k]) for s in range(16)])]
    ppermute x0 -> x3, waiting for transfers between devices: none -> 3.75 us  [scatter_by_four(): lax.ppermute(parts[k], axis, [(s, s ^ masks[k]) for s in range(16)])]
    ppermute x16 -> x14, starting transfers between devices: 25.4 us -> 22.6 us  [swap(): return lax.ppermute(x, axis, [(s, s ^ 1 << bit) for s in range(16)])]
    pallas_call x2, Pallas kernels: 8.69 us -> 9.78 us  [product(): pl.pallas_call(backward_kernel if backward else forward_kernel, in_specs=...]
  transfers between devices with their start and end apart: 16 -> 17, of which waited for: 9 -> 7; matrix products, arithmetic and copies ran while one was open for 3% -> 3% of each run, Pallas kernels for 14% -> 10%
where the time goes in v4:
time: 63.6 us; the launch traced here: 63.4 us
  starting transfers between devices  26.8 us (42%)
  waiting for transfers between devices  19.4 us (31%)
  Pallas kernels  11.7 us (18%)
  local copies, waits for them, and re-layouts  3.14 us (5%)
  other arithmetic  1.6 us (3%)
  between operations  0.84 us (1%)
    ppermute x14, starting transfers between devices, swap(): return lax.ppermute(x, axis, [(s, s ^ 1 << bit) for s in range(16)])  22.6 us
    ppermute x14, waiting for transfers between devices, swap(): return lax.ppermute(x, axis, [(s, s ^ 1 << bit) for s in range(16)])  15.6 us
    pallas_call x2, Pallas kernels, product(): pl.pallas_call(backward_kernel if backward else forward_kernel, in_specs=...  9.78 us
    ppermute x3, starting transfers between devices, scatter_by_four(): lax.ppermute(parts[k], axis, [(s, s ^ masks[k]) for s in range(16)])  4.18 us
    ppermute x3, waiting for transfers between devices, scatter_by_four(): lax.ppermute(parts[k], axis, [(s, s ^ masks[k]) for s in range(16)])  3.75 us
    unnamed x10, local copies, waits for them, and re-layouts  2.25 us
  transfers between devices with their start and end apart: 17, of which 7 were waited for; matrix products, arithmetic and copies ran while one was open for 3% of the time, Pallas kernels for 10%

profile of v4, /device:TPU:6, one launch (start us, length us, event | category | flops | bytes accessed | tf_op | source)
XLA Modules:
  0.0 63.4 jit_solution(2499386537213752876)
XLA Ops:
  0.0 0.7 %reshape.94 = bf16[64,128]{1,0:T(8,128)(2,1)S(1)} reshape(bf16[8,1024]{1,0:T(8,128)(2,1)} %param.5) | data formatting | bytes 32768 | tf_op jit(solution)/shard_map/reshape | solution.py:234
  0.7 7.3 %collective-permute-start = (bf16[64,128]{1,0:T(8,128)(2,1)S(1)}, bf16[64,128]{1,0:T(8,128)(2,1)S(1)}, u32[]{:S(2)}, u32[]{:S(2)}) collective-permute-start(bf16[64,128]{1,0:T(8,128)(2,1)S(1)} %reshape.94), channel_id=1, source_target_pairs={{0,2},{1,3},{2,0},{3,1},{4,6},{5,7},{6,4},{7,5},{8,10},{9,11},{10,... | collective-permute-start | bytes 49160 | tf_op jit(solution)/shard_map/ppermute | solution.py:191
  8.0 1.4 %collective-permute-start.1 = (bf16[8,8,128]{2,1,0:T(8,128)(2,1)S(1)}, bf16[8,8,128]{2,1,0:T(8,128)(2,1)S(1)}, u32[]{:S(2)}, u32[]{:S(2)}) collective-permute-start(bf16[8,8,128]{2,1,0:T(8,128)(2,1)S(1)} %bitcast.15), channel_id=1, source_target_pairs={{0,128},{16,144},{32,160},{48,176},{64,192},{80,208},{96,224},{112... | collective-permute-start | bytes 49160 | tf_op jit(solution)/shard_map/ppermute | solution.py:191
  10.1 0.0 collective-permute-done
  10.1 3.2 %collective-permute-done.1 = bf16[8,8,128]{2,1,0:T(8,128)(2,1)S(1)} collective-permute-done((bf16[8,8,128]{2,1,0:T(8,128)(2,1)S(1)}, bf16[8,8,128]{2,1,0:T(8,128)(2,1)S(1)}, u32[]{:S(2)}, u32[]{:S(2)}) %collective-permute-start.1) | collective-permute-done | bytes 16416 | tf_op jit(solution)/shard_map/ppermute | solution.py:191
  13.3 0.8 %collective-permute-start.2 = (bf16[16,8,128]{2,1,0:T(8,128)(2,1)S(1)}, bf16[16,8,128]{2,1,0:T(8,128)(2,1)S(1)}, u32[]{:S(2)}, u32[]{:S(2)}) collective-permute-start(bf16[16,8,128]{2,1,0:T(8,128)(2,1)S(1)} %pad_maximum_fusion.4), channel_id=1, source_target_pairs={{0,64},{16,80},{32,96},{48,112},{64,0},{80,16},{96,32},{112,48},{1... | collective-permute-start | bytes 98312 | tf_op jit(solution)/shard_map/ppermute | solution.py:191
  14.1 0.7 %add_multiply_fusion = (s32[1,1,512]{2,1,0:T(1,128)S(1)}, s32[1,1,512]{2,1,0:T(1,128)S(1)}) fusion(s32[1,1,512]{2,1,0:T(1,128)} %param.8, s32[]{:T(128)S(6)} %axis_index.25, s32[1,1,512]{2,1,0:T(1,128)} %param.7, s32[]{:T(128)S(6)} %axis_index.22), kind=kLoop, calls=%fused_computation.31 | loop fusion | flops 21504 | bytes 8200 | tf_op jit(solution)/shard_map/mul | solution.py:228
  14.8 0.7 %compare_select_fusion = f32[1,1,512]{2,1,0:T(1,128)S(1)} fusion(s32[1,1,512]{2,1,0:T(1,128)} %param.7, s32[1,1,512]{2,1,0:T(1,128)} %param.8, s32[]{:T(128)S(6)} %mul.37, s32[]{:T(128)S(6)} %axis_index.22), kind=kLoop, calls=%fused_computation.30 | loop fusion | flops 4608 | bytes 6152 | tf_op jit(solution)/shard_map/jit(_where)/select_n | solution.py:249
  15.5 1.6 %collective-permute-start.5 = (bf16[128,128]{1,0:T(8,128)(2,1)S(1)}, bf16[128,128]{1,0:T(8,128)(2,1)S(1)}, u32[]{:S(2)}, u32[]{:S(2)}) collective-permute-start(bf16[128,128]{1,0:T(8,128)(2,1)S(1)} %pad_maximum_fusion.5), channel_id=1, source_target_pairs={{0,1},{1,0},{2,3},{3,2},{4,5},{5,4},{6,7},{7,6},{8,9},{9,8},{10,11... | collective-permute-start | bytes 98312 | tf_op jit(solution)/shard_map/ppermute | solution.py:191
  17.1 0.1 collective-permute-done.2
  17.2 1.1 %collective-permute-start.3 = (bf16[32,8,128]{2,1,0:T(8,128)(2,1)S(1)}, bf16[32,8,128]{2,1,0:T(8,128)(2,1)S(1)}, u32[]{:S(2)}, u32[]{:S(2)}) collective-permute-start(bf16[32,8,128]{2,1,0:T(8,128)(2,1)S(1)} %pad_maximum_fusion.2), channel_id=1, source_target_pairs={{0,32},{16,48},{32,0},{48,16},{64,96},{80,112},{96,64},{112,80},{1... | collective-permute-start | bytes 196616 | tf_op jit(solution)/shard_map/ppermute | solution.py:191
  18.3 2.1 %collective-permute-done.5 = bf16[128,128]{1,0:T(8,128)(2,1)S(1)} collective-permute-done((bf16[128,128]{1,0:T(8,128)(2,1)S(1)}, bf16[128,128]{1,0:T(8,128)(2,1)S(1)}, u32[]{:S(2)}, u32[]{:S(2)}) %collective-permute-start.5) | collective-permute-done | bytes 32800 | tf_op jit(solution)/shard_map/ppermute | solution.py:191
  20.4 0.1 broadcast_in_dim.21.weight_ref
  20.6 3.3 %collective-permute-start.11 = (bf16[256,128]{1,0:T(8,128)(2,1)S(1)}, bf16[256,128]{1,0:T(8,128)(2,1)S(1)}, u32[]{:S(2)}, u32[]{:S(2)}) collective-permute-start(bf16[256,128]{1,0:T(8,128)(2,1)S(1)} %pad_maximum_fusion.3), channel_id=1, source_target_pairs={{0,8},{1,9},{2,10},{3,11},{4,12},{5,13},{6,14},{7,15},{8,0},{9,1},... | collective-permute-start | bytes 196616 | tf_op jit(solution)/shard_map/ppermute | solution.py:191
  23.9 0.0 copy-start
  23.9 2.2 %copy-done = bf16[1,1,512,4096]{3,2,1,0:T(8,128)(2,1)S(1)} copy-done((bf16[1,1,512,4096]{3,2,1,0:T(8,128)(2,1)S(1)}, bf16[1,1,512,4096]{3,2,1,0:T(8,128)(2,1)}, u32[]{:S(2)}) %copy-start) | copy-done | bytes 4194328
  26.0 1.0 %relayout.1.w_ref = bf16[16384,128]{1,0:T(8,128)(2,1)S(1)} custom-call(bf16[512,4096]{1,0:T(8,128)(2,1)S(1)} %bitcast.9, f32[512,128]{1,0:T(8,128)S(1)} %broadcast_in_dim.21.weight_ref), custom_call_target="tpu_custom_call" | custom-call | tf_op jit(solution)/shard_map/relayout/pallas_call | solution.py:35
  27.1 0.0 collective-permute-done.3
  27.2 0.1 collective-permute-start.4
  27.3 0.0 collective-permute-done.11
  27.3 0.8 %collective-permute-start.12 = (bf16[512,128]{1,0:T(8,128)(2,1)S(1)}, bf16[512,128]{1,0:T(8,128)(2,1)S(1)}, u32[]{:S(2)}, u32[]{:S(2)}) collective-permute-start(bf16[512,128]{1,0:T(8,128)(2,1)S(1)} %pad_maximum_fusion.1), channel_id=1, source_target_pairs={{0,4},{1,5},{2,6},{3,7},{4,0},{5,1},{6,2},{7,3},{8,12},{9,13},{10,... | collective-permute-start | bytes 393224 | tf_op jit(solution)/shard_map/ppermute | solution.py:191
  28.1 0.4 collective-permute-done.4
  28.6 5.0 %forward.1 = (f32[256,128]{1,0:T(8,128)S(1)}, f32[256,128]{1,0:T(8,128)S(1)}, f32[256,128]{1,0:T(8,128)S(1)}, f32[256,128]{1,0:T(8,128)S(1)}) custom-call(s32[1,1]{1,0:T(1,128)} %copy.14.count_ref, s32[512]{0:T(512)S(1)} %bitcast.13, s32[512]{0:T(512)S(1)} %bitcast.11, bf16[1024,128]{1,0:T(8,128)(2,1)S(1)} %bitcast.10, bf16[16384,128]{1,0:T(8,128)(2,1)S(1)} %relayout.1.w_ref), custom_call_target="tpu_custom_call" | custom-call | tf_op jit(solution)/shard_map/forward/pallas_call | solution.py:152
  33.6 0.0 collective-permute-done.12
  33.7 4.7 %backward.1 = (f32[512,128]{1,0:T(8,128)S(1)}, f32[512,128]{1,0:T(8,128)S(1)}) custom-call(s32[1,1]{1,0:T(1,128)} %copy.14.count_ref, s32[512]{0:T(512)S(1)} %bitcast.14, s32[512]{0:T(512)S(1)} %bitcast.12, bf16[1024,128]{1,0:T(8,128)(2,1)S(1)} %constant_dynamic-update-slice_fusion.5.x_ref, bf16[16384,128]{1,0:T(8,128)(2,1)S(1)} %relayout.1.w_ref), custom_call_target="tpu_custom_call" | custom-call | tf_op jit(solution)/shard_map/backward/pallas_call | solution.py:152
  38.4 0.1 collective-permute-start.13
  38.5 1.1 %collective-permute-start.8 = (f32[256,128]{1,0:T(8,128)S(1)}, f32[256,128]{1,0:T(8,128)S(1)}, u32[]{:S(2)}, u32[]{:S(2)}) collective-permute-start(f32[256,128]{1,0:T(8,128)S(1)} %get-tuple-element.23), channel_id=1, source_target_pairs={{0,4},{1,5},{2,6},{3,7},{4,0},{5,1},{6,2},{7,3},{8,12},{9,13},{10,... | collective-permute-start | bytes 393224 | tf_op jit(solution)/shard_map/ppermute | solution.py:215
  39.6 1.0 %collective-permute-start.7 = (f32[256,128]{1,0:T(8,128)S(1)}, f32[256,128]{1,0:T(8,128)S(1)}, u32[]{:S(2)}, u32[]{:S(2)}) collective-permute-start(f32[256,128]{1,0:T(8,128)S(1)} %get-tuple-element.22), channel_id=1, source_target_pairs={{0,12},{1,13},{2,14},{3,15},{4,8},{5,9},{6,10},{7,11},{8,4},{9,5},... | collective-permute-start | bytes 393224 | tf_op jit(solution)/shard_map/ppermute | solution.py:215
  40.6 2.1 %collective-permute-start.6 = (f32[256,128]{1,0:T(8,128)S(1)}, f32[256,128]{1,0:T(8,128)S(1)}, u32[]{:S(2)}, u32[]{:S(2)}) collective-permute-start(f32[256,128]{1,0:T(8,128)S(1)} %get-tuple-element.21), channel_id=1, source_target_pairs={{0,8},{1,9},{2,10},{3,11},{4,12},{5,13},{6,14},{7,15},{8,0},{9,1},... | collective-permute-start | bytes 393224 | tf_op jit(solution)/shard_map/ppermute | solution.py:215
  42.7 0.0 collective-permute-done.13
  42.8 2.4 %collective-permute-start.14 = (f32[256,128]{1,0:T(8,128)S(1)}, f32[256,128]{1,0:T(8,128)S(1)}, u32[]{:S(2)}, u32[]{:S(2)}) collective-permute-start(f32[256,128]{1,0:T(8,128)S(1)} %get-tuple-element.28), channel_id=1, source_target_pairs={{0,32},{16,48},{32,0},{48,16},{64,96},{80,112},{96,64},{112,80},{1... | collective-permute-start | bytes 393224 | tf_op jit(solution)/shard_map/ppermute | solution.py:191
  45.1 0.0 collective-permute-done.8
  45.1 3.7 %collective-permute-done.7 = f32[256,128]{1,0:T(8,128)S(1)} collective-permute-done((f32[256,128]{1,0:T(8,128)S(1)}, f32[256,128]{1,0:T(8,128)S(1)}, u32[]{:S(2)}, u32[]{:S(2)}) %collective-permute-start.7) | collective-permute-done | bytes 131104 | tf_op jit(solution)/shard_map/ppermute | solution.py:215
  48.9 0.0 collective-permute-done.6
  48.9 1.1 %collective-permute-start.9 = (f32[128,128]{1,0:T(8,128)S(1)}, f32[128,128]{1,0:T(8,128)S(1)}, u32[]{:S(2)}, u32[]{:S(2)}) collective-permute-start(f32[128,128]{1,0:T(8,128)S(1)} %get-tuple-element.30), channel_id=1, source_target_pairs={{0,1},{1,0},{2,3},{3,2},{4,5},{5,4},{6,7},{7,6},{8,9},{9,8},{10,11... | collective-permute-start | bytes 196616 | tf_op jit(solution)/shard_map/ppermute | solution.py:191
  50.1 0.0 collective-permute-done.14
  50.1 0.1 collective-permute-start.15
  50.2 4.4 %collective-permute-done.9 = f32[128,128]{1,0:T(8,128)S(1)} collective-permute-done((f32[128,128]{1,0:T(8,128)S(1)}, f32[128,128]{1,0:T(8,128)S(1)}, u32[]{:S(2)}, u32[]{:S(2)}) %collective-permute-start.9) | collective-permute-done | bytes 65568 | tf_op jit(solution)/shard_map/ppermute | solution.py:191
  54.6 2.4 %collective-permute-start.10 = (f32[64,128]{1,0:T(8,128)S(1)}, f32[64,128]{1,0:T(8,128)S(1)}, u32[]{:S(2)}, u32[]{:S(2)}) collective-permute-start(f32[64,128]{1,0:T(8,128)S(1)} %get-tuple-element.35), channel_id=1, source_target_pairs={{0,2},{1,3},{2,0},{3,1},{4,6},{5,7},{6,4},{7,5},{8,10},{9,11},{10,... | collective-permute-start | bytes 98312 | tf_op jit(solution)/shard_map/ppermute | solution.py:191
  57.0 0.0 collective-permute-done.15
  57.0 0.1 collective-permute-start.16
  57.1 5.4 %collective-permute-done.10.a1_ref = f32[64,128]{1,0:T(8,128)S(1)} collective-permute-done((f32[64,128]{1,0:T(8,128)S(1)}, f32[64,128]{1,0:T(8,128)S(1)}, u32[]{:S(2)}, u32[]{:S(2)}) %collective-permute-start.10) | collective-permute-done | bytes 32800 | tf_op jit(solution)/shard_map/ppermute | solution.py:191
  62.5 0.0 collective-permute-done.16.b1_ref
  62.5 0.9 %finish.1 = f32[8,1024]{1,0:T(8,128)} custom-call(f32[64,128]{1,0:T(8,128)S(1)} %get-tuple-element.36.a0_ref, f32[64,128]{1,0:T(8,128)S(1)} %collective-permute-done.10.a1_ref, f32[64,128]{1,0:T(8,128)S(1)} %get-tuple-element.34.b0_ref, f32[64,128]{1,0:T(8,128)S(1)} %collective-permute-done.16.b1_ref), custom_call_target="tpu_custom_call" | custom-call | tf_op jit(solution)/shard_map/finish/pallas_call | solution.py:179
  (22 shorter events, 0.3 us)
Async XLA Ops:
  0.7 9.3 %collective-permute-start = (bf16[64,128]{1,0:T(8,128)(2,1)S(1)}, bf16[64,128]{1,0:T(8,128)(2,1)S(1)}, u32[]{:S(2)}, u32[]{:S(2)}) collective-permute-start(bf16[64,128]{1,0:T(8,128)(2,1)S(1)} %reshape.94), channel_id=1, source_target_pairs={{0,2},{1,3},{2,0},{3,1},{4,6},{5,7},{6,4},{7,5},{8,10},{9,11},{10,... | collective-permute-start | bytes 49160 | tf_op jit(solution)/shard_map/ppermute | solution.py:191
  8.0 5.2 %collective-permute-start.1 = (bf16[8,8,128]{2,1,0:T(8,128)(2,1)S(1)}, bf16[8,8,128]{2,1,0:T(8,128)(2,1)S(1)}, u32[]{:S(2)}, u32[]{:S(2)}) collective-permute-start(bf16[8,8,128]{2,1,0:T(8,128)(2,1)S(1)} %bitcast.15), channel_id=1, source_target_pairs={{0,128},{16,144},{32,160},{48,176},{64,192},{80,208},{96,224},{112... | collective-permute-start | bytes 49160 | tf_op jit(solution)/shard_map/ppermute | solution.py:191
  13.3 3.9 %collective-permute-start.2 = (bf16[16,8,128]{2,1,0:T(8,128)(2,1)S(1)}, bf16[16,8,128]{2,1,0:T(8,128)(2,1)S(1)}, u32[]{:S(2)}, u32[]{:S(2)}) collective-permute-start(bf16[16,8,128]{2,1,0:T(8,128)(2,1)S(1)} %pad_maximum_fusion.4), channel_id=1, source_target_pairs={{0,64},{16,80},{32,96},{48,112},{64,0},{80,16},{96,32},{112,48},{1... | collective-permute-start | bytes 98312 | tf_op jit(solution)/shard_map/ppermute | solution.py:191
  15.5 4.9 %collective-permute-start.5 = (bf16[128,128]{1,0:T(8,128)(2,1)S(1)}, bf16[128,128]{1,0:T(8,128)(2,1)S(1)}, u32[]{:S(2)}, u32[]{:S(2)}) collective-permute-start(bf16[128,128]{1,0:T(8,128)(2,1)S(1)} %pad_maximum_fusion.5), channel_id=1, source_target_pairs={{0,1},{1,0},{2,3},{3,2},{4,5},{5,4},{6,7},{7,6},{8,9},{9,8},{10,11... | collective-permute-start | bytes 98312 | tf_op jit(solution)/shard_map/ppermute | solution.py:191
  17.2 9.9 %collective-permute-start.3 = (bf16[32,8,128]{2,1,0:T(8,128)(2,1)S(1)}, bf16[32,8,128]{2,1,0:T(8,128)(2,1)S(1)}, u32[]{:S(2)}, u32[]{:S(2)}) collective-permute-start(bf16[32,8,128]{2,1,0:T(8,128)(2,1)S(1)} %pad_maximum_fusion.2), channel_id=1, source_target_pairs={{0,32},{16,48},{32,0},{48,16},{64,96},{80,112},{96,64},{112,80},{1... | collective-permute-start | bytes 196616 | tf_op jit(solution)/shard_map/ppermute | solution.py:191
  20.6 6.7 %collective-permute-start.11 = (bf16[256,128]{1,0:T(8,128)(2,1)S(1)}, bf16[256,128]{1,0:T(8,128)(2,1)S(1)}, u32[]{:S(2)}, u32[]{:S(2)}) collective-permute-start(bf16[256,128]{1,0:T(8,128)(2,1)S(1)} %pad_maximum_fusion.3), channel_id=1, source_target_pairs={{0,8},{1,9},{2,10},{3,11},{4,12},{5,13},{6,14},{7,15},{8,0},{9,1},... | collective-permute-start | bytes 196616 | tf_op jit(solution)/shard_map/ppermute | solution.py:191
  23.9 2.2 %copy-start = (bf16[1,1,512,4096]{3,2,1,0:T(8,128)(2,1)S(1)}, bf16[1,1,512,4096]{3,2,1,0:T(8,128)(2,1)}, u32[]{:S(2)}) copy-start(bf16[1,1,512,4096]{3,2,1,0:T(8,128)(2,1)} %param.6) | copy-start | bytes 12582916
  27.2 1.4 %collective-permute-start.4 = (bf16[64,8,128]{2,1,0:T(8,128)(2,1)S(1)}, bf16[64,8,128]{2,1,0:T(8,128)(2,1)S(1)}, u32[]{:S(2)}, u32[]{:S(2)}) collective-permute-start(bf16[64,8,128]{2,1,0:T(8,128)(2,1)S(1)} %pad_maximum_fusion), channel_id=1, source_target_pairs={{0,16},{16,0},{32,48},{48,32},{64,80},{80,64},{96,112},{112,96},{1... | collective-permute-start | bytes 393224 | tf_op jit(solution)/shard_map/ppermute | solution.py:191
  27.3 6.4 %collective-permute-start.12 = (bf16[512,128]{1,0:T(8,128)(2,1)S(1)}, bf16[512,128]{1,0:T(8,128)(2,1)S(1)}, u32[]{:S(2)}, u32[]{:S(2)}) collective-permute-start(bf16[512,128]{1,0:T(8,128)(2,1)S(1)} %pad_maximum_fusion.1), channel_id=1, source_target_pairs={{0,4},{1,5},{2,6},{3,7},{4,0},{5,1},{6,2},{7,3},{8,12},{9,13},{10,... | collective-permute-start | bytes 393224 | tf_op jit(solution)/shard_map/ppermute | solution.py:191
  38.4 4.3 %collective-permute-start.13 = (f32[512,128]{1,0:T(8,128)S(1)}, f32[512,128]{1,0:T(8,128)S(1)}, u32[]{:S(2)}, u32[]{:S(2)}) collective-permute-start(f32[512,128]{1,0:T(8,128)S(1)} %get-tuple-element.26), channel_id=1, source_target_pairs={{0,16},{16,0},{32,48},{48,32},{64,80},{80,64},{96,112},{112,96},{1... | collective-permute-start | bytes 786440 | tf_op jit(solution)/shard_map/ppermute | solution.py:191
  38.5 6.6 %collective-permute-start.8 = (f32[256,128]{1,0:T(8,128)S(1)}, f32[256,128]{1,0:T(8,128)S(1)}, u32[]{:S(2)}, u32[]{:S(2)}) collective-permute-start(f32[256,128]{1,0:T(8,128)S(1)} %get-tuple-element.23), channel_id=1, source_target_pairs={{0,4},{1,5},{2,6},{3,7},{4,0},{5,1},{6,2},{7,3},{8,12},{9,13},{10,... | collective-permute-start | bytes 393224 | tf_op jit(solution)/shard_map/ppermute | solution.py:215
  39.6 9.2 %collective-permute-start.7 = (f32[256,128]{1,0:T(8,128)S(1)}, f32[256,128]{1,0:T(8,128)S(1)}, u32[]{:S(2)}, u32[]{:S(2)}) collective-permute-start(f32[256,128]{1,0:T(8,128)S(1)} %get-tuple-element.22), channel_id=1, source_target_pairs={{0,12},{1,13},{2,14},{3,15},{4,8},{5,9},{6,10},{7,11},{8,4},{9,5},... | collective-permute-start | bytes 393224 | tf_op jit(solution)/shard_map/ppermute | solution.py:215
  40.6 8.3 %collective-permute-start.6 = (f32[256,128]{1,0:T(8,128)S(1)}, f32[256,128]{1,0:T(8,128)S(1)}, u32[]{:S(2)}, u32[]{:S(2)}) collective-permute-start(f32[256,128]{1,0:T(8,128)S(1)} %get-tuple-element.21), channel_id=1, source_target_pairs={{0,8},{1,9},{2,10},{3,11},{4,12},{5,13},{6,14},{7,15},{8,0},{9,1},... | collective-permute-start | bytes 393224 | tf_op jit(solution)/shard_map/ppermute | solution.py:215
  42.8 7.3 %collective-permute-start.14 = (f32[256,128]{1,0:T(8,128)S(1)}, f32[256,128]{1,0:T(8,128)S(1)}, u32[]{:S(2)}, u32[]{:S(2)}) collective-permute-start(f32[256,128]{1,0:T(8,128)S(1)} %get-tuple-element.28), channel_id=1, source_target_pairs={{0,32},{16,48},{32,0},{48,16},{64,96},{80,112},{96,64},{112,80},{1... | collective-permute-start | bytes 393224 | tf_op jit(solution)/shard_map/ppermute | solution.py:191
  48.9 5.6 %collective-permute-start.9 = (f32[128,128]{1,0:T(8,128)S(1)}, f32[128,128]{1,0:T(8,128)S(1)}, u32[]{:S(2)}, u32[]{:S(2)}) collective-permute-start(f32[128,128]{1,0:T(8,128)S(1)} %get-tuple-element.30), channel_id=1, source_target_pairs={{0,1},{1,0},{2,3},{3,2},{4,5},{5,4},{6,7},{7,6},{8,9},{9,8},{10,11... | collective-permute-start | bytes 196616 | tf_op jit(solution)/shard_map/ppermute | solution.py:191
  50.1 6.9 %collective-permute-start.15 = (f32[128,128]{1,0:T(8,128)S(1)}, f32[128,128]{1,0:T(8,128)S(1)}, u32[]{:S(2)}, u32[]{:S(2)}) collective-permute-start(f32[128,128]{1,0:T(8,128)S(1)} %get-tuple-element.32), channel_id=1, source_target_pairs={{0,64},{16,80},{32,96},{48,112},{64,0},{80,16},{96,32},{112,48},{1... | collective-permute-start | bytes 196616 | tf_op jit(solution)/shard_map/ppermute | solution.py:191
  54.6 7.9 %collective-permute-start.10 = (f32[64,128]{1,0:T(8,128)S(1)}, f32[64,128]{1,0:T(8,128)S(1)}, u32[]{:S(2)}, u32[]{:S(2)}) collective-permute-start(f32[64,128]{1,0:T(8,128)S(1)} %get-tuple-element.35), channel_id=1, source_target_pairs={{0,2},{1,3},{2,0},{3,1},{4,6},{5,7},{6,4},{7,5},{8,10},{9,11},{10,... | collective-permute-start | bytes 98312 | tf_op jit(solution)/shard_map/ppermute | solution.py:191
  57.0 5.5 %collective-permute-start.16 = (f32[64,128]{1,0:T(8,128)S(1)}, f32[64,128]{1,0:T(8,128)S(1)}, u32[]{:S(2)}, u32[]{:S(2)}) collective-permute-start(f32[64,128]{1,0:T(8,128)S(1)} %get-tuple-element.33), channel_id=1, source_target_pairs={{0,128},{16,144},{32,160},{48,176},{64,192},{80,208},{96,224},{112... | collective-permute-start | bytes 98312 | tf_op jit(solution)/shard_map/ppermute | solution.py:191

commit v5 on v3

--- a/solution.py
+++ b/solution.py
@@ -6,6 +6,7 @@
 from jax.experimental import pallas as pl
 from jax.experimental.pallas import tpu as pltpu
 from jax.sharding import PartitionSpec as P
+
 
 NV = 16
 BS = 64
@@ -19,28 +20,41 @@
 MIB = 1 << 20
 
 
-def relayout_kernel(v_ref, weight_ref, w_ref, f_ref):
-    weight = weight_ref[...]
-    for t in range(32):
-        x = v_ref[:, t * 128 : (t + 1) * 128].astype(jnp.float32) * weight
-        for h in range(GROUP // 8):
-            f_ref[pl.ds(h * 8 * PAD + t, 8, stride=PAD), :] = x[h * 8 : (h + 1) * 8]
-    for s in range(GROUP):
-        w_ref[s * 32 : (s + 1) * 32] = f_ref[s * PAD : s * PAD + 32].astype(jnp.bfloat16)
+def relayout_kernel(v_hbm, weight_ref, w_ref, v_ref, f_ref, sem):
+    copies = [
+        pltpu.make_async_copy(
+            v_hbm.at[pl.ds(i * GROUP, GROUP), :], v_ref.at[pl.ds(i * GROUP, GROUP), :], sem.at[i]
+        )
+        for i in range(SLOTS // GROUP)
+    ]
+    for copy in copies:
+        copy.start()
+    for i, copy in enumerate(copies):
+        copy.wait()
+        here = slice(i * GROUP, (i + 1) * GROUP)
+        weight = weight_ref[here, :]
+        for t in range(32):
+            x = v_ref[here, t * 128 : (t + 1) * 128].astype(jnp.float32) * weight
+            for h in range(GROUP // 8):
+                f_ref[pl.ds(h * 8 * PAD + t, 8, stride=PAD), :] = x[h * 8 : (h + 1) * 8]
+        for s in range(GROUP):
+            to = (i * GROUP + s) * 32
+            w_ref[to : to + 32] = f_ref[s * PAD : s * PAD + 32].astype(jnp.bfloat16)
 
 
 def relayout(values, weight):
+    vmem = pl.BlockSpec(memory_space=pltpu.VMEM)
     return pl.pallas_call(
         relayout_kernel,
-        grid=(SLOTS // GROUP,),
-        in_specs=[
-            pl.BlockSpec((GROUP, BS * BS), lambda i: (i, 0)),
-            pl.BlockSpec((GROUP, 128), lambda i: (i, 0)),
+        in_specs=[pl.BlockSpec(memory_space=pltpu.HBM), vmem],
+        out_specs=vmem,
+        out_shape=jax.ShapeDtypeStruct((SLOTS * 32, 128), jnp.bfloat16),
+        scratch_shapes=[
+            pltpu.VMEM((SLOTS, BS * BS), jnp.bfloat16),
+            pltpu.VMEM((GROUP * PAD, 128), jnp.float32),
+            pltpu.SemaphoreType.DMA((SLOTS // GROUP,)),
         ],
-        out_specs=pl.BlockSpec((GROUP * 32, 128), lambda i: (i, 0)),
-        out_shape=jax.ShapeDtypeStruct((SLOTS * 32, 128), jnp.bfloat16),
-        scratch_shapes=[pltpu.VMEM((GROUP * PAD, 128), jnp.float32)],
-        compiler_params=pltpu.CompilerParams(vmem_limit_bytes=16 * MIB),
+        compiler_params=pltpu.CompilerParams(vmem_limit_bytes=20 * MIB),
         name="relayout",
     )(values, weight)
 
@@ -73,7 +87,62 @@
     )
 
 
-def forward_kernel(count_ref, rows_ref, cols_ref, x_ref, w_ref, keep_ref, send_ref, xlo, xhi, acc):
+def to_fixed(totals, out):
+    peak = functools.reduce(jnp.maximum, [jnp.abs(total) for total in totals])
+    exponent = jnp.floor(jnp.log2(jnp.maximum(peak, 1e-30))) - 14.0
+    scale = jnp.exp2(-exponent)
+    for i in range(0, len(totals), 2):
+        fixed = jnp.concatenate([totals[i] * scale, totals[i + 1] * scale], 0)
+        fixed = jnp.clip(jnp.round(fixed), -32767.0, 32767.0)
+        out[i * 8 : i * 8 + 16, :] = fixed.astype(jnp.int32).astype(jnp.int16)
+    last = len(totals) * 8
+    exponent = jnp.concatenate([exponent, exponent], 0)
+    out[last : last + 16, :] = exponent.astype(jnp.int32).astype(jnp.int16)
+
+
+def from_fixed(ref):
+    last = ref.shape[0] - 16
+    scale = jnp.exp2(ref[last : last + 16, :].astype(jnp.int32).astype(jnp.float32))
+    return [
+        ref[i : i + 16, :].astype(jnp.int32).astype(jnp.float32) * scale
+        for i in range(0, last, 16)
+    ]
+
+
+def combine_kernel(own_ref, *refs):
+    *got, keep_ref, send_ref = refs
+    pieces = [from_fixed(ref) for ref in got]
+    count = own_ref.shape[0] // 16
+    totals = []
+    for i in range(count):
+        total = own_ref[i * 16 : (i + 1) * 16, :]
+        for piece in pieces:
+            total = total + piece[i]
+        if i < count // 2:
+            keep_ref[i * 16 : (i + 1) * 16, :] = total
+        else:
+            totals += [total[:8], total[8:]]
+    to_fixed(totals, send_ref)
+
+
+def combine(own, *got):
+    vmem = pl.BlockSpec(memory_space=pltpu.VMEM)
+    half = own.shape[0] // 2
+    return pl.pallas_call(
+        combine_kernel,
+        in_specs=[vmem] * (1 + len(got)),
+        out_specs=[vmem] * 2,
+        out_shape=[
+            jax.ShapeDtypeStruct((half, 128), jnp.float32),
+            jax.ShapeDtypeStruct((half + 16, 128), jnp.int16),
+        ],
+        compiler_params=pltpu.CompilerParams(vmem_limit_bytes=4 * MIB),
+        name="combine",
+    )(own, *got)
+
+
+def forward_kernel(count_ref, rows_ref, cols_ref, x_ref, w_ref, *outs_and_scratch):
+    *outs, xlo, xhi, acc = outs_and_scratch
     low = below((16, 128))
     for b in range(NB // 2):
         x = x_ref[b * 16 : (b + 1) * 16, :].astype(jnp.float32)
@@ -100,13 +169,20 @@
 
     lax.fori_loop(0, (count_ref[0, 0] + UNROLL - 1) // UNROLL, step, 0)
     low = below((8, 128))
-    for b in range(NB):
-        a0, a1 = acc[b * 16 : b * 16 + 8, :], acc[b * 16 + 8 : b * 16 + 16, :]
-        out, i = (keep_ref, b) if b < NB // 2 else (send_ref, b - NB // 2)
-        out[i * 8 : (i + 1) * 8, :] = jnp.where(low, a0, pltpu.roll(a1, 64, 1))
-
-
-def backward_kernel(count_ref, rows_ref, cols_ref, x_ref, w_ref, keep_ref, send_ref, xs, acc):
+    for part, out in enumerate(outs):
+        totals = []
+        for b in range(part * NB // 4, (part + 1) * NB // 4):
+            a0, a1 = acc[b * 16 : b * 16 + 8, :], acc[b * 16 + 8 : b * 16 + 16, :]
+            totals.append(jnp.where(low, a0, pltpu.roll(a1, 64, 1)))
+        if part == 0:
+            for i, total in enumerate(totals):
+                out[i * 8 : (i + 1) * 8, :] = total
+        else:
+            to_fixed(totals, out)
+
+
+def backward_kernel(count_ref, rows_ref, cols_ref, x_ref, w_ref, *outs_and_scratch):
+    *outs, xs, acc = outs_and_scratch
     order = even_odd(jnp.bfloat16)
     for b in range(NB // 8):
         x = jnp.dot(
@@ -135,7 +211,7 @@
     low = below((8, 128))
     for b in range(NB):
         a0, a1 = acc[b * 16 : b * 16 + 8, :], acc[b * 16 + 8 : b * 16 + 16, :]
-        out, i = (keep_ref, b) if b < NB // 2 else (send_ref, b - NB // 2)
+        out, i = outs[b * len(outs) // NB], b % (NB // len(outs))
         out[i * 8 : (i + 1) * 8, :] = jnp.where(
             low, a0 + pltpu.roll(a0, 64, 1), a1 + pltpu.roll(a1, 64, 1)
         )
@@ -144,12 +220,18 @@
 def product(backward, count, rows, cols, x, w):
     smem = pl.BlockSpec(memory_space=pltpu.SMEM)
     vmem = pl.BlockSpec(memory_space=pltpu.VMEM)
-    tables = 1 if backward else 2
+    if backward:
+        tables, outs = 1, 2
+        out_shape = [jax.ShapeDtypeStruct((NB * 4, 128), jnp.float32)] * 2
+    else:
+        tables, outs = 2, 4
+        out_shape = [jax.ShapeDtypeStruct((NB * 2, 128), jnp.float32)]
+        out_shape += [jax.ShapeDtypeStruct((NB * 2 + 16, 128), jnp.int16)] * 3
     return pl.pallas_call(
         backward_kernel if backward else forward_kernel,
         in_specs=[smem] * 3 + [vmem] * 2,
-        out_specs=[vmem] * 2,
-        out_shape=[jax.ShapeDtypeStruct((NB * 4, 128), jnp.float32)] * 2,
+        out_specs=[vmem] * outs,
+        out_shape=out_shape,
         scratch_shapes=[pltpu.VMEM((NB * NV, 128), jnp.bfloat16)] * tables
         + [pltpu.VMEM((NB * NV, 128), jnp.float32)],
         compiler_params=pltpu.CompilerParams(vmem_limit_bytes=16 * MIB),
@@ -160,7 +242,7 @@
 def finish_kernel(a0_ref, a1_ref, b0_ref, b1_ref, o_ref, tmp):
     back = even_odd(jnp.float32)
     tmp[...] = (b0_ref[...] + b1_ref[...]) + lax.dot_general(
-        a0_ref[...] + a1_ref[...],
+        a0_ref[...] + jnp.concatenate(from_fixed(a1_ref), 0),
         back,
         (((1,), (1,)), ((), ())),
         preferred_element_type=jnp.float32,
@@ -183,50 +265,63 @@
     )(*a, *b)
 
 
-def swap(x, axis, bit):
-    return lax.ppermute(x, axis, [(s, s ^ (1 << bit)) for s in range(16)])
-
-
-def gather(x, axis, bits):
+def swap(x, axis, mask):
+    return lax.ppermute(x, axis, [(s, s ^ mask) for s in range(16)])
+
+
+def gather(x, axis, bits, after=None):
     for bit in bits:
-        x = jnp.concatenate([x, swap(x, axis, bit)], 0)
+        y = swap(x, axis, 1 << bit)
+        if after is not None:
+            after.append(y)
+        x = jnp.concatenate([x, y], 0)
     return x
 
 
 def scatter(keep, send, axis, bits):
-    for k in reversed(range(4)):
-        received = swap(send, axis, bits[k])
+    for k in reversed(range(len(bits))):
+        received = swap(send, axis, 1 << bits[k])
         if k == 0:
             return keep, received
         half = keep.shape[0] // 2
         keep, send = keep[:half] + received[:half], keep[half:] + received[half:]
 
 
+def scatter_by_four(parts, axis, bits):
+    masks = [0, 1 << bits[2], 1 << bits[3], (1 << bits[2]) | (1 << bits[3])]
+    got = [swap(parts[k], axis, masks[k]) for k in (1, 3, 2)]
+    keep, send = combine(parts[0], *got)
+    keep, send = combine(keep, swap(send, axis, 1 << bits[1]))
+    return keep, swap(send, axis, 1 << bits[0])
+
+
 def place(position, me, bits):
     m = (position >> 3) ^ me
     slot = sum(((m >> bit) & 1) << k for k, bit in enumerate(bits))
     return (slot * 8 + (position & 7)) * 16
 
 
-def on_device(vectors, block_values, block_rows, block_cols, block_count):
+def apply(vectors, block_values, block_rows, block_cols, block_count):
     row_index = lax.axis_index("row")
     col_index = lax.axis_index("col")
-    piece = vectors.reshape(64, 128)
-    column_set = gather(piece, "row", ROW_BITS)
+    piece = lax.optimization_barrier(vectors.reshape(64, 128))
     row_segment = gather(piece, "col", COL_BITS)
+    column_set = gather(piece.reshape(8, 8, 128), "row", ROW_BITS).reshape(NB * 8, 128)
     local_rows = block_rows.reshape(SLOTS)
     local_cols = block_cols.reshape(SLOTS)
+    rows = place(local_rows, col_index, COL_BITS)
+    cols = place(local_cols, row_index, ROW_BITS)
     global_row = row_index * NB + local_rows
     global_col = ((local_cols >> 3) * 16 + col_index) * 8 + (local_cols & 7)
     live = jnp.arange(SLOTS, dtype=jnp.int32) < block_count.reshape(())
     weight = jnp.where(live, jnp.where(global_row == global_col, 0.5, 1.0), 0.0)
     weight = jnp.broadcast_to(weight.astype(jnp.float32)[:, None], (SLOTS, 128))
-    w = relayout(block_values.reshape(SLOTS, BS * BS), weight)
-    rows = place(local_rows, col_index, COL_BITS)
-    cols = place(local_cols, row_index, ROW_BITS)
+    values = pltpu.with_memory_space_constraint(block_values.reshape(SLOTS, BS * BS), pltpu.HBM)
+    w = relayout(values, weight)
     row_part = product(False, block_count, rows, cols, column_set, w)
+    row_segment, _ = lax.optimization_barrier((row_segment, row_part[0]))
     col_part = product(True, block_count, rows, cols, row_segment, w)
-    mine_rows = scatter(*row_part, "col", COL_BITS)
+    mine_rows = scatter_by_four(row_part, "col", COL_BITS)
     mine_cols = scatter(*col_part, "row", ROW_BITS)
     return finish(mine_rows, mine_cols)
 
@@ -240,5 +335,5 @@
         P("row", "col"),
     )
     return jax.shard_map(
-        on_device, mesh=mesh, in_specs=placed, out_specs=P(("row", "col"), None), check_vma=False
+        apply, mesh=mesh, in_specs=placed, out_specs=P(("row", "col"), None), check_vma=False
     )

time: 72.8 us -> 61.8 us (0.85)
  waiting for transfers between devices: 29.6 us -> 17.8 us
  Pallas kernels: 10.6 us -> 13.3 us
  local copies, waits for them, and re-layouts: 3.16 us -> 0.96 us
  starting transfers between devices: 25.4 us -> 26.2 us
    ppermute x16 -> x17, waiting for transfers between devices: 29.6 us -> 17.8 us  [swap(): return lax.ppermute(x, axis, [(s, s ^ mask) for s in range(16)])]
    unnamed x10 -> x8, local copies, waits for them, and re-layouts: 2.27 us -> 0.07 us
    pallas_call x1 -> x3, Pallas kernels: 1.03 us -> 2.57 us  [the longest x1 2.46 us: relayout(): pl.pallas_call(relayout_kernel, in_specs=[pl.BlockSpec(memory_space=pltpu...]
    pallas_call x2, Pallas kernels: 8.69 us -> 9.86 us  [product(): pl.pallas_call(backward_kernel if backward else forward_kernel, in_specs=...]
    ppermute x16 -> x17, starting transfers between devices: 25.4 us -> 26.2 us  [swap(): return lax.ppermute(x, axis, [(s, s ^ mask) for s in range(16)])]
  transfers between devices with their start and end apart: 16 -> 17, of which waited for: 9 -> 9; matrix products, arithmetic and copies ran while one was open for 3% -> 4% of each run, Pallas kernels for 14% -> 13%
where the time goes in v5:
time: 61.8 us; the launch traced here: 61.4 us
  starting transfers between devices  26.2 us (42%)
  waiting for transfers between devices  17.8 us (29%)
  Pallas kernels  13.3 us (22%)
  other arithmetic  2.23 us (4%)
  local copies, waits for them, and re-layouts  0.96 us (2%)
  between operations  0.87 us (1%)
    ppermute x17, starting transfers between devices, swap(): return lax.ppermute(x, axis, [(s, s ^ mask) for s in range(16)])  26.2 us
    ppermute x17, waiting for transfers between devices, swap(): return lax.ppermute(x, axis, [(s, s ^ mask) for s in range(16)])  17.8 us
    pallas_call x2, Pallas kernels, product(): pl.pallas_call(backward_kernel if backward else forward_kernel, in_specs=...  9.86 us
    pallas_call x1, Pallas kernels, relayout(): pl.pallas_call(relayout_kernel, in_specs=[pl.BlockSpec(memory_space=pltpu...  2.46 us
    mul x2, other arithmetic, place(): return (slot * 8 + (position & 7)) * 16  1.4 us
  transfers between devices with their start and end apart: 17, of which 9 were waited for; matrix products, arithmetic and copies ran while one was open for 4% of the time, Pallas kernels for 13%

profile of v5, /device:TPU:6, one launch (start us, length us, event | category | flops | bytes accessed | tf_op | source)
XLA Modules:
  0.0 61.4 jit_solution(12663995522714549656)
XLA Ops:
  0.0 0.7 %reshape.94 = bf16[64,128]{1,0:T(8,128)(2,1)S(1)} reshape(bf16[8,1024]{1,0:T(8,128)(2,1)} %param.5) | data formatting | bytes 32768 | tf_op jit(solution)/shard_map/reshape | solution.py:307
  0.7 7.3 %collective-permute-start.9 = (bf16[64,128]{1,0:T(8,128)(2,1)S(1)}, bf16[64,128]{1,0:T(8,128)(2,1)S(1)}, u32[]{:S(2)}, u32[]{:S(2)}) collective-permute-start(bf16[64,128]{1,0:T(8,128)(2,1)S(1)} %reshape.94), channel_id=1, source_target_pairs={{0,2},{1,3},{2,0},{3,1},{4,6},{5,7},{6,4},{7,5},{8,10},{9,11},{10,... | collective-permute-start | bytes 49160 | tf_op jit(solution)/shard_map/ppermute | solution.py:269
  8.0 1.4 %collective-permute-start = (bf16[8,8,128]{2,1,0:T(8,128)(2,1)S(1)}, bf16[8,8,128]{2,1,0:T(8,128)(2,1)S(1)}, u32[]{:S(2)}, u32[]{:S(2)}) collective-permute-start(bf16[8,8,128]{2,1,0:T(8,128)(2,1)S(1)} %bitcast.15), channel_id=1, source_target_pairs={{0,128},{16,144},{32,160},{48,176},{64,192},{80,208},{96,224},{112... | collective-permute-start | bytes 49160 | tf_op jit(solution)/shard_map/ppermute | solution.py:269
  10.1 0.7 %add_multiply_fusion = s32[1,1,512]{2,1,0:T(1,128)S(1)} fusion(s32[1,1,512]{2,1,0:T(1,128)} %param.8, s32[]{:T(128)S(6)} %axis_index.25), kind=kLoop, calls=%fused_computation.23 | loop fusion | flops 10752 | bytes 4100 | tf_op jit(solution)/shard_map/mul | solution.py:301
  10.8 0.7 %add_multiply_fusion.1 = s32[1,1,512]{2,1,0:T(1,128)S(1)} fusion(s32[1,1,512]{2,1,0:T(1,128)} %param.7, s32[]{:T(128)S(6)} %axis_index.22), kind=kLoop, calls=%fused_computation.24 | loop fusion | flops 10752 | bytes 4100 | tf_op jit(solution)/shard_map/mul | solution.py:301
  11.5 0.7 %compare_select_fusion = f32[1,1,512]{2,1,0:T(1,128)S(1)} fusion(s32[1,1,512]{2,1,0:T(1,128)} %param.7, s32[1,1,512]{2,1,0:T(1,128)} %param.8, s32[]{:T(128)S(6)} %mul.37, s32[]{:T(128)S(6)} %axis_index.22), kind=kLoop, calls=%fused_computation.22 | loop fusion | flops 4608 | bytes 6152 | tf_op jit(solution)/shard_map/jit(_where)/select_n | solution.py:317
  12.2 0.1 broadcast_in_dim.21.weight_ref
  12.3 2.5 %relayout.1.w_ref = bf16[16384,128]{1,0:T(8,128)(2,1)S(1)} custom-call(bf16[512,4096]{1,0:T(8,128)(2,1)} %bitcast.14, f32[512,128]{1,0:T(8,128)S(1)} %broadcast_in_dim.21.weight_ref), custom_call_target="tpu_custom_call" | custom-call | tf_op jit(solution)/shard_map/relayout/pallas_call | solution.py:47
  14.8 0.0 collective-permute-done
  14.8 0.1 collective-permute-start.1
  14.9 0.0 collective-permute-done.9
  15.0 1.6 %collective-permute-start.10 = (bf16[128,128]{1,0:T(8,128)(2,1)S(1)}, bf16[128,128]{1,0:T(8,128)(2,1)S(1)}, u32[]{:S(2)}, u32[]{:S(2)}) collective-permute-start(bf16[128,128]{1,0:T(8,128)(2,1)S(1)} %pad_maximum_fusion.5), channel_id=1, source_target_pairs={{0,1},{1,0},{2,3},{3,2},{4,5},{5,4},{6,7},{7,6},{8,9},{9,8},{10,11... | collective-permute-start | bytes 98312 | tf_op jit(solution)/shard_map/ppermute | solution.py:269
  16.5 2.3 %collective-permute-done.1 = bf16[16,8,128]{2,1,0:T(8,128)(2,1)S(1)} collective-permute-done((bf16[16,8,128]{2,1,0:T(8,128)(2,1)S(1)}, bf16[16,8,128]{2,1,0:T(8,128)(2,1)S(1)}, u32[]{:S(2)}, u32[]{:S(2)}) %collective-permute-start.1) | collective-permute-done | bytes 32800 | tf_op jit(solution)/shard_map/ppermute | solution.py:269
  18.8 1.1 %collective-permute-start.2 = (bf16[32,8,128]{2,1,0:T(8,128)(2,1)S(1)}, bf16[32,8,128]{2,1,0:T(8,128)(2,1)S(1)}, u32[]{:S(2)}, u32[]{:S(2)}) collective-permute-start(bf16[32,8,128]{2,1,0:T(8,128)(2,1)S(1)} %pad_maximum_fusion.2), channel_id=1, source_target_pairs={{0,32},{16,48},{32,0},{48,16},{64,96},{80,112},{96,64},{112,80},{1... | collective-permute-start | bytes 196616 | tf_op jit(solution)/shard_map/ppermute | solution.py:269
  20.0 0.0 collective-permute-done.10
  20.0 3.3 %collective-permute-start.11 = (bf16[256,128]{1,0:T(8,128)(2,1)S(1)}, bf16[256,128]{1,0:T(8,128)(2,1)S(1)}, u32[]{:S(2)}, u32[]{:S(2)}) collective-permute-start(bf16[256,128]{1,0:T(8,128)(2,1)S(1)} %pad_maximum_fusion.3), channel_id=1, source_target_pairs={{0,8},{1,9},{2,10},{3,11},{4,12},{5,13},{6,14},{7,15},{8,0},{9,1},... | collective-permute-start | bytes 196616 | tf_op jit(solution)/shard_map/ppermute | solution.py:269
  23.3 0.0 collective-permute-done.2
  23.3 0.1 collective-permute-start.3
  23.4 2.4 %collective-permute-done.11 = bf16[256,128]{1,0:T(8,128)(2,1)S(1)} collective-permute-done((bf16[256,128]{1,0:T(8,128)(2,1)S(1)}, bf16[256,128]{1,0:T(8,128)(2,1)S(1)}, u32[]{:S(2)}, u32[]{:S(2)}) %collective-permute-start.11) | collective-permute-done | bytes 65568 | tf_op jit(solution)/shard_map/ppermute | solution.py:269
  25.8 1.7 %collective-permute-start.12 = (bf16[512,128]{1,0:T(8,128)(2,1)S(1)}, bf16[512,128]{1,0:T(8,128)(2,1)S(1)}, u32[]{:S(2)}, u32[]{:S(2)}) collective-permute-start(bf16[512,128]{1,0:T(8,128)(2,1)S(1)} %pad_maximum_fusion.1), channel_id=1, source_target_pairs={{0,4},{1,5},{2,6},{3,7},{4,0},{5,1},{6,2},{7,3},{8,12},{9,13},{10,... | collective-permute-start | bytes 393224 | tf_op jit(solution)/shard_map/ppermute | solution.py:269
  27.5 0.0 collective-permute-done.3
  27.6 5.1 %forward.1 = (f32[256,128]{1,0:T(8,128)S(1)}, s16[272,128]{1,0:T(8,128)(2,1)S(1)}, s16[272,128]{1,0:T(8,128)(2,1)S(1)}, s16[272,128]{1,0:T(8,128)(2,1)S(1)}) custom-call(s32[1,1]{1,0:T(1,128)} %copy.14.count_ref, s32[512]{0:T(512)S(1)} %bitcast.12, s32[512]{0:T(512)S(1)} %bitcast.10, bf16[1024,128]{1,0:T(8,128)(2,1)S(1)} %bitcast.9, ...), custom_call_target="tpu_custom_call" | custom-call | tf_op jit(solution)/shard_map/forward/pallas_call | solution.py:230
  32.7 0.0 collective-permute-done.12
  32.7 4.7 %backward.1 = (f32[512,128]{1,0:T(8,128)S(1)}, f32[512,128]{1,0:T(8,128)S(1)}) custom-call(s32[1,1]{1,0:T(1,128)} %copy.14.count_ref, s32[512]{0:T(512)S(1)} %bitcast.13, s32[512]{0:T(512)S(1)} %bitcast.11, bf16[1024,128]{1,0:T(8,128)(2,1)S(1)} %constant_dynamic-update-slice_fusion.5.x_ref, bf16[16384,128]{1,0:T(8,128)(2,1)S(1)} %relayout.1.w_ref), custom_call_target="tpu_custom_call" | custom-call | tf_op jit(solution)/shard_map/backward/pallas_call | solution.py:230
  37.5 0.1 collective-permute-start.13
  37.6 1.5 %collective-permute-done.13 = f32[512,128]{1,0:T(8,128)S(1)} collective-permute-done((f32[512,128]{1,0:T(8,128)S(1)}, f32[512,128]{1,0:T(8,128)S(1)}, u32[]{:S(2)}, u32[]{:S(2)}) %collective-permute-start.13) | collective-permute-done | bytes 262176 | tf_op jit(solution)/shard_map/ppermute | solution.py:269
  39.1 1.1 %collective-permute-start.14 = (f32[256,128]{1,0:T(8,128)S(1)}, f32[256,128]{1,0:T(8,128)S(1)}, u32[]{:S(2)}, u32[]{:S(2)}) collective-permute-start(f32[256,128]{1,0:T(8,128)S(1)} %get-tuple-element.28), channel_id=1, source_target_pairs={{0,32},{16,48},{32,0},{48,16},{64,96},{80,112},{96,64},{112,80},{1... | collective-permute-start | bytes 393224 | tf_op jit(solution)/shard_map/ppermute | solution.py:269
  40.2 1.8 %collective-permute-start.4 = (s16[272,128]{1,0:T(8,128)(2,1)S(1)}, s16[272,128]{1,0:T(8,128)(2,1)S(1)}, u32[]{:S(2)}, u32[]{:S(2)}) collective-permute-start(s16[272,128]{1,0:T(8,128)(2,1)S(1)} %get-tuple-element.17), channel_id=1, source_target_pairs={{0,8},{1,9},{2,10},{3,11},{4,12},{5,13},{6,14},{7,15},{8,0},{9,1},... | collective-permute-start | bytes 208904 | tf_op jit(solution)/shard_map/ppermute | solution.py:269
  42.0 1.4 %collective-permute-start.5 = (s16[272,128]{1,0:T(8,128)(2,1)S(1)}, s16[272,128]{1,0:T(8,128)(2,1)S(1)}, u32[]{:S(2)}, u32[]{:S(2)}) collective-permute-start(s16[272,128]{1,0:T(8,128)(2,1)S(1)} %get-tuple-element.18), channel_id=1, source_target_pairs={{0,12},{1,13},{2,14},{3,15},{4,8},{5,9},{6,10},{7,11},{8,4},{9,5},... | collective-permute-start | bytes 208904 | tf_op jit(solution)/shard_map/ppermute | solution.py:269
  43.4 0.3 collective-permute-start.6
  43.7 1.1 %collective-permute-done.14 = f32[256,128]{1,0:T(8,128)S(1)} collective-permute-done((f32[256,128]{1,0:T(8,128)S(1)}, f32[256,128]{1,0:T(8,128)S(1)}, u32[]{:S(2)}, u32[]{:S(2)}) %collective-permute-start.14) | collective-permute-done | bytes 131104 | tf_op jit(solution)/shard_map/ppermute | solution.py:269
  44.8 0.1 collective-permute-start.15
  44.9 1.2 %collective-permute-done.4.refs_0_ = s16[272,128]{1,0:T(8,128)(2,1)S(1)} collective-permute-done((s16[272,128]{1,0:T(8,128)(2,1)S(1)}, s16[272,128]{1,0:T(8,128)(2,1)S(1)}, u32[]{:S(2)}, u32[]{:S(2)}) %collective-permute-start.4) | collective-permute-done | bytes 69664 | tf_op jit(solution)/shard_map/ppermute | solution.py:269
  46.1 1.4 %collective-permute-done.5.refs_1_ = s16[272,128]{1,0:T(8,128)(2,1)S(1)} collective-permute-done((s16[272,128]{1,0:T(8,128)(2,1)S(1)}, s16[272,128]{1,0:T(8,128)(2,1)S(1)}, u32[]{:S(2)}, u32[]{:S(2)}) %collective-permute-start.5) | collective-permute-done | bytes 69664 | tf_op jit(solution)/shard_map/ppermute | solution.py:269
  47.5 0.1 collective-permute-done.6.refs_2_
  47.7 0.1 combine.2
  47.8 2.6 %collective-permute-start.7 = (s16[144,128]{1,0:T(8,128)(2,1)S(1)}, s16[144,128]{1,0:T(8,128)(2,1)S(1)}, u32[]{:S(2)}, u32[]{:S(2)}) collective-permute-start(s16[144,128]{1,0:T(8,128)(2,1)S(1)} %get-tuple-element.21), channel_id=1, source_target_pairs={{0,1},{1,0},{2,3},{3,2},{4,5},{5,4},{6,7},{7,6},{8,9},{9,8},{10,11... | collective-permute-start | bytes 110600 | tf_op jit(solution)/shard_map/ppermute | solution.py:269
  50.3 0.0 collective-permute-done.15
  50.3 0.1 collective-permute-start.16
  50.4 2.3 %collective-permute-done.7.refs_0_ = s16[144,128]{1,0:T(8,128)(2,1)S(1)} collective-permute-done((s16[144,128]{1,0:T(8,128)(2,1)S(1)}, s16[144,128]{1,0:T(8,128)(2,1)S(1)}, u32[]{:S(2)}, u32[]{:S(2)}) %collective-permute-start.7) | collective-permute-done | bytes 36896 | tf_op jit(solution)/shard_map/ppermute | solution.py:269
  52.8 2.4 %collective-permute-start.8 = (s16[80,128]{1,0:T(8,128)(2,1)S(1)}, s16[80,128]{1,0:T(8,128)(2,1)S(1)}, u32[]{:S(2)}, u32[]{:S(2)}) collective-permute-start(s16[80,128]{1,0:T(8,128)(2,1)S(1)} %get-tuple-element.23), channel_id=1, source_target_pairs={{0,2},{1,3},{2,0},{3,1},{4,6},{5,7},{6,4},{7,5},{8,10},{9,11},{10,... | collective-permute-start | bytes 61448 | tf_op jit(solution)/shard_map/ppermute | solution.py:269
  55.1 5.4 %collective-permute-done.8.a1_ref = s16[80,128]{1,0:T(8,128)(2,1)S(1)} collective-permute-done((s16[80,128]{1,0:T(8,128)(2,1)S(1)}, s16[80,128]{1,0:T(8,128)(2,1)S(1)}, u32[]{:S(2)}, u32[]{:S(2)}) %collective-permute-start.8) | collective-permute-done | bytes 20512 | tf_op jit(solution)/shard_map/ppermute | solution.py:269
  60.5 0.0 collective-permute-done.16.b1_ref
  60.5 0.9 %finish.1 = f32[8,1024]{1,0:T(8,128)} custom-call(f32[64,128]{1,0:T(8,128)S(1)} %get-tuple-element.22.a0_ref, s16[80,128]{1,0:T(8,128)(2,1)S(1)} %collective-permute-done.8.a1_ref, f32[64,128]{1,0:T(8,128)S(1)} %get-tuple-element.32.b0_ref, f32[64,128]{1,0:T(8,128)S(1)} %collective-permute-done.16.b1_ref), custom_call_target="tpu_custom_call" | custom-call | tf_op jit(solution)/shard_map/finish/pallas_call | solution.py:257
  (21 shorter events, 0.2 us)
Async XLA Ops:
  0.7 14.2 %collective-permute-start.9 = (bf16[64,128]{1,0:T(8,128)(2,1)S(1)}, bf16[64,128]{1,0:T(8,128)(2,1)S(1)}, u32[]{:S(2)}, u32[]{:S(2)}) collective-permute-start(bf16[64,128]{1,0:T(8,128)(2,1)S(1)} %reshape.94), channel_id=1, source_target_pairs={{0,2},{1,3},{2,0},{3,1},{4,6},{5,7},{6,4},{7,5},{8,10},{9,11},{10,... | collective-permute-start | bytes 49160 | tf_op jit(solution)/shard_map/ppermute | solution.py:269
  8.0 6.8 %collective-permute-start = (bf16[8,8,128]{2,1,0:T(8,128)(2,1)S(1)}, bf16[8,8,128]{2,1,0:T(8,128)(2,1)S(1)}, u32[]{:S(2)}, u32[]{:S(2)}) collective-permute-start(bf16[8,8,128]{2,1,0:T(8,128)(2,1)S(1)} %bitcast.15), channel_id=1, source_target_pairs={{0,128},{16,144},{32,160},{48,176},{64,192},{80,208},{96,224},{112... | collective-permute-start | bytes 49160 | tf_op jit(solution)/shard_map/ppermute | solution.py:269
  14.8 4.0 %collective-permute-start.1 = (bf16[16,8,128]{2,1,0:T(8,128)(2,1)S(1)}, bf16[16,8,128]{2,1,0:T(8,128)(2,1)S(1)}, u32[]{:S(2)}, u32[]{:S(2)}) collective-permute-start(bf16[16,8,128]{2,1,0:T(8,128)(2,1)S(1)} %pad_maximum_fusion.4), channel_id=1, source_target_pairs={{0,64},{16,80},{32,96},{48,112},{64,0},{80,16},{96,32},{112,48},{1... | collective-permute-start | bytes 98312 | tf_op jit(solution)/shard_map/ppermute | solution.py:269
  15.0 5.0 %collective-permute-start.10 = (bf16[128,128]{1,0:T(8,128)(2,1)S(1)}, bf16[128,128]{1,0:T(8,128)(2,1)S(1)}, u32[]{:S(2)}, u32[]{:S(2)}) collective-permute-start(bf16[128,128]{1,0:T(8,128)(2,1)S(1)} %pad_maximum_fusion.5), channel_id=1, source_target_pairs={{0,1},{1,0},{2,3},{3,2},{4,5},{5,4},{6,7},{7,6},{8,9},{9,8},{10,11... | collective-permute-start | bytes 98312 | tf_op jit(solution)/shard_map/ppermute | solution.py:269
  18.8 4.4 %collective-permute-start.2 = (bf16[32,8,128]{2,1,0:T(8,128)(2,1)S(1)}, bf16[32,8,128]{2,1,0:T(8,128)(2,1)S(1)}, u32[]{:S(2)}, u32[]{:S(2)}) collective-permute-start(bf16[32,8,128]{2,1,0:T(8,128)(2,1)S(1)} %pad_maximum_fusion.2), channel_id=1, source_target_pairs={{0,32},{16,48},{32,0},{48,16},{64,96},{80,112},{96,64},{112,80},{1... | collective-permute-start | bytes 196616 | tf_op jit(solution)/shard_map/ppermute | solution.py:269
  20.0 5.9 %collective-permute-start.11 = (bf16[256,128]{1,0:T(8,128)(2,1)S(1)}, bf16[256,128]{1,0:T(8,128)(2,1)S(1)}, u32[]{:S(2)}, u32[]{:S(2)}) collective-permute-start(bf16[256,128]{1,0:T(8,128)(2,1)S(1)} %pad_maximum_fusion.3), channel_id=1, source_target_pairs={{0,8},{1,9},{2,10},{3,11},{4,12},{5,13},{6,14},{7,15},{8,0},{9,1},... | collective-permute-start | bytes 196616 | tf_op jit(solution)/shard_map/ppermute | solution.py:269
  23.3 4.2 %collective-permute-start.3 = (bf16[64,8,128]{2,1,0:T(8,128)(2,1)S(1)}, bf16[64,8,128]{2,1,0:T(8,128)(2,1)S(1)}, u32[]{:S(2)}, u32[]{:S(2)}) collective-permute-start(bf16[64,8,128]{2,1,0:T(8,128)(2,1)S(1)} %pad_maximum_fusion), channel_id=1, source_target_pairs={{0,16},{16,0},{32,48},{48,32},{64,80},{80,64},{96,112},{112,96},{1... | collective-permute-start | bytes 393224 | tf_op jit(solution)/shard_map/ppermute | solution.py:269
  25.8 6.9 %collective-permute-start.12 = (bf16[512,128]{1,0:T(8,128)(2,1)S(1)}, bf16[512,128]{1,0:T(8,128)(2,1)S(1)}, u32[]{:S(2)}, u32[]{:S(2)}) collective-permute-start(bf16[512,128]{1,0:T(8,128)(2,1)S(1)} %pad_maximum_fusion.1), channel_id=1, source_target_pairs={{0,4},{1,5},{2,6},{3,7},{4,0},{5,1},{6,2},{7,3},{8,12},{9,13},{10,... | collective-permute-start | bytes 393224 | tf_op jit(solution)/shard_map/ppermute | solution.py:269
  37.5 1.6 %collective-permute-start.13 = (f32[512,128]{1,0:T(8,128)S(1)}, f32[512,128]{1,0:T(8,128)S(1)}, u32[]{:S(2)}, u32[]{:S(2)}) collective-permute-start(f32[512,128]{1,0:T(8,128)S(1)} %get-tuple-element.26), channel_id=1, source_target_pairs={{0,16},{16,0},{32,48},{48,32},{64,80},{80,64},{96,112},{112,96},{1... | collective-permute-start | bytes 786440 | tf_op jit(solution)/shard_map/ppermute | solution.py:269
  39.1 5.6 %collective-permute-start.14 = (f32[256,128]{1,0:T(8,128)S(1)}, f32[256,128]{1,0:T(8,128)S(1)}, u32[]{:S(2)}, u32[]{:S(2)}) collective-permute-start(f32[256,128]{1,0:T(8,128)S(1)} %get-tuple-element.28), channel_id=1, source_target_pairs={{0,32},{16,48},{32,0},{48,16},{64,96},{80,112},{96,64},{112,80},{1... | collective-permute-start | bytes 393224 | tf_op jit(solution)/shard_map/ppermute | solution.py:269
  40.2 5.9 %collective-permute-start.4 = (s16[272,128]{1,0:T(8,128)(2,1)S(1)}, s16[272,128]{1,0:T(8,128)(2,1)S(1)}, u32[]{:S(2)}, u32[]{:S(2)}) collective-permute-start(s16[272,128]{1,0:T(8,128)(2,1)S(1)} %get-tuple-element.17), channel_id=1, source_target_pairs={{0,8},{1,9},{2,10},{3,11},{4,12},{5,13},{6,14},{7,15},{8,0},{9,1},... | collective-permute-start | bytes 208904 | tf_op jit(solution)/shard_map/ppermute | solution.py:269
  42.0 5.5 %collective-permute-start.5 = (s16[272,128]{1,0:T(8,128)(2,1)S(1)}, s16[272,128]{1,0:T(8,128)(2,1)S(1)}, u32[]{:S(2)}, u32[]{:S(2)}) collective-permute-start(s16[272,128]{1,0:T(8,128)(2,1)S(1)} %get-tuple-element.18), channel_id=1, source_target_pairs={{0,12},{1,13},{2,14},{3,15},{4,8},{5,9},{6,10},{7,11},{8,4},{9,5},... | collective-permute-start | bytes 208904 | tf_op jit(solution)/shard_map/ppermute | solution.py:269
  43.4 4.3 %collective-permute-start.6 = (s16[272,128]{1,0:T(8,128)(2,1)S(1)}, s16[272,128]{1,0:T(8,128)(2,1)S(1)}, u32[]{:S(2)}, u32[]{:S(2)}) collective-permute-start(s16[272,128]{1,0:T(8,128)(2,1)S(1)} %get-tuple-element.19), channel_id=1, source_target_pairs={{0,4},{1,5},{2,6},{3,7},{4,0},{5,1},{6,2},{7,3},{8,12},{9,13},{10,... | collective-permute-start | bytes 208904 | tf_op jit(solution)/shard_map/ppermute | solution.py:269
  44.8 5.5 %collective-permute-start.15 = (f32[128,128]{1,0:T(8,128)S(1)}, f32[128,128]{1,0:T(8,128)S(1)}, u32[]{:S(2)}, u32[]{:S(2)}) collective-permute-start(f32[128,128]{1,0:T(8,128)S(1)} %get-tuple-element.30), channel_id=1, source_target_pairs={{0,64},{16,80},{32,96},{48,112},{64,0},{80,16},{96,32},{112,48},{1... | collective-permute-start | bytes 196616 | tf_op jit(solution)/shard_map/ppermute | solution.py:269
  47.8 5.0 %collective-permute-start.7 = (s16[144,128]{1,0:T(8,128)(2,1)S(1)}, s16[144,128]{1,0:T(8,128)(2,1)S(1)}, u32[]{:S(2)}, u32[]{:S(2)}) collective-permute-start(s16[144,128]{1,0:T(8,128)(2,1)S(1)} %get-tuple-element.21), channel_id=1, source_target_pairs={{0,1},{1,0},{2,3},{3,2},{4,5},{5,4},{6,7},{7,6},{8,9},{9,8},{10,11... | collective-permute-start | bytes 110600 | tf_op jit(solution)/shard_map/ppermute | solution.py:269
  50.3 10.2 %collective-permute-start.16 = (f32[64,128]{1,0:T(8,128)S(1)}, f32[64,128]{1,0:T(8,128)S(1)}, u32[]{:S(2)}, u32[]{:S(2)}) collective-permute-start(f32[64,128]{1,0:T(8,128)S(1)} %get-tuple-element.31), channel_id=1, source_target_pairs={{0,128},{16,144},{32,160},{48,176},{64,192},{80,208},{96,224},{112... | collective-permute-start | bytes 98312 | tf_op jit(solution)/shard_map/ppermute | solution.py:269
  52.8 7.8 %collective-permute-start.8 = (s16[80,128]{1,0:T(8,128)(2,1)S(1)}, s16[80,128]{1,0:T(8,128)(2,1)S(1)}, u32[]{:S(2)}, u32[]{:S(2)}) collective-permute-start(s16[80,128]{1,0:T(8,128)(2,1)S(1)} %get-tuple-element.23), channel_id=1, source_target_pairs={{0,2},{1,3},{2,0},{3,1},{4,6},{5,7},{6,4},{7,5},{8,10},{9,11},{10,... | collective-permute-start | bytes 61448 | tf_op jit(solution)/shard_map/ppermute | solution.py:269

commit v6 on v5

--- a/solution.py
+++ b/solution.py
@@ -14,7 +14,7 @@
 SLOTS = 512
 GROUP = 128
 PAD = 33
-UNROLL = 64
+UNROLL = 256
 ROW_BITS = (3, 2, 1, 0)
 COL_BITS = (1, 0, 3, 2)
 MIB = 1 << 20
@@ -101,6 +101,8 @@
 
 
 def from_fixed(ref):
+    if ref.dtype == jnp.float32:
+        return [ref[i : i + 16, :] for i in range(0, ref.shape[0], 16)]
     last = ref.shape[0] - 16
     scale = jnp.exp2(ref[last : last + 16, :].astype(jnp.int32).astype(jnp.float32))
     return [
@@ -241,7 +243,7 @@
 
 def finish_kernel(a0_ref, a1_ref, b0_ref, b1_ref, o_ref, tmp):
     back = even_odd(jnp.float32)
-    tmp[...] = (b0_ref[...] + b1_ref[...]) + lax.dot_general(
+    tmp[...] = (b0_ref[...] + jnp.concatenate(from_fixed(b1_ref), 0)) + lax.dot_general(
         a0_ref[...] + jnp.concatenate(from_fixed(a1_ref), 0),
         back,
         (((1,), (1,)), ((), ())),
@@ -279,12 +281,11 @@
 
 
 def scatter(keep, send, axis, bits):
-    for k in reversed(range(len(bits))):
+    for k in reversed(range(4)):
         received = swap(send, axis, 1 << bits[k])
         if k == 0:
             return keep, received
-        half = keep.shape[0] // 2
-        keep, send = keep[:half] + received[:half], keep[half:] + received[half:]
+        keep, send = combine(keep, received)
 
 
 def scatter_by_four(parts, axis, bits):

time: 61.8 us -> 59.4 us (0.961)
  waiting for transfers between devices: 17.8 us -> 17 us
  Pallas kernels: 13.3 us -> 12.6 us
  starting transfers between devices: 26.2 us -> 25.5 us
    pallas_call x2, Pallas kernels: 9.86 us -> 9.01 us  [product(): pl.pallas_call(backward_kernel if backward else forward_kernel, in_specs=...]
    ppermute x17, waiting for transfers between devices: 17.8 us -> 17 us  [swap(): return lax.ppermute(x, axis, [(s, s ^ mask) for s in range(16)])]
    ppermute x17, starting transfers between devices: 26.2 us -> 25.5 us  [swap(): return lax.ppermute(x, axis, [(s, s ^ mask) for s in range(16)])]
  transfers between devices with their start and end apart: 17 -> 17, of which waited for: 9 -> 7; matrix products, arithmetic and copies ran while one was open for 4% -> 4% of each run, Pallas kernels for 13% -> 13%
where the time goes in v6:
time: 59.4 us; the launch traced here: 59.1 us
  starting transfers between devices  25.5 us (43%)
  waiting for transfers between devices  17 us (29%)
  Pallas kernels  12.6 us (21%)
  other arithmetic  2.17 us (4%)
  local copies, waits for them, and re-layouts  0.96 us (2%)
  between operations  0.87 us (1%)
    ppermute x17, starting transfers between devices, swap(): return lax.ppermute(x, axis, [(s, s ^ mask) for s in range(16)])  25.5 us
    ppermute x17, waiting for transfers between devices, swap(): return lax.ppermute(x, axis, [(s, s ^ mask) for s in range(16)])  17 us
    pallas_call x2, Pallas kernels, product(): pl.pallas_call(backward_kernel if backward else forward_kernel, in_specs=...  9.01 us
    pallas_call x1, Pallas kernels, relayout(): pl.pallas_call(relayout_kernel, in_specs=[pl.BlockSpec(memory_space=pltpu...  2.46 us
    mul x2, other arithmetic, place(): return (slot * 8 + (position & 7)) * 16  1.4 us
  transfers between devices with their start and end apart: 17, of which 7 were waited for; matrix products, arithmetic and copies ran while one was open for 4% of the time, Pallas kernels for 13%

profile of v6, /device:TPU:6, one launch (start us, length us, event | category | flops | bytes accessed | tf_op | source)
XLA Modules:
  0.0 59.1 jit_solution(7562788943851078496)
XLA Ops:
  0.0 0.7 %reshape.94 = bf16[64,128]{1,0:T(8,128)(2,1)S(1)} reshape(bf16[8,1024]{1,0:T(8,128)(2,1)} %param.5) | data formatting | bytes 32768 | tf_op jit(solution)/shard_map/reshape | solution.py:308
  0.7 7.3 %collective-permute-start.9 = (bf16[64,128]{1,0:T(8,128)(2,1)S(1)}, bf16[64,128]{1,0:T(8,128)(2,1)S(1)}, u32[]{:S(2)}, u32[]{:S(2)}) collective-permute-start(bf16[64,128]{1,0:T(8,128)(2,1)S(1)} %reshape.94), channel_id=1, source_target_pairs={{0,2},{1,3},{2,0},{3,1},{4,6},{5,7},{6,4},{7,5},{8,10},{9,11},{10,... | collective-permute-start | bytes 49160 | tf_op jit(solution)/shard_map/ppermute | solution.py:271
  8.0 1.4 %collective-permute-start = (bf16[8,8,128]{2,1,0:T(8,128)(2,1)S(1)}, bf16[8,8,128]{2,1,0:T(8,128)(2,1)S(1)}, u32[]{:S(2)}, u32[]{:S(2)}) collective-permute-start(bf16[8,8,128]{2,1,0:T(8,128)(2,1)S(1)} %bitcast.15), channel_id=1, source_target_pairs={{0,128},{16,144},{32,160},{48,176},{64,192},{80,208},{96,224},{112... | collective-permute-start | bytes 49160 | tf_op jit(solution)/shard_map/ppermute | solution.py:271
  10.1 0.7 %add_multiply_fusion = s32[1,1,512]{2,1,0:T(1,128)S(1)} fusion(s32[1,1,512]{2,1,0:T(1,128)} %param.8, s32[]{:T(128)S(6)} %axis_index.25), kind=kLoop, calls=%fused_computation.17 | loop fusion | flops 10752 | bytes 4100 | tf_op jit(solution)/shard_map/mul | solution.py:302
  10.8 0.7 %add_multiply_fusion.1 = s32[1,1,512]{2,1,0:T(1,128)S(1)} fusion(s32[1,1,512]{2,1,0:T(1,128)} %param.7, s32[]{:T(128)S(6)} %axis_index.22), kind=kLoop, calls=%fused_computation.18 | loop fusion | flops 10752 | bytes 4100 | tf_op jit(solution)/shard_map/mul | solution.py:302
  11.5 0.7 %compare_select_fusion = f32[1,1,512]{2,1,0:T(1,128)S(1)} fusion(s32[1,1,512]{2,1,0:T(1,128)} %param.7, s32[1,1,512]{2,1,0:T(1,128)} %param.8, s32[]{:T(128)S(6)} %mul.37, s32[]{:T(128)S(6)} %axis_index.22), kind=kLoop, calls=%fused_computation.16 | loop fusion | flops 4608 | bytes 6152 | tf_op jit(solution)/shard_map/jit(_where)/select_n | solution.py:318
  12.2 0.1 broadcast_in_dim.21.weight_ref
  12.3 2.5 %relayout.1.w_ref = bf16[16384,128]{1,0:T(8,128)(2,1)S(1)} custom-call(bf16[512,4096]{1,0:T(8,128)(2,1)} %bitcast.14, f32[512,128]{1,0:T(8,128)S(1)} %broadcast_in_dim.21.weight_ref), custom_call_target="tpu_custom_call" | custom-call | tf_op jit(solution)/shard_map/relayout/pallas_call | solution.py:47
  14.8 0.0 collective-permute-done
  14.8 0.1 collective-permute-start.1
  14.9 0.0 collective-permute-done.9
  15.0 1.6 %collective-permute-start.10 = (bf16[128,128]{1,0:T(8,128)(2,1)S(1)}, bf16[128,128]{1,0:T(8,128)(2,1)S(1)}, u32[]{:S(2)}, u32[]{:S(2)}) collective-permute-start(bf16[128,128]{1,0:T(8,128)(2,1)S(1)} %pad_maximum_fusion.5), channel_id=1, source_target_pairs={{0,1},{1,0},{2,3},{3,2},{4,5},{5,4},{6,7},{7,6},{8,9},{9,8},{10,11... | collective-permute-start | bytes 98312 | tf_op jit(solution)/shard_map/ppermute | solution.py:271
  16.5 2.3 %collective-permute-done.1 = bf16[16,8,128]{2,1,0:T(8,128)(2,1)S(1)} collective-permute-done((bf16[16,8,128]{2,1,0:T(8,128)(2,1)S(1)}, bf16[16,8,128]{2,1,0:T(8,128)(2,1)S(1)}, u32[]{:S(2)}, u32[]{:S(2)}) %collective-permute-start.1) | collective-permute-done | bytes 32800 | tf_op jit(solution)/shard_map/ppermute | solution.py:271
  18.8 1.1 %collective-permute-start.2 = (bf16[32,8,128]{2,1,0:T(8,128)(2,1)S(1)}, bf16[32,8,128]{2,1,0:T(8,128)(2,1)S(1)}, u32[]{:S(2)}, u32[]{:S(2)}) collective-permute-start(bf16[32,8,128]{2,1,0:T(8,128)(2,1)S(1)} %pad_maximum_fusion.2), channel_id=1, source_target_pairs={{0,32},{16,48},{32,0},{48,16},{64,96},{80,112},{96,64},{112,80},{1... | collective-permute-start | bytes 196616 | tf_op jit(solution)/shard_map/ppermute | solution.py:271
  20.0 0.0 collective-permute-done.10
  20.0 3.3 %collective-permute-start.11 = (bf16[256,128]{1,0:T(8,128)(2,1)S(1)}, bf16[256,128]{1,0:T(8,128)(2,1)S(1)}, u32[]{:S(2)}, u32[]{:S(2)}) collective-permute-start(bf16[256,128]{1,0:T(8,128)(2,1)S(1)} %pad_maximum_fusion.3), channel_id=1, source_target_pairs={{0,8},{1,9},{2,10},{3,11},{4,12},{5,13},{6,14},{7,15},{8,0},{9,1},... | collective-permute-start | bytes 196616 | tf_op jit(solution)/shard_map/ppermute | solution.py:271
  23.3 0.0 collective-permute-done.2
  23.3 0.1 collective-permute-start.3
  23.4 2.4 %collective-permute-done.11 = bf16[256,128]{1,0:T(8,128)(2,1)S(1)} collective-permute-done((bf16[256,128]{1,0:T(8,128)(2,1)S(1)}, bf16[256,128]{1,0:T(8,128)(2,1)S(1)}, u32[]{:S(2)}, u32[]{:S(2)}) %collective-permute-start.11) | collective-permute-done | bytes 65568 | tf_op jit(solution)/shard_map/ppermute | solution.py:271
  25.8 1.7 %collective-permute-start.12 = (bf16[512,128]{1,0:T(8,128)(2,1)S(1)}, bf16[512,128]{1,0:T(8,128)(2,1)S(1)}, u32[]{:S(2)}, u32[]{:S(2)}) collective-permute-start(bf16[512,128]{1,0:T(8,128)(2,1)S(1)} %pad_maximum_fusion.1), channel_id=1, source_target_pairs={{0,4},{1,5},{2,6},{3,7},{4,0},{5,1},{6,2},{7,3},{8,12},{9,13},{10,... | collective-permute-start | bytes 393224 | tf_op jit(solution)/shard_map/ppermute | solution.py:271
  27.5 0.0 collective-permute-done.3
  27.6 4.7 %forward.1 = (f32[256,128]{1,0:T(8,128)S(1)}, s16[272,128]{1,0:T(8,128)(2,1)S(1)}, s16[272,128]{1,0:T(8,128)(2,1)S(1)}, s16[272,128]{1,0:T(8,128)(2,1)S(1)}) custom-call(s32[1,1]{1,0:T(1,128)} %copy.14.count_ref, s32[512]{0:T(512)S(1)} %bitcast.12, s32[512]{0:T(512)S(1)} %bitcast.10, bf16[1024,128]{1,0:T(8,128)(2,1)S(1)} %bitcast.9, ...), custom_call_target="tpu_custom_call" | custom-call | tf_op jit(solution)/shard_map/forward/pallas_call | solution.py:232
  32.2 0.0 collective-permute-done.12
  32.3 4.3 %backward.1 = (f32[512,128]{1,0:T(8,128)S(1)}, f32[512,128]{1,0:T(8,128)S(1)}) custom-call(s32[1,1]{1,0:T(1,128)} %copy.14.count_ref, s32[512]{0:T(512)S(1)} %bitcast.13, s32[512]{0:T(512)S(1)} %bitcast.11, bf16[1024,128]{1,0:T(8,128)(2,1)S(1)} %constant_dynamic-update-slice_fusion.5.x_ref, bf16[16384,128]{1,0:T(8,128)(2,1)S(1)} %relayout.1.w_ref), custom_call_target="tpu_custom_call" | custom-call | tf_op jit(solution)/shard_map/backward/pallas_call | solution.py:232
  36.6 0.1 collective-permute-start.13
  36.7 2.9 %collective-permute-start.4 = (s16[272,128]{1,0:T(8,128)(2,1)S(1)}, s16[272,128]{1,0:T(8,128)(2,1)S(1)}, u32[]{:S(2)}, u32[]{:S(2)}) collective-permute-start(s16[272,128]{1,0:T(8,128)(2,1)S(1)} %get-tuple-element.23), channel_id=1, source_target_pairs={{0,8},{1,9},{2,10},{3,11},{4,12},{5,13},{6,14},{7,15},{8,0},{9,1},... | collective-permute-start | bytes 208904 | tf_op jit(solution)/shard_map/ppermute | solution.py:271
  39.7 0.2 collective-permute-start.5
  39.9 0.4 collective-permute-start.6
  40.3 0.0 collective-permute-done.13.refs_0_
  40.3 0.1 combine.7
  40.4 1.2 %collective-permute-start.14 = (s16[272,128]{1,0:T(8,128)(2,1)S(1)}, s16[272,128]{1,0:T(8,128)(2,1)S(1)}, u32[]{:S(2)}, u32[]{:S(2)}) collective-permute-start(s16[272,128]{1,0:T(8,128)(2,1)S(1)} %get-tuple-element.34), channel_id=1, source_target_pairs={{0,32},{16,48},{32,0},{48,16},{64,96},{80,112},{96,64},{112,80},{1... | collective-permute-start | bytes 208904 | tf_op jit(solution)/shard_map/ppermute | solution.py:271
  41.6 1.2 %collective-permute-done.4.refs_0_ = s16[272,128]{1,0:T(8,128)(2,1)S(1)} collective-permute-done((s16[272,128]{1,0:T(8,128)(2,1)S(1)}, s16[272,128]{1,0:T(8,128)(2,1)S(1)}, u32[]{:S(2)}, u32[]{:S(2)}) %collective-permute-start.4) | collective-permute-done | bytes 69664 | tf_op jit(solution)/shard_map/ppermute | solution.py:271
  42.8 2.4 %collective-permute-done.5.refs_1_ = s16[272,128]{1,0:T(8,128)(2,1)S(1)} collective-permute-done((s16[272,128]{1,0:T(8,128)(2,1)S(1)}, s16[272,128]{1,0:T(8,128)(2,1)S(1)}, u32[]{:S(2)}, u32[]{:S(2)}) %collective-permute-start.5) | collective-permute-done | bytes 69664 | tf_op jit(solution)/shard_map/ppermute | solution.py:271
  45.2 0.0 collective-permute-done.6.refs_2_
  45.2 0.1 combine.5
  45.3 1.6 %collective-permute-start.7 = (s16[144,128]{1,0:T(8,128)(2,1)S(1)}, s16[144,128]{1,0:T(8,128)(2,1)S(1)}, u32[]{:S(2)}, u32[]{:S(2)}) collective-permute-start(s16[144,128]{1,0:T(8,128)(2,1)S(1)} %get-tuple-element.27), channel_id=1, source_target_pairs={{0,1},{1,0},{2,3},{3,2},{4,5},{5,4},{6,7},{7,6},{8,9},{9,8},{10,11... | collective-permute-start | bytes 110600 | tf_op jit(solution)/shard_map/ppermute | solution.py:271
  46.9 0.0 collective-permute-done.14.refs_0_
  46.9 0.9 %collective-permute-start.15 = (s16[144,128]{1,0:T(8,128)(2,1)S(1)}, s16[144,128]{1,0:T(8,128)(2,1)S(1)}, u32[]{:S(2)}, u32[]{:S(2)}) collective-permute-start(s16[144,128]{1,0:T(8,128)(2,1)S(1)} %get-tuple-element.36), channel_id=1, source_target_pairs={{0,64},{16,80},{32,96},{48,112},{64,0},{80,16},{96,32},{112,48},{1... | collective-permute-start | bytes 110600 | tf_op jit(solution)/shard_map/ppermute | solution.py:271
  47.8 2.4 %collective-permute-done.7.refs_0_ = s16[144,128]{1,0:T(8,128)(2,1)S(1)} collective-permute-done((s16[144,128]{1,0:T(8,128)(2,1)S(1)}, s16[144,128]{1,0:T(8,128)(2,1)S(1)}, u32[]{:S(2)}, u32[]{:S(2)}) %collective-permute-start.7) | collective-permute-done | bytes 36896 | tf_op jit(solution)/shard_map/ppermute | solution.py:271
  50.3 0.6 %collective-permute-start.8 = (s16[80,128]{1,0:T(8,128)(2,1)S(1)}, s16[80,128]{1,0:T(8,128)(2,1)S(1)}, u32[]{:S(2)}, u32[]{:S(2)}) collective-permute-start(s16[80,128]{1,0:T(8,128)(2,1)S(1)} %get-tuple-element.29), channel_id=1, source_target_pairs={{0,2},{1,3},{2,0},{3,1},{4,6},{5,7},{6,4},{7,5},{8,10},{9,11},{10,... | collective-permute-start | bytes 61448 | tf_op jit(solution)/shard_map/ppermute | solution.py:271
  50.9 0.1 collective-permute-done.15.refs_0_
  51.0 1.0 %collective-permute-start.16 = (s16[80,128]{1,0:T(8,128)(2,1)S(1)}, s16[80,128]{1,0:T(8,128)(2,1)S(1)}, u32[]{:S(2)}, u32[]{:S(2)}) collective-permute-start(s16[80,128]{1,0:T(8,128)(2,1)S(1)} %get-tuple-element.38), channel_id=1, source_target_pairs={{0,128},{16,144},{32,160},{48,176},{64,192},{80,208},{96,224},{112... | collective-permute-start | bytes 61448 | tf_op jit(solution)/shard_map/ppermute | solution.py:271
  52.0 6.2 %collective-permute-done.8.a1_ref = s16[80,128]{1,0:T(8,128)(2,1)S(1)} collective-permute-done((s16[80,128]{1,0:T(8,128)(2,1)S(1)}, s16[80,128]{1,0:T(8,128)(2,1)S(1)}, u32[]{:S(2)}, u32[]{:S(2)}) %collective-permute-start.8) | collective-permute-done | bytes 20512 | tf_op jit(solution)/shard_map/ppermute | solution.py:271
  58.3 0.0 collective-permute-done.16.b1_ref
  58.3 0.9 %finish.1 = f32[8,1024]{1,0:T(8,128)} custom-call(f32[64,128]{1,0:T(8,128)S(1)} %get-tuple-element.28.a0_ref, s16[80,128]{1,0:T(8,128)(2,1)S(1)} %collective-permute-done.8.a1_ref, f32[64,128]{1,0:T(8,128)S(1)} %get-tuple-element.37.b0_ref, s16[80,128]{1,0:T(8,128)(2,1)S(1)} %collective-permute-done.16.b1_ref), custom_call_target="tpu_custom_call" | custom-call | tf_op jit(solution)/shard_map/finish/pallas_call | solution.py:259
  (20 shorter events, 0.3 us)
Async XLA Ops:
  0.7 14.2 %collective-permute-start.9 = (bf16[64,128]{1,0:T(8,128)(2,1)S(1)}, bf16[64,128]{1,0:T(8,128)(2,1)S(1)}, u32[]{:S(2)}, u32[]{:S(2)}) collective-permute-start(bf16[64,128]{1,0:T(8,128)(2,1)S(1)} %reshape.94), channel_id=1, source_target_pairs={{0,2},{1,3},{2,0},{3,1},{4,6},{5,7},{6,4},{7,5},{8,10},{9,11},{10,... | collective-permute-start | bytes 49160 | tf_op jit(solution)/shard_map/ppermute | solution.py:271
  8.0 6.8 %collective-permute-start = (bf16[8,8,128]{2,1,0:T(8,128)(2,1)S(1)}, bf16[8,8,128]{2,1,0:T(8,128)(2,1)S(1)}, u32[]{:S(2)}, u32[]{:S(2)}) collective-permute-start(bf16[8,8,128]{2,1,0:T(8,128)(2,1)S(1)} %bitcast.15), channel_id=1, source_target_pairs={{0,128},{16,144},{32,160},{48,176},{64,192},{80,208},{96,224},{112... | collective-permute-start | bytes 49160 | tf_op jit(solution)/shard_map/ppermute | solution.py:271
  14.8 4.0 %collective-permute-start.1 = (bf16[16,8,128]{2,1,0:T(8,128)(2,1)S(1)}, bf16[16,8,128]{2,1,0:T(8,128)(2,1)S(1)}, u32[]{:S(2)}, u32[]{:S(2)}) collective-permute-start(bf16[16,8,128]{2,1,0:T(8,128)(2,1)S(1)} %pad_maximum_fusion.4), channel_id=1, source_target_pairs={{0,64},{16,80},{32,96},{48,112},{64,0},{80,16},{96,32},{112,48},{1... | collective-permute-start | bytes 98312 | tf_op jit(solution)/shard_map/ppermute | solution.py:271
  15.0 5.0 %collective-permute-start.10 = (bf16[128,128]{1,0:T(8,128)(2,1)S(1)}, bf16[128,128]{1,0:T(8,128)(2,1)S(1)}, u32[]{:S(2)}, u32[]{:S(2)}) collective-permute-start(bf16[128,128]{1,0:T(8,128)(2,1)S(1)} %pad_maximum_fusion.5), channel_id=1, source_target_pairs={{0,1},{1,0},{2,3},{3,2},{4,5},{5,4},{6,7},{7,6},{8,9},{9,8},{10,11... | collective-permute-start | bytes 98312 | tf_op jit(solution)/shard_map/ppermute | solution.py:271
  18.8 4.4 %collective-permute-start.2 = (bf16[32,8,128]{2,1,0:T(8,128)(2,1)S(1)}, bf16[32,8,128]{2,1,0:T(8,128)(2,1)S(1)}, u32[]{:S(2)}, u32[]{:S(2)}) collective-permute-start(bf16[32,8,128]{2,1,0:T(8,128)(2,1)S(1)} %pad_maximum_fusion.2), channel_id=1, source_target_pairs={{0,32},{16,48},{32,0},{48,16},{64,96},{80,112},{96,64},{112,80},{1... | collective-permute-start | bytes 196616 | tf_op jit(solution)/shard_map/ppermute | solution.py:271
  20.0 5.9 %collective-permute-start.11 = (bf16[256,128]{1,0:T(8,128)(2,1)S(1)}, bf16[256,128]{1,0:T(8,128)(2,1)S(1)}, u32[]{:S(2)}, u32[]{:S(2)}) collective-permute-start(bf16[256,128]{1,0:T(8,128)(2,1)S(1)} %pad_maximum_fusion.3), channel_id=1, source_target_pairs={{0,8},{1,9},{2,10},{3,11},{4,12},{5,13},{6,14},{7,15},{8,0},{9,1},... | collective-permute-start | bytes 196616 | tf_op jit(solution)/shard_map/ppermute | solution.py:271
  23.3 4.2 %collective-permute-start.3 = (bf16[64,8,128]{2,1,0:T(8,128)(2,1)S(1)}, bf16[64,8,128]{2,1,0:T(8,128)(2,1)S(1)}, u32[]{:S(2)}, u32[]{:S(2)}) collective-permute-start(bf16[64,8,128]{2,1,0:T(8,128)(2,1)S(1)} %pad_maximum_fusion), channel_id=1, source_target_pairs={{0,16},{16,0},{32,48},{48,32},{64,80},{80,64},{96,112},{112,96},{1... | collective-permute-start | bytes 393224 | tf_op jit(solution)/shard_map/ppermute | solution.py:271
  25.8 6.4 %collective-permute-start.12 = (bf16[512,128]{1,0:T(8,128)(2,1)S(1)}, bf16[512,128]{1,0:T(8,128)(2,1)S(1)}, u32[]{:S(2)}, u32[]{:S(2)}) collective-permute-start(bf16[512,128]{1,0:T(8,128)(2,1)S(1)} %pad_maximum_fusion.1), channel_id=1, source_target_pairs={{0,4},{1,5},{2,6},{3,7},{4,0},{5,1},{6,2},{7,3},{8,12},{9,13},{10,... | collective-permute-start | bytes 393224 | tf_op jit(solution)/shard_map/ppermute | solution.py:271
  36.6 3.7 %collective-permute-start.13 = (f32[512,128]{1,0:T(8,128)S(1)}, f32[512,128]{1,0:T(8,128)S(1)}, u32[]{:S(2)}, u32[]{:S(2)}) collective-permute-start(f32[512,128]{1,0:T(8,128)S(1)} %get-tuple-element.32), channel_id=1, source_target_pairs={{0,16},{16,0},{32,48},{48,32},{64,80},{80,64},{96,112},{112,96},{1... | collective-permute-start | bytes 786440 | tf_op jit(solution)/shard_map/ppermute | solution.py:271
  36.7 6.1 %collective-permute-start.4 = (s16[272,128]{1,0:T(8,128)(2,1)S(1)}, s16[272,128]{1,0:T(8,128)(2,1)S(1)}, u32[]{:S(2)}, u32[]{:S(2)}) collective-permute-start(s16[272,128]{1,0:T(8,128)(2,1)S(1)} %get-tuple-element.23), channel_id=1, source_target_pairs={{0,8},{1,9},{2,10},{3,11},{4,12},{5,13},{6,14},{7,15},{8,0},{9,1},... | collective-permute-start | bytes 208904 | tf_op jit(solution)/shard_map/ppermute | solution.py:271
  39.7 5.5 %collective-permute-start.5 = (s16[272,128]{1,0:T(8,128)(2,1)S(1)}, s16[272,128]{1,0:T(8,128)(2,1)S(1)}, u32[]{:S(2)}, u32[]{:S(2)}) collective-permute-start(s16[272,128]{1,0:T(8,128)(2,1)S(1)} %get-tuple-element.24), channel_id=1, source_target_pairs={{0,12},{1,13},{2,14},{3,15},{4,8},{5,9},{6,10},{7,11},{8,4},{9,5},... | collective-permute-start | bytes 208904 | tf_op jit(solution)/shard_map/ppermute | solution.py:271
  39.9 5.3 %collective-permute-start.6 = (s16[272,128]{1,0:T(8,128)(2,1)S(1)}, s16[272,128]{1,0:T(8,128)(2,1)S(1)}, u32[]{:S(2)}, u32[]{:S(2)}) collective-permute-start(s16[272,128]{1,0:T(8,128)(2,1)S(1)} %get-tuple-element.25), channel_id=1, source_target_pairs={{0,4},{1,5},{2,6},{3,7},{4,0},{5,1},{6,2},{7,3},{8,12},{9,13},{10,... | collective-permute-start | bytes 208904 | tf_op jit(solution)/shard_map/ppermute | solution.py:271
  40.4 6.5 %collective-permute-start.14 = (s16[272,128]{1,0:T(8,128)(2,1)S(1)}, s16[272,128]{1,0:T(8,128)(2,1)S(1)}, u32[]{:S(2)}, u32[]{:S(2)}) collective-permute-start(s16[272,128]{1,0:T(8,128)(2,1)S(1)} %get-tuple-element.34), channel_id=1, source_target_pairs={{0,32},{16,48},{32,0},{48,16},{64,96},{80,112},{96,64},{112,80},{1... | collective-permute-start | bytes 208904 | tf_op jit(solution)/shard_map/ppermute | solution.py:271
  45.3 4.9 %collective-permute-start.7 = (s16[144,128]{1,0:T(8,128)(2,1)S(1)}, s16[144,128]{1,0:T(8,128)(2,1)S(1)}, u32[]{:S(2)}, u32[]{:S(2)}) collective-permute-start(s16[144,128]{1,0:T(8,128)(2,1)S(1)} %get-tuple-element.27), channel_id=1, source_target_pairs={{0,1},{1,0},{2,3},{3,2},{4,5},{5,4},{6,7},{7,6},{8,9},{9,8},{10,11... | collective-permute-start | bytes 110600 | tf_op jit(solution)/shard_map/ppermute | solution.py:271
  46.9 4.0 %collective-permute-start.15 = (s16[144,128]{1,0:T(8,128)(2,1)S(1)}, s16[144,128]{1,0:T(8,128)(2,1)S(1)}, u32[]{:S(2)}, u32[]{:S(2)}) collective-permute-start(s16[144,128]{1,0:T(8,128)(2,1)S(1)} %get-tuple-element.36), channel_id=1, source_target_pairs={{0,64},{16,80},{32,96},{48,112},{64,0},{80,16},{96,32},{112,48},{1... | collective-permute-start | bytes 110600 | tf_op jit(solution)/shard_map/ppermute | solution.py:271
  50.3 8.0 %collective-permute-start.8 = (s16[80,128]{1,0:T(8,128)(2,1)S(1)}, s16[80,128]{1,0:T(8,128)(2,1)S(1)}, u32[]{:S(2)}, u32[]{:S(2)}) collective-permute-start(s16[80,128]{1,0:T(8,128)(2,1)S(1)} %get-tuple-element.29), channel_id=1, source_target_pairs={{0,2},{1,3},{2,0},{3,1},{4,6},{5,7},{6,4},{7,5},{8,10},{9,11},{10,... | collective-permute-start | bytes 61448 | tf_op jit(solution)/shard_map/ppermute | solution.py:271
  51.0 7.3 %collective-permute-start.16 = (s16[80,128]{1,0:T(8,128)(2,1)S(1)}, s16[80,128]{1,0:T(8,128)(2,1)S(1)}, u32[]{:S(2)}, u32[]{:S(2)}) collective-permute-start(s16[80,128]{1,0:T(8,128)(2,1)S(1)} %get-tuple-element.38), channel_id=1, source_target_pairs={{0,128},{16,144},{32,160},{48,176},{64,192},{80,208},{96,224},{112... | collective-permute-start | bytes 61448 | tf_op jit(solution)/shard_map/ppermute | solution.py:271
